TPU v7x, 256 devices: a whole 4x4x8 slice. The times are simulated.
256 devices in a mesh: row: 8 (over y_lo, x), col: 16 (over z, y_hi), lag: 2 (over core).
Axes of the slice: x: 4, y: 4 (y_hi: 2, y_lo: 2; y = y_hi * 2 + y_lo), z: 8, core: 2. Of those that a mesh axis runs over, the one named last changes fastest.
Arguments:
- history: bfloat16 [8, 16, 128, 4096], P('lag', 'col', None, 'row'), may hold values from -6 to 6
- kernel_tiles: bfloat16 [8, 16, 8, 12, 256, 256], P('row', 'col', 'lag'), may hold values from -0.046875 to 0.046875
- tile_rows: int32 [8, 16, 8, 12], P('row', 'col', 'lag'), may hold values from 0 to 31
- tile_cols: int32 [8, 16, 8, 12], P('row', 'col', 'lag'), may hold values from 0 to 15
- tile_count: int32 [8, 16, 8], P('row', 'col', 'lag'), may hold values from 3 to 12, as said below
- base_stress: float32 [128, 65536], P(None, ('row', 'col', 'lag')), may hold values from -6 to 6
- prev_rate: float32 [128, 65536], P(None, ('row', 'col', 'lag')), may hold values from -6 to 6
- direct_effect: float32 [128, 65536], P(None, ('row', 'col', 'lag')), may hold values from 0.5 to 2
- state_var: float32 [128, 65536], P(None, ('row', 'col', 'lag')), may hold values from -2 to 2
Outputs:
- stress_change: float32 [128, 65536], P(None, ('row', 'col', 'lag'))
- new_rate: float32 [128, 65536], P(None, ('row', 'col', 'lag'))
Inputs may be any that keep to these rules, and one draw needn't show every extreme that they name: `tile_count`: every draw has some device and lag with all 12 slots live.
All inputs are finite; a program needn't handle non-finite values.
Results may differ from a plain program's by a relative error of at most 0.0003.
Values may be sent and summed in bfloat16 or wider, within the bound.
A program may use at most 64 MiB of HBM per device.

v0:
```python
import jax
import jax.numpy as jnp
from jax import lax
from jax.sharding import PartitionSpec as P

NEWTON = 4


def inverse_sinh(value):
    magnitude = jnp.abs(value)
    return jnp.sign(value) * jnp.log(magnitude + jnp.sqrt(1.0 + magnitude * magnitude))


def local(
    history,
    kernel_tiles,
    tile_rows,
    tile_cols,
    tile_count,
    base_stress,
    prev_rate,
    direct_effect,
    state_var,
):
    gathered = lax.all_gather(history, "row", axis=3, tiled=True)
    lag_local = gathered.shape[0]
    sims_count = gathered.shape[2]
    tile_side = kernel_tiles.shape[4]
    slots = kernel_tiles.shape[3]
    col_blocks = gathered.shape[3] // tile_side
    blocks = gathered.reshape(lag_local, sims_count, col_blocks, tile_side)
    choose = jax.nn.one_hot(tile_cols[0, 0], col_blocks, dtype=jnp.bfloat16)
    picked = jnp.einsum(
        "lkb,lsbj->lksj", choose, blocks, preferred_element_type=jnp.float32
    ).astype(jnp.bfloat16)
    contrib = jnp.einsum(
        "lksj,lkij->slki", picked, kernel_tiles[0, 0], preferred_element_type=jnp.float32
    )
    rec_local = base_stress.shape[1] * lax.axis_size(("col", "lag"))
    row_blocks = rec_local // tile_side
    alive_mask = (jnp.arange(slots)[None, :] < tile_count[0, 0][:, None]).astype(jnp.float32)
    masked = (contrib * alive_mask[None, :, :, None]).reshape(
        sims_count, lag_local * slots, tile_side
    )
    targets = tile_rows[0, 0].reshape(lag_local * slots)
    placed = (
        jnp.zeros((sims_count, row_blocks, tile_side), jnp.float32).at[:, targets, :].add(masked)
    )
    partial_stress = placed.reshape(sims_count, rec_local)
    owned = base_stress.shape[1]
    summed = lax.psum(partial_stress, ("col", "lag"))
    offset = lax.axis_index(("col", "lag")) * owned
    stress_change = lax.dynamic_slice_in_dim(summed, offset, owned, 1)
    driving = base_stress + stress_change
    factor = jnp.exp(state_var) / 2.0
    velocity = prev_rate
    for step in range(NEWTON):
        scaled = velocity * factor
        misfit = direct_effect * inverse_sinh(scaled) + 0.5 * velocity - driving
        slope = direct_effect * factor / jnp.sqrt(1.0 + scaled * scaled) + 0.5
        velocity = velocity - misfit / slope
    return (stress_change, velocity)


def solution(mesh):
    return jax.shard_map(
        local,
        mesh=mesh,
        in_specs=(
            P("lag", "col", None, "row"),
            P("row", "col", "lag", None, None, None),
            P("row", "col", "lag", None),
            P("row", "col", "lag", None),
            P("row", "col", "lag"),
            P(None, ("row", "col", "lag")),
            P(None, ("row", "col", "lag")),
            P(None, ("row", "col", "lag")),
            P(None, ("row", "col", "lag")),
        ),
        out_specs=(P(None, ("row", "col", "lag")), P(None, ("row", "col", "lag"))),
        check_vma=False,
    )
```

profile of v0, /device:TPU:1, one launch (start us, length us, event | category | flops | bytes accessed | tf_op | source)
XLA Modules:
  0.0 392.8 jit_solution(5973830863412099391)
XLA Ops:
  7.2 0.0 all-gather.2.cloned.1.call-start
  7.2 0.7 all-gather.2.cloned.1.call-update
  7.9 0.0 all-reduce.2.cloned.1.call-start
  7.9 0.8 reshape_squeeze.3
  8.7 0.7 fusion.12
  9.4 59.3 %all-gather.2.cloned.1.call-done = bf16[4,1,128,4096]{3,2,1,0:T(8,128)(2,1)} async-done(((bf16[4,1,128,512]{3,2,1,0:T(8,128)(2,1)}), bf16[4,1,128,4096]{3,2,1,0:T(8,128)(2,1)}) %all-gather.2.cloned.1.call-update) | async-done | bytes 4194320 | tf_op jit(solution)/shard_map/all_gather | solution.py:25
  68.8 3.8 copy.26
  72.5 0.0 slice-start.1
  72.6 1.3 fusion.2
  73.9 0.3 slice-done.1
  74.1 4.8 %broadcast_multiply_fusion = f32[4,12,128,256]{3,2,1,0:T(8,128)} fusion(f32[4,12]{1,0:T(4,128)S(1)} %fusion.12, bf16[1,1,4,12,256,256]{5,4,3,2,1,0:T(8,128)(2,1)S(1)} %bitcast.33, bf16[4,12,128,256]{3,1,2,0:T(8,128)(2,1)S(1)} %fusion.2), kind=kOutput, calls=%fused_computation.6 | convolution fusion | flops 806879232 | bytes 15728832 | tf_op jit(solution)/shard_map/lksj,lkij->slki/dot_general | solution.py:36
  79.0 2.5 broadcast_in_dim.4
  81.5 14.6 %scatter_fusion = f32[128,32,256]{2,0,1:T(8,128)} fusion(f32[128,32,256]{2,0,1:T(8,128)} %broadcast_in_dim.4, s32[48]{0:T(128)S(1)} %fusion.13, f32[48,128,256]{2,1,0:T(8,128)} %bitcast.29), kind=kCustom, calls=%fused_computation | custom fusion | flops 1572864 | bytes 18874560 | tf_op jit(solution)/shard_map/scatter-add | solution.py:47
  96.1 5.6 %copy.11 = f32[128,32,256]{0,2,1:T(8,128)} copy(f32[128,32,256]{2,0,1:T(8,128)} %scatter_fusion) | data formatting | bytes 8388608 | tf_op jit(solution)/shard_map/scatter-add | solution.py:47
  101.7 0.0 all-reduce.2.cloned.1.call-update
  101.7 0.9 copy-done
  102.6 0.1 copy.12
  102.7 0.1 copy.14
  102.8 0.1 copy.16
  102.9 0.1 copy.18
  103.0 279.9 %all-reduce.2.cloned.1.call-done = f32[128,8192]{0,1:T(8,128)} async-done(((f32[128,8192]{0,1:T(8,128)}), f32[128,8192]{0,1:T(8,128)}) %all-reduce.2.cloned.1.call-update) | async-done | bytes 4194320 | tf_op jit(solution)/shard_map/psum | solution.py:51
  382.9 1.5 divide_subtract_fusion
  384.4 0.8 copy.22
  385.2 0.8 copy.23
  (13 shorter events, 0.0 us)
Async XLA Ops:
  7.2 61.6 %all-gather.2.cloned.1.call-start = ((), (), s32[]{:S(2)}) async-start(), calls=%async_computation | async-start | bytes 4718592 | tf_op jit(solution)/shard_map/all_gather | solution.py:25
  7.9 375.0 %all-reduce.2.cloned.1.call-start = ((), (), s32[]{:S(2)}) async-start(), calls=%async_computation.1 | async-start | bytes 8388608 | tf_op jit(solution)/shard_map/psum | solution.py:51
  68.7 3.8 copy-start.4
  68.8 5.1 %slice-start = ((s8[6291456]{0:T(1024)(128)(4,1)}), s8[4194304]{0:T(1024)(128)(4,1)S(1)}, s32[]{:S(2)}) async-start(s8[6291456]{0:T(1024)(128)(4,1)} %bitcast.32), calls=%async_computation.2 | async-start | bytes 8388608
  72.5 1.6 slice-start.1
  101.7 0.9 copy-start
  101.7 1.0 copy-start.1
  101.7 1.1 copy-start.2
  101.7 1.2 copy-start.3
Sparse Core Ops, SparseCore 0:
  9.8 58.9 all-gather.1
  101.8 281.0 all-reduce.1
where the time goes:
time: 393 us
  waiting for transfers between devices  340 us (87%)
  other arithmetic  16.9 us (4%)
  local copies, waits for them, and re-layouts  15.6 us (4%)
  between operations  14.1 us (4%)
  matrix products  6.13 us (2%)
    psum x1, waiting for transfers between devices, local(): summed = lax.psum(partial_stress, ('col', 'lag'))  280 us
    all_gather x1, waiting for transfers between devices, local(): gathered = lax.all_gather(history, 'row', axis=3, tiled=True)  59.3 us
    scatter-add x1, other arithmetic, local(): jnp.zeros((sims_count, row_blocks, tile_side), jnp.float32)  14.6 us
  transfers between devices with their start and end apart: 2, of which 2 were waited for; matrix products, arithmetic and copies ran while one was open for 0% of the time, Pallas kernels for 0%

commit v1 on v0

--- a/solution.py
+++ b/solution.py
@@ -47,10 +47,9 @@
         jnp.zeros((sims_count, row_blocks, tile_side), jnp.float32).at[:, targets, :].add(masked)
     )
     partial_stress = placed.reshape(sims_count, rec_local)
-    owned = base_stress.shape[1]
-    summed = lax.psum(partial_stress, ("col", "lag"))
-    offset = lax.axis_index(("col", "lag")) * owned
-    stress_change = lax.dynamic_slice_in_dim(summed, offset, owned, 1)
+    stress_change = lax.psum_scatter(
+        partial_stress, ("col", "lag"), scatter_dimension=1, tiled=True
+    )
     driving = base_stress + stress_change
     factor = jnp.exp(state_var) / 2.0
     velocity = prev_rate

time: 393 us -> 239 us (0.61); the launches traced: 393 us -> 235 us
  waiting for transfers between devices: 340 us -> 181 us
    psum x1 -> x0, waiting for transfers between devices: 280 us -> none  [local(): summed = lax.psum(partial_stress, ('col', 'lag'))]
    reduce_scatter x0 -> x1, waiting for transfers between devices: none -> 121 us  [local(): lax.psum_scatter(partial_stress, ('col', 'lag'), scatter_dimension=1, til...]
  transfers between devices with their start and end apart: 2 -> 2, of which waited for: 2 -> 2; matrix products, arithmetic and copies ran while one was open for 0% -> 1% of each run, Pallas kernels for 0% -> 0%
where the time goes in v1:
time: 239 us; the launch traced here: 235 us
  waiting for transfers between devices  181 us (76%)
  other arithmetic  17 us (7%)
  local copies, waits for them, and re-layouts  16.5 us (7%)
  between operations  14.1 us (6%)
  matrix products  6.13 us (3%)
    reduce_scatter x1, waiting for transfers between devices, local(): lax.psum_scatter(partial_stress, ('col', 'lag'), scatter_dimension=1, til...  121 us
    all_gather x1, waiting for transfers between devices, local(): gathered = lax.all_gather(history, 'row', axis=3, tiled=True)  59.3 us
    scatter-add x1, other arithmetic, local(): jnp.zeros((sims_count, row_blocks, tile_side), jnp.float32)  14.8 us
    unnamed x21, local copies, waits for them, and re-layouts  7.69 us
    scatter-add x1, local copies, waits for them, and re-layouts, local(): jnp.zeros((sims_count, row_blocks, tile_side), jnp.float32)  5.58 us
    dot_general x1, matrix products, local(): jnp.einsum('lksj,lkij->slki', picked, kernel_tiles[0, 0], preferred_eleme...  4.83 us
  transfers between devices with their start and end apart: 2, of which 2 were waited for; matrix products, arithmetic and copies ran while one was open for 1% of the time, Pallas kernels for 0%

profile of v1, /device:TPU:1, one launch (start us, length us, event | category | flops | bytes accessed | tf_op | source)
XLA Modules:
  0.0 234.7 jit_solution(9200661468580223937)
XLA Ops:
  7.2 0.0 all-gather.2.cloned.1.call-start
  7.2 0.7 all-gather.2.cloned.1.call-update
  7.9 0.0 reduce-scatter.2.cloned.1.call-start
  7.9 0.8 reshape_squeeze.3
  8.7 0.7 fusion.12
  9.4 59.3 %all-gather.2.cloned.1.call-done = bf16[4,1,128,4096]{3,2,1,0:T(8,128)(2,1)} async-done(((bf16[4,1,128,512]{3,2,1,0:T(8,128)(2,1)}), bf16[4,1,128,4096]{3,2,1,0:T(8,128)(2,1)}) %all-gather.2.cloned.1.call-update) | async-done | bytes 4194320 | tf_op jit(solution)/shard_map/all_gather | solution.py:25
  68.8 3.8 %copy.26 = bf16[64,8,16,256]{3,2,1,0:T(8,128)(2,1)S(1)} copy(bf16[64,8,16,256]{3,1,2,0:T(8,128)(2,1)} %bitcast.34) | data formatting | bytes 8388608
  72.5 0.0 slice-start.1
  72.5 1.3 fusion.2
  73.9 0.3 slice-done.1
  74.1 4.8 %broadcast_multiply_fusion = f32[4,12,128,256]{3,2,1,0:T(8,128)} fusion(f32[4,12]{1,0:T(4,128)S(1)} %fusion.12, bf16[1,1,4,12,256,256]{5,4,3,2,1,0:T(8,128)(2,1)S(1)} %bitcast.33, bf16[4,12,128,256]{3,1,2,0:T(8,128)(2,1)S(1)} %fusion.2), kind=kOutput, calls=%fused_computation.6 | convolution fusion | flops 806879232 | bytes 15728832 | tf_op jit(solution)/shard_map/lksj,lkij->slki/dot_general | solution.py:36
  79.0 2.5 %broadcast_in_dim.4 = f32[128,32,256]{2,0,1:T(8,128)} broadcast(f32[]{:T(128)} %constant.5.clone.1), dimensions={} | broadcast | bytes 4194308 | tf_op jit(solution)/shard_map/broadcast_in_dim | solution.py:47
  81.5 14.8 %scatter_fusion = f32[128,32,256]{2,0,1:T(8,128)} fusion(f32[128,32,256]{2,0,1:T(8,128)} %broadcast_in_dim.4, s32[48]{0:T(128)S(1)} %fusion.13, f32[48,128,256]{2,1,0:T(8,128)} %bitcast.29), kind=kCustom, calls=%fused_computation | custom fusion | flops 1572864 | bytes 18874560 | tf_op jit(solution)/shard_map/scatter-add | solution.py:47
  96.3 5.6 %copy.11 = f32[128,32,256]{0,2,1:T(8,128)} copy(f32[128,32,256]{2,0,1:T(8,128)} %scatter_fusion) | data formatting | bytes 8388608 | tf_op jit(solution)/shard_map/scatter-add | solution.py:47
  101.9 0.0 reduce-scatter.2.cloned.1.call-update
  101.9 0.9 copy-done
  102.8 0.1 copy.12
  102.9 0.1 copy.14
  103.0 0.1 copy.16
  103.1 0.1 copy.18
  103.2 120.8 %reduce-scatter.2.cloned.1.call-done = f32[128,256]{0,1:T(8,128)} async-done(((f32[128,8192]{0,1:T(8,128)}), f32[128,256]{0,1:T(8,128)}) %reduce-scatter.2.cloned.1.call-update) | async-done | bytes 131088 | tf_op jit(solution)/shard_map/reduce_scatter | solution.py:50
  224.0 1.5 divide_subtract_fusion
  225.5 0.8 copy.23
  226.2 1.7 copy.22
  (13 shorter events, 0.0 us)
Async XLA Ops:
  7.2 61.6 %all-gather.2.cloned.1.call-start = ((), (), s32[]{:S(2)}) async-start(), calls=%async_computation.1 | async-start | bytes 4718592 | tf_op jit(solution)/shard_map/all_gather | solution.py:25
  7.9 216.1 %reduce-scatter.2.cloned.1.call-start = ((), (), s32[]{:S(2)}) async-start(), calls=%async_computation.2 | async-start | bytes 4325376 | tf_op jit(solution)/shard_map/reduce_scatter | solution.py:50
  68.7 3.8 %copy-start.4 = (s32[1,1,4,12]{3,2,1,0:T(4,128)S(1)}, s32[1,1,4,12]{3,2,1,0:T(4,128)}, u32[]{:S(2)}) copy-start(s32[1,1,4,12]{3,2,1,0:T(4,128)} %param.12) | copy-start | bytes 580
  68.8 5.1 %slice-start = ((s8[6291456]{0:T(1024)(128)(4,1)}), s8[4194304]{0:T(1024)(128)(4,1)S(1)}, s32[]{:S(2)}) async-start(s8[6291456]{0:T(1024)(128)(4,1)} %bitcast.32), calls=%async_computation.3 | async-start | bytes 8388608
  72.5 1.6 slice-start.1
  101.9 0.9 copy-start
  101.9 1.0 copy-start.1
  101.9 1.1 copy-start.2
  101.9 1.2 copy-start.3
Sparse Core Ops, SparseCore 0:
  9.8 58.9 all-gather.1
  102.0 121.8 reduce-scatter.1

commit v2 on v1

--- a/solution.py
+++ b/solution.py
@@ -1,9 +1,14 @@
+import functools
+
 import jax
 import jax.numpy as jnp
 from jax import lax
+from jax.experimental import pallas as pl
+from jax.experimental.pallas import tpu as pltpu
 from jax.sharding import PartitionSpec as P
 
 NEWTON = 4
+MESH = pl.DeviceIdType.MESH
 
 
 def inverse_sinh(value):
@@ -11,7 +16,73 @@
     return jnp.sign(value) * jnp.log(magnitude + jnp.sqrt(1.0 + magnitude * magnitude))
 
 
+def scatter_kernel(n_col, n_lag, part_ref, out_ref, slots, send_sem, recv_sem):
+    row = lax.axis_index("row")
+    me = lax.axis_index("col") * n_lag + lax.axis_index("lag")
+    group = n_col * n_lag
+
+    def peer(t):
+        return (row, t // n_lag, t % n_lag)
+
+    barrier = pltpu.get_barrier_semaphore()
+    for d in range(1, group):
+        t = lax.rem(me + d, group)
+        pl.semaphore_signal(barrier, inc=1, device_id=peer(t), device_id_type=MESH)
+    pl.semaphore_wait(barrier, group - 1)
+
+    sends = []
+    for d in range(1, group):
+        t = lax.rem(me + d, group)
+        copy = pltpu.make_async_remote_copy(
+            src_ref=part_ref.at[t],
+            dst_ref=slots.at[me],
+            send_sem=send_sem.at[t],
+            recv_sem=recv_sem.at[me],
+            device_id=peer(t),
+            device_id_type=MESH,
+        )
+        copy.start()
+        sends.append(copy)
+
+    total = part_ref[me]
+    for d in range(1, group):
+        s = lax.rem(me + group - d, group)
+        incoming = pltpu.make_async_remote_copy(
+            src_ref=part_ref.at[s],
+            dst_ref=slots.at[s],
+            send_sem=send_sem.at[s],
+            recv_sem=recv_sem.at[s],
+            device_id=peer(s),
+            device_id_type=MESH,
+        )
+        incoming.wait_recv()
+        total = total + slots[s]
+    out_ref[...] = total
+    for copy in sends:
+        copy.wait_send()
+
+
+def reduce_scatter(part, n_col, n_lag):
+    group, sims, tile = part.shape
+    return pl.pallas_call(
+        functools.partial(scatter_kernel, n_col, n_lag),
+        out_shape=jax.ShapeDtypeStruct((sims, tile), jnp.float32),
+        in_specs=[pl.BlockSpec(memory_space=pltpu.VMEM)],
+        out_specs=pl.BlockSpec(memory_space=pltpu.VMEM),
+        scratch_shapes=[
+            pltpu.VMEM((group, sims, tile), jnp.float32),
+            pltpu.SemaphoreType.DMA((group,)),
+            pltpu.SemaphoreType.DMA((group,)),
+        ],
+        compiler_params=pltpu.CompilerParams(
+            collective_id=0, has_side_effects=True, vmem_limit_bytes=48 * 1024 * 1024
+        ),
+    )(part)
+
+
 def local(
+    n_col,
+    n_lag,
     history,
     kernel_tiles,
     tile_rows,
@@ -34,22 +105,18 @@
         "lkb,lsbj->lksj", choose, blocks, preferred_element_type=jnp.float32
     ).astype(jnp.bfloat16)
     contrib = jnp.einsum(
-        "lksj,lkij->slki", picked, kernel_tiles[0, 0], preferred_element_type=jnp.float32
+        "lksj,lkij->lksi", picked, kernel_tiles[0, 0], preferred_element_type=jnp.float32
     )
-    rec_local = base_stress.shape[1] * lax.axis_size(("col", "lag"))
-    row_blocks = rec_local // tile_side
+    row_blocks = n_col * n_lag
     alive_mask = (jnp.arange(slots)[None, :] < tile_count[0, 0][:, None]).astype(jnp.float32)
-    masked = (contrib * alive_mask[None, :, :, None]).reshape(
-        sims_count, lag_local * slots, tile_side
+    masked = (contrib * alive_mask[:, :, None, None]).reshape(
+        lag_local * slots, sims_count, tile_side
     )
     targets = tile_rows[0, 0].reshape(lag_local * slots)
     placed = (
-        jnp.zeros((sims_count, row_blocks, tile_side), jnp.float32).at[:, targets, :].add(masked)
+        jnp.zeros((row_blocks, sims_count, tile_side), jnp.float32).at[targets].add(masked)
     )
-    partial_stress = placed.reshape(sims_count, rec_local)
-    stress_change = lax.psum_scatter(
-        partial_stress, ("col", "lag"), scatter_dimension=1, tiled=True
-    )
+    stress_change = reduce_scatter(placed, n_col, n_lag)
     driving = base_stress + stress_change
     factor = jnp.exp(state_var) / 2.0
     velocity = prev_rate
@@ -63,7 +130,7 @@
 
 def solution(mesh):
     return jax.shard_map(
-        local,
+        functools.partial(local, mesh.shape["col"], mesh.shape["lag"]),
         mesh=mesh,
         in_specs=(
             P("lag", "col", None, "row"),

time: 239 us -> 210 us (0.88)
  waiting for transfers between devices: 181 us -> 60 us
  Pallas kernels: 0 us -> 99.6 us
  local copies, waits for them, and re-layouts: 16.5 us -> 10.2 us
    reduce_scatter x1 -> x0, waiting for transfers between devices: 121 us -> none  [local(): lax.psum_scatter(partial_stress, ('col', 'lag'), scatter_dimension=1, til...]
    pallas_call x0 -> x1, Pallas kernels: none -> 99.6 us  [reduce_scatter(): pl.pallas_call(functools.partial(scatter_kernel, n_col, n_lag), out_shape...]
    scatter-add x1 -> x0, local copies, waits for them, and re-layouts: 5.58 us -> none  [local(): jnp.zeros((sims_count, row_blocks, tile_side), jnp.float32)]
    unnamed x21 -> x18, local copies, waits for them, and re-layouts: 7.69 us -> 6.9 us
  transfers between devices with their start and end apart: 2 -> 1, of which waited for: 2 -> 1; matrix products, arithmetic and copies ran while one was open for 1% -> 1% of each run, Pallas kernels for 0% -> 0%
where the time goes in v2:
time: 210 us; the launch traced here: 207 us
  Pallas kernels  99.6 us (47%)
  waiting for transfers between devices  60 us (29%)
  other arithmetic  16.7 us (8%)
  between operations  14.1 us (7%)
  local copies, waits for them, and re-layouts  10.2 us (5%)
  matrix products  6.12 us (3%)
    pallas_call x1, Pallas kernels, reduce_scatter(): pl.pallas_call(functools.partial(scatter_kernel, n_col, n_lag), out_shape...  99.6 us
    all_gather x1, waiting for transfers between devices, local(): gathered = lax.all_gather(history, 'row', axis=3, tiled=True)  59.4 us
    scatter-add x1, other arithmetic, local(): jnp.zeros((row_blocks, sims_count, tile_side), jnp.float32).at[targets]  14.7 us
    unnamed x18, local copies, waits for them, and re-layouts  6.9 us
    dot_general x1, matrix products, local(): jnp.einsum('lksj,lkij->lksi', picked, kernel_tiles[0, 0], preferred_eleme...  4.83 us
  transfers between devices with their start and end apart: 1, of which 1 were waited for; matrix products, arithmetic and copies ran while one was open for 1% of the time, Pallas kernels for 0%

profile of v2, /device:TPU:1, one launch (start us, length us, event | category | flops | bytes accessed | tf_op | source)
XLA Modules:
  0.0 206.8 jit_solution(16552599969055120336)
XLA Ops:
  7.2 0.0 all-gather.2.cloned.1.call-start
  7.2 0.7 all-gather.2.cloned.1.call-update
  7.9 0.8 reshape_squeeze.3
  8.7 0.7 fusion.12
  9.4 59.4 %all-gather.2.cloned.1.call-done = bf16[4,1,128,4096]{3,2,1,0:T(8,128)(2,1)} async-done(((bf16[4,1,128,512]{3,2,1,0:T(8,128)(2,1)}), bf16[4,1,128,4096]{3,2,1,0:T(8,128)(2,1)}) %all-gather.2.cloned.1.call-update) | async-done | bytes 4194320 | tf_op jit(solution)/shard_map/all_gather | solution.py:96
  68.7 0.0 copy-start.1
  68.8 0.0 slice-start
  68.8 3.8 %copy.13 = bf16[64,8,16,256]{3,2,1,0:T(8,128)(2,1)S(1)} copy(bf16[64,8,16,256]{3,1,2,0:T(8,128)(2,1)} %bitcast.28) | data formatting | bytes 8388608
  72.5 0.0 slice-start.1
  72.5 0.0 copy-done.1
  72.5 1.3 fusion.2
  73.8 0.0 slice-done
  73.9 0.3 slice-done.1
  74.1 4.8 %broadcast_multiply_fusion = f32[4,12,128,256]{3,2,1,0:T(8,128)} fusion(f32[4,12]{1,0:T(4,128)S(1)} %fusion.12, bf16[1,1,4,12,256,256]{5,4,3,2,1,0:T(8,128)(2,1)S(1)} %bitcast.27, bf16[4,12,128,256]{3,1,2,0:T(8,128)(2,1)S(1)} %fusion.2), kind=kOutput, calls=%fused_computation.6 | convolution fusion | flops 806879232 | bytes 15728832 | tf_op jit(solution)/shard_map/lksj,lkij->lksi/dot_general | solution.py:107
  79.0 2.5 %broadcast_in_dim.4 = f32[32,128,256]{2,1,0:T(8,128)} broadcast(f32[]{:T(128)} %constant.5.clone.1), dimensions={} | broadcast | bytes 4194308 | tf_op jit(solution)/shard_map/broadcast_in_dim | solution.py:117
  81.5 14.7 %scatter_fusion = f32[32,128,256]{2,1,0:T(8,128)} fusion(f32[32,128,256]{2,1,0:T(8,128)} %broadcast_in_dim.4, s32[48]{0:T(128)S(1)} %fusion.13, f32[48,128,256]{2,1,0:T(8,128)} %bitcast.24), kind=kCustom, calls=%fused_computation | custom fusion | flops 1572864 | bytes 18874560 | tf_op jit(solution)/shard_map/scatter-add | solution.py:117
  96.1 2.2 %copy-done = f32[32,128,256]{2,1,0:T(8,128)S(1)} copy-done((f32[32,128,256]{2,1,0:T(8,128)S(1)}, f32[32,128,256]{2,1,0:T(8,128)}, u32[]{:S(2)}) %copy-start) | copy-done | bytes 4194328
  98.3 99.6 %shard_map.104 = f32[128,256]{1,0:T(8,128)S(1)} custom-call(f32[32,128,256]{2,1,0:T(8,128)S(1)} %copy-done), custom_call_target="tpu_custom_call" | custom-call | tf_op jit(solution)/shard_map/pallas_call | solution.py:67
  198.0 0.0 copy-done.2
  198.0 0.0 copy-done.3
  198.0 0.0 copy-done.4
  198.0 0.0 copy-done.5
  198.0 1.3 divide_subtract_fusion
  199.3 0.7 copy.20
  (7 shorter events, 0.0 us)
Async XLA Ops:
  7.2 61.6 %all-gather.2.cloned.1.call-start = ((), (), s32[]{:S(2)}) async-start(), calls=%async_computation | async-start | bytes 4718592 | tf_op jit(solution)/shard_map/all_gather | solution.py:96
  68.7 3.8 %copy-start.1 = (s32[1,1,4,12]{3,2,1,0:T(4,128)S(1)}, s32[1,1,4,12]{3,2,1,0:T(4,128)}, u32[]{:S(2)}) copy-start(s32[1,1,4,12]{3,2,1,0:T(4,128)} %param.12) | copy-start | bytes 580
  68.8 5.1 %slice-start = ((s8[6291456]{0:T(1024)(128)(4,1)}), s8[4194304]{0:T(1024)(128)(4,1)S(1)}, s32[]{:S(2)}) async-start(s8[6291456]{0:T(1024)(128)(4,1)} %bitcast.26), calls=%async_computation.1 | async-start | bytes 8388608
  72.5 1.6 slice-start.1
  96.1 2.2 %copy-start = (f32[32,128,256]{2,1,0:T(8,128)S(1)}, f32[32,128,256]{2,1,0:T(8,128)}, u32[]{:S(2)}) copy-start(f32[32,128,256]{2,1,0:T(8,128)} %scatter_fusion) | copy-start | bytes 12582916
  98.3 99.6 %copy-start.2 = (f32[128,256]{1,0:T(8,128)S(1)}, f32[128,256]{1,0:T(8,128)}, u32[]{:S(2)}) copy-start(f32[128,256]{1,0:T(8,128)} %param.16) | copy-start | bytes 393220
  98.3 99.7 %copy-start.3 = (f32[128,256]{1,0:T(8,128)S(1)}, f32[128,256]{1,0:T(8,128)}, u32[]{:S(2)}) copy-start(f32[128,256]{1,0:T(8,128)} %param.15) | copy-start | bytes 393220
  98.3 99.7 %copy-start.4 = (f32[128,256]{1,0:T(8,128)S(1)}, f32[128,256]{1,0:T(8,128)}, u32[]{:S(2)}) copy-start(f32[128,256]{1,0:T(8,128)} %param.14) | copy-start | bytes 393220
  98.3 99.7 %copy-start.5 = (f32[128,256]{1,0:T(8,128)S(1)}, f32[128,256]{1,0:T(8,128)}, u32[]{:S(2)}) copy-start(f32[128,256]{1,0:T(8,128)} %param.17) | copy-start | bytes 393220
Sparse Core Ops, SparseCore 0:
  9.8 58.9 all-gather.1

commit v3 on v2

--- a/solution.py
+++ b/solution.py
@@ -16,23 +16,23 @@
     return jnp.sign(value) * jnp.log(magnitude + jnp.sqrt(1.0 + magnitude * magnitude))
 
 
-def scatter_kernel(n_col, n_lag, part_ref, out_ref, slots, send_sem, recv_sem):
+def scatter_kernel(n_col, part_ref, out_ref, slots, send_sem, recv_sem):
     row = lax.axis_index("row")
-    me = lax.axis_index("col") * n_lag + lax.axis_index("lag")
-    group = n_col * n_lag
+    me = lax.axis_index("col")
+    lag = lax.axis_index("lag")
 
     def peer(t):
-        return (row, t // n_lag, t % n_lag)
+        return (row, t, lag)
 
     barrier = pltpu.get_barrier_semaphore()
-    for d in range(1, group):
-        t = lax.rem(me + d, group)
+    for d in range(1, n_col):
+        t = lax.rem(me + d, n_col)
         pl.semaphore_signal(barrier, inc=1, device_id=peer(t), device_id_type=MESH)
-    pl.semaphore_wait(barrier, group - 1)
+    pl.semaphore_wait(barrier, n_col - 1)
 
     sends = []
-    for d in range(1, group):
-        t = lax.rem(me + d, group)
+    for d in range(1, n_col):
+        t = lax.rem(me + d, n_col)
         copy = pltpu.make_async_remote_copy(
             src_ref=part_ref.at[t],
             dst_ref=slots.at[me],
@@ -45,8 +45,8 @@
         sends.append(copy)
 
     total = part_ref[me]
-    for d in range(1, group):
-        s = lax.rem(me + group - d, group)
+    for d in range(1, n_col):
+        s = lax.rem(me + n_col - d, n_col)
         incoming = pltpu.make_async_remote_copy(
             src_ref=part_ref.at[s],
             dst_ref=slots.at[s],
@@ -62,10 +62,10 @@
         copy.wait_send()
 
 
-def reduce_scatter(part, n_col, n_lag):
+def reduce_scatter(part, n_col):
     group, sims, tile = part.shape
     return pl.pallas_call(
-        functools.partial(scatter_kernel, n_col, n_lag),
+        functools.partial(scatter_kernel, n_col),
         out_shape=jax.ShapeDtypeStruct((sims, tile), jnp.float32),
         in_specs=[pl.BlockSpec(memory_space=pltpu.VMEM)],
         out_specs=pl.BlockSpec(memory_space=pltpu.VMEM),
@@ -116,7 +116,12 @@
     placed = (
         jnp.zeros((row_blocks, sims_count, tile_side), jnp.float32).at[targets].add(masked)
     )
-    stress_change = reduce_scatter(placed, n_col, n_lag)
+    by_chip = placed.reshape(n_col, n_lag, sims_count, tile_side)
+    lag = lax.axis_index("lag")
+    own = lax.dynamic_index_in_dim(by_chip, lag, axis=1, keepdims=False)
+    other = lax.dynamic_index_in_dim(by_chip, n_lag - 1 - lag, axis=1, keepdims=False)
+    from_partner = lax.ppermute(other, "lag", perm=[(0, 1), (1, 0)])
+    stress_change = reduce_scatter(own + from_partner, n_col)
     driving = base_stress + stress_change
     factor = jnp.exp(state_var) / 2.0
     velocity = prev_rate

time: 210 us -> 169 us (0.80); the launches traced: 207 us -> 168 us
  Pallas kernels: 99.6 us -> 53.2 us
  waiting for transfers between devices: 60 us -> 64 us
    pallas_call x1, Pallas kernels: 99.6 us -> 53.2 us  [reduce_scatter(): pl.pallas_call(functools.partial(scatter_kernel, n_col), out_shape=jax.Sh...]
    ppermute x0 -> x1, waiting for transfers between devices: none -> 3.99 us  [local(): from_partner = lax.ppermute(other, 'lag', perm=[(0, 1), (1, 0)])]
    squeeze x0 -> x1, local copies, waits for them, and re-layouts: none -> 3.11 us  [local(): lax.dynamic_index_in_dim(by_chip, n_lag - 1 - lag, axis=1, keepdims=False)]
    unnamed x18 -> x16, local copies, waits for them, and re-layouts: 6.9 us -> 4.71 us
  transfers between devices with their start and end apart: 1 -> 2, of which waited for: 1 -> 2; matrix products, arithmetic and copies ran while one was open for 1% -> 1% of each run, Pallas kernels for 0% -> 0%
where the time goes in v3:
time: 169 us; the launch traced here: 168 us
  waiting for transfers between devices  64 us (38%)
  Pallas kernels  53.2 us (31%)
  other arithmetic  18.5 us (11%)
  between operations  14.1 us (8%)
  local copies, waits for them, and re-layouts  11.1 us (7%)
  matrix products  6.12 us (4%)
    all_gather x1, waiting for transfers between devices, local(): gathered = lax.all_gather(history, 'row', axis=3, tiled=True)  59.3 us
    pallas_call x1, Pallas kernels, reduce_scatter(): pl.pallas_call(functools.partial(scatter_kernel, n_col), out_shape=jax.Sh...  53.2 us
    scatter-add x1, other arithmetic, local(): jnp.zeros((row_blocks, sims_count, tile_side), jnp.float32).at[targets]  14.7 us
    dot_general x1, matrix products, local(): jnp.einsum('lksj,lkij->lksi', picked, kernel_tiles[0, 0], preferred_eleme...  4.83 us
    unnamed x16, local copies, waits for them, and re-layouts  4.71 us
    ppermute x1, waiting for transfers between devices, local(): from_partner = lax.ppermute(other, 'lag', perm=[(0, 1), (1, 0)])  3.99 us
  transfers between devices with their start and end apart: 2, of which 2 were waited for; matrix products, arithmetic and copies ran while one was open for 1% of the time, Pallas kernels for 0%

profile of v3, /device:TPU:1, one launch (start us, length us, event | category | flops | bytes accessed | tf_op | source)
XLA Modules:
  0.0 167.9 jit_solution(12132615841135069499)
XLA Ops:
  7.2 0.0 all-gather.2.cloned.1.call-start
  7.2 0.7 all-gather.2.cloned.1.call-update
  7.9 0.8 reshape_squeeze.3
  8.7 0.7 fusion.12
  9.4 59.3 %all-gather.2.cloned.1.call-done = bf16[4,1,128,4096]{3,2,1,0:T(8,128)(2,1)} async-done(((bf16[4,1,128,512]{3,2,1,0:T(8,128)(2,1)}), bf16[4,1,128,4096]{3,2,1,0:T(8,128)(2,1)}) %all-gather.2.cloned.1.call-update) | async-done | bytes 4194320 | tf_op jit(solution)/shard_map/all_gather | solution.py:96
  68.8 3.8 %copy.13 = bf16[64,8,16,256]{3,2,1,0:T(8,128)(2,1)S(1)} copy(bf16[64,8,16,256]{3,1,2,0:T(8,128)(2,1)} %bitcast.35) | data formatting | bytes 8388608
  72.5 0.0 slice-start.1
  72.5 0.0 copy-done
  72.5 1.3 fusion.2
  73.8 0.0 slice-done
  73.9 0.3 slice-done.1
  74.1 4.8 %broadcast_multiply_fusion = f32[4,12,128,256]{3,2,1,0:T(8,128)} fusion(f32[4,12]{1,0:T(4,128)S(1)} %fusion.12, bf16[1,1,4,12,256,256]{5,4,3,2,1,0:T(8,128)(2,1)S(1)} %bitcast.34, bf16[4,12,128,256]{3,1,2,0:T(8,128)(2,1)S(1)} %fusion.2), kind=kOutput, calls=%fused_computation.6 | convolution fusion | flops 806879232 | bytes 15728832 | tf_op jit(solution)/shard_map/lksj,lkij->lksi/dot_general | solution.py:107
  79.0 2.5 %broadcast_in_dim.4 = f32[32,128,256]{2,1,0:T(8,128)} broadcast(f32[]{:T(128)} %constant.9.clone.1), dimensions={} | broadcast | bytes 4194308 | tf_op jit(solution)/shard_map/broadcast_in_dim | solution.py:117
  81.5 14.7 %scatter_fusion = f32[32,128,256]{2,1,0:T(8,128)} fusion(f32[32,128,256]{2,1,0:T(8,128)} %broadcast_in_dim.4, s32[48]{0:T(128)S(1)} %fusion.13, f32[48,128,256]{2,1,0:T(8,128)} %bitcast.31), kind=kCustom, calls=%fused_computation | custom fusion | flops 1572864 | bytes 18874560 | tf_op jit(solution)/shard_map/scatter-add | solution.py:117
  96.1 3.1 %dynamic-slice_bitcast_fusion = f32[16,128,256]{2,1,0:T(8,128)} fusion(f32[16,2,128,256]{3,2,1,0:T(8,128)} %bitcast.29, s32[]{:T(128)S(6)} %select_n.19), kind=kLoop, calls=%fused_computation.8 | loop fusion | bytes 4194308 | tf_op jit(solution)/shard_map/jit(dynamic_index_in_dim)/squeeze | solution.py:122
  99.2 0.8 collective-permute-start
  100.0 4.0 %collective-permute-done = f32[16,128,256]{2,1,0:T(8,128)S(1)} collective-permute-done((f32[16,128,256]{2,1,0:T(8,128)}, f32[16,128,256]{2,1,0:T(8,128)S(1)}, u32[]{:S(2)}, u32[]{:S(2)}) %collective-permute-start) | collective-permute-done | bytes 2097184 | tf_op jit(solution)/shard_map/ppermute | solution.py:123
  104.0 1.9 %bitcast_add_fusion.part_ref = f32[16,128,256]{2,1,0:T(8,128)S(1)} fusion(f32[16,128,256]{2,1,0:T(8,128)S(1)} %collective-permute-done, f32[16,2,128,256]{3,2,1,0:T(8,128)} %bitcast.30, s32[]{:T(128)S(6)} %select_n.18), kind=kLoop, calls=%fused_computation.7 | loop fusion | flops 524288 | bytes 6291460 | tf_op jit(solution)/shard_map/add | solution.py:124
  105.9 53.2 %shard_map.104 = f32[128,256]{1,0:T(8,128)S(1)} custom-call(f32[16,128,256]{2,1,0:T(8,128)S(1)} %bitcast_add_fusion.part_ref), custom_call_target="tpu_custom_call" | custom-call | tf_op jit(solution)/shard_map/pallas_call | solution.py:67
  159.1 0.0 copy-done.1
  159.1 0.0 copy-done.2
  159.1 0.0 copy-done.3
  159.1 1.3 divide_subtract_fusion
  160.4 0.7 copy.20
  (9 shorter events, 0.0 us)
Async XLA Ops:
  7.2 61.6 %all-gather.2.cloned.1.call-start = ((), (), s32[]{:S(2)}) async-start(), calls=%async_computation | async-start | bytes 4718592 | tf_op jit(solution)/shard_map/all_gather | solution.py:96
  68.7 3.8 %copy-start = (s32[1,1,4,12]{3,2,1,0:T(4,128)S(1)}, s32[1,1,4,12]{3,2,1,0:T(4,128)}, u32[]{:S(2)}) copy-start(s32[1,1,4,12]{3,2,1,0:T(4,128)} %param.12) | copy-start | bytes 580
  68.8 5.1 %slice-start = ((s8[6291456]{0:T(1024)(128)(4,1)}), s8[4194304]{0:T(1024)(128)(4,1)S(1)}, s32[]{:S(2)}) async-start(s8[6291456]{0:T(1024)(128)(4,1)} %bitcast.33), calls=%async_computation.1 | async-start | bytes 8388608
  72.5 1.6 slice-start.1
  99.2 4.8 %collective-permute-start = (f32[16,128,256]{2,1,0:T(8,128)}, f32[16,128,256]{2,1,0:T(8,128)S(1)}, u32[]{:S(2)}, u32[]{:S(2)}) collective-permute-start(f32[16,128,256]{2,1,0:T(8,128)} %dynamic-slice_bitcast_fusion), channel_id=1, source_target_pairs={{0,1},{1,0},{2,3},{3,2},{4,5},{5,4},{6,7},{7,6},{8,9},{9,8},{10,11... | collective-permute-start | bytes 6291464 | tf_op jit(solution)/shard_map/ppermute | solution.py:123
  100.0 59.1 %copy-start.1 = (f32[128,256]{1,0:T(8,128)S(1)}, f32[128,256]{1,0:T(8,128)}, u32[]{:S(2)}) copy-start(f32[128,256]{1,0:T(8,128)} %param.16) | copy-start | bytes 393220
  100.0 59.1 %copy-start.2 = (f32[128,256]{1,0:T(8,128)S(1)}, f32[128,256]{1,0:T(8,128)}, u32[]{:S(2)}) copy-start(f32[128,256]{1,0:T(8,128)} %param.15) | copy-start | bytes 393220
  100.0 59.1 %copy-start.3 = (f32[128,256]{1,0:T(8,128)S(1)}, f32[128,256]{1,0:T(8,128)}, u32[]{:S(2)}) copy-start(f32[128,256]{1,0:T(8,128)} %param.14) | copy-start | bytes 393220
  100.0 59.1 %copy-start.4 = (f32[128,256]{1,0:T(8,128)S(1)}, f32[128,256]{1,0:T(8,128)}, u32[]{:S(2)}) copy-start(f32[128,256]{1,0:T(8,128)} %param.17) | copy-start | bytes 393220
Sparse Core Ops, SparseCore 0:
  9.8 58.9 all-gather.1

commit v4 on v3

--- a/solution.py
+++ b/solution.py
@@ -80,6 +80,51 @@
     )(part)
 
 
+def parts_kernel(n_lag, rows_ref, cols_ref, count_ref, lag_ref, hist_ref, tiles_ref, out_ref):
+    lag = pl.program_id(0)
+    slots = tiles_ref.shape[1]
+    side = tiles_ref.shape[2]
+
+    @pl.when(lag == 0)
+    def _():
+        out_ref[...] = jnp.zeros_like(out_ref)
+
+    for k in range(slots):
+        @pl.when(k < count_ref[lag])
+        def _():
+            col = cols_ref[lag * slots + k]
+            row = rows_ref[lag * slots + k]
+            start = pl.multiple_of(col * side, side)
+            history = hist_ref[0, :, pl.ds(start, side)]
+            contrib = lax.dot_general(
+                history, tiles_ref[0, k], (((1,), (1,)), ((), ())),
+                preferred_element_type=jnp.float32,
+            )
+            half = jnp.where(row % n_lag == lag_ref[0], 0, 1)
+            out_ref[half, row // n_lag] += contrib
+
+
+def stress_parts(history, tiles, rows, cols, count, n_col, n_lag):
+    lags, sims, sources = history.shape
+    _, slots, side, _ = tiles.shape
+    lag = lax.axis_index("lag").astype(jnp.int32).reshape(1)
+    grid_spec = pltpu.PrefetchScalarGridSpec(
+        num_scalar_prefetch=4,
+        grid=(lags,),
+        in_specs=[
+            pl.BlockSpec((1, sims, sources), lambda l, *_: (l, 0, 0)),
+            pl.BlockSpec((1, slots, side, side), lambda l, *_: (l, 0, 0, 0)),
+        ],
+        out_specs=pl.BlockSpec((2, n_col, sims, side), lambda l, *_: (0, 0, 0, 0)),
+    )
+    return pl.pallas_call(
+        functools.partial(parts_kernel, n_lag),
+        out_shape=jax.ShapeDtypeStruct((2, n_col, sims, side), jnp.float32),
+        grid_spec=grid_spec,
+        compiler_params=pltpu.CompilerParams(vmem_limit_bytes=48 * 1024 * 1024),
+    )(rows.reshape(-1), cols.reshape(-1), count, lag, history, tiles)
+
+
 def local(
     n_col,
     n_lag,
@@ -94,32 +139,10 @@
     state_var,
 ):
     gathered = lax.all_gather(history, "row", axis=3, tiled=True)
-    lag_local = gathered.shape[0]
-    sims_count = gathered.shape[2]
     tile_side = kernel_tiles.shape[4]
-    slots = kernel_tiles.shape[3]
-    col_blocks = gathered.shape[3] // tile_side
-    blocks = gathered.reshape(lag_local, sims_count, col_blocks, tile_side)
-    choose = jax.nn.one_hot(tile_cols[0, 0], col_blocks, dtype=jnp.bfloat16)
-    picked = jnp.einsum(
-        "lkb,lsbj->lksj", choose, blocks, preferred_element_type=jnp.float32
-    ).astype(jnp.bfloat16)
-    contrib = jnp.einsum(
-        "lksj,lkij->lksi", picked, kernel_tiles[0, 0], preferred_element_type=jnp.float32
-    )
-    row_blocks = n_col * n_lag
-    alive_mask = (jnp.arange(slots)[None, :] < tile_count[0, 0][:, None]).astype(jnp.float32)
-    masked = (contrib * alive_mask[:, :, None, None]).reshape(
-        lag_local * slots, sims_count, tile_side
-    )
-    targets = tile_rows[0, 0].reshape(lag_local * slots)
-    placed = (
-        jnp.zeros((row_blocks, sims_count, tile_side), jnp.float32).at[targets].add(masked)
-    )
-    by_chip = placed.reshape(n_col, n_lag, sims_count, tile_side)
-    lag = lax.axis_index("lag")
-    own = lax.dynamic_index_in_dim(by_chip, lag, axis=1, keepdims=False)
-    other = lax.dynamic_index_in_dim(by_chip, n_lag - 1 - lag, axis=1, keepdims=False)
+    parts = stress_parts(gathered[:, 0], kernel_tiles[0, 0], tile_rows[0, 0],
+                         tile_cols[0, 0], tile_count[0, 0], n_col, n_lag)
+    own, other = parts[0], parts[1]
     from_partner = lax.ppermute(other, "lag", perm=[(0, 1), (1, 0)])
     stress_change = reduce_scatter(own + from_partner, n_col)
     driving = base_stress + stress_change

time: 169 us -> 148 us (0.88)
  other arithmetic: 18.5 us -> 1.69 us
  Pallas kernels: 53.2 us -> 62.6 us
  local copies, waits for them, and re-layouts: 11.1 us -> 3 us
  matrix products: 6.12 us -> 0 us
    scatter-add x1 -> x0, other arithmetic: 14.7 us -> none  [local(): jnp.zeros((row_blocks, sims_count, tile_side), jnp.float32).at[targets]]
    pallas_call x0 -> x1, Pallas kernels: none -> 9.81 us  [stress_parts(): pl.pallas_call(functools.partial(parts_kernel, n_lag), out_shape=jax.Shap...]
    dot_general x2 -> x0, matrix products: 6.12 us -> none  [the longest x1 4.83 us: local(): jnp.einsum('lksj,lkij->lksi', picked, kernel_tiles[0, 0], preferred_eleme...]
    unnamed x16 -> x11, local copies, waits for them, and re-layouts: 4.71 us -> 1.33 us
    squeeze x1, local copies, waits for them, and re-layouts: 3.11 us -> 0.14 us  [local(): own, other = (parts[0], parts[1])]
    broadcast_in_dim x1 -> x0, local copies, waits for them, and re-layouts: 2.51 us -> none  [local(): jnp.zeros((row_blocks, sims_count, tile_side), jnp.float32).at[targets]]
where the time goes in v4:
time: 148 us; the launch traced here: 146 us
  waiting for transfers between devices  64.1 us (43%)
  Pallas kernels  62.6 us (42%)
  between operations  14.1 us (10%)
  local copies, waits for them, and re-layouts  3 us (2%)
  other arithmetic  1.69 us (1%)
    all_gather x1, waiting for transfers between devices, local(): gathered = lax.all_gather(history, 'row', axis=3, tiled=True)  59.3 us
    pallas_call x1, Pallas kernels, reduce_scatter(): pl.pallas_call(functools.partial(scatter_kernel, n_col), out_shape=jax.Sh...  52.7 us
    pallas_call x1, Pallas kernels, stress_parts(): pl.pallas_call(functools.partial(parts_kernel, n_lag), out_shape=jax.Shap...  9.81 us
    ppermute x1, waiting for transfers between devices, local(): from_partner = lax.ppermute(other, 'lag', perm=[(0, 1), (1, 0)])  4.15 us
  transfers between devices with their start and end apart: 2, of which 2 were waited for; matrix products, arithmetic and copies ran while one was open for 1% of the time, Pallas kernels for 0%

profile of v4, /device:TPU:1, one launch (start us, length us, event | category | flops | bytes accessed | tf_op | source)
XLA Modules:
  0.0 145.7 jit_solution(3018936040992939904)
XLA Ops:
  7.2 0.0 all-gather.2.cloned.1.call-start
  7.2 0.7 all-gather.2.cloned.1.call-update
  7.9 0.8 reshape_squeeze.6.rows_ref
  8.7 0.8 reshape_squeeze.7.cols_ref
  9.4 59.3 %all-gather.2.cloned.1.call-done = bf16[4,1,128,4096]{3,2,0,1:T(8,128)(2,1)} async-done(((bf16[4,1,128,512]{3,2,0,1:T(8,128)(2,1)}), bf16[4,1,128,4096]{3,2,0,1:T(8,128)(2,1)}) %all-gather.2.cloned.1.call-update) | async-done | bytes 4194320 | tf_op jit(solution)/shard_map/all_gather | solution.py:141
  68.7 0.0 copy-start
  68.8 0.7 copy-done
  69.4 9.8 %shard_map.104 = f32[2,16,128,256]{3,2,1,0:T(8,128)S(1)} custom-call(s32[48]{0:T(128)S(1)} %reshape_squeeze.6.rows_ref, s32[48]{0:T(128)S(1)} %reshape_squeeze.7.cols_ref, s32[4]{0:T(128)S(1)} %bitcast.11, s32[1]{0:T(128)} %bitcast.1.lag_ref, bf16[4,128,4096]{2,1,0:T(8,128)(2,1)} %bitcast.13, bf16[4,12,256,256]{3,2,1,0:T(8,128)(2,1)} %bitcast.12), custom_call_target="tpu_custom_call" | custom-call | tf_op jit(solution)/shard_map/pallas_call | solution.py:120
  79.2 0.1 slice_bitcast_fusion
  79.4 0.1 collective-permute-start
  79.5 4.1 %collective-permute-done = f32[16,128,256]{2,1,0:T(8,128)S(1)} collective-permute-done((f32[16,128,256]{2,1,0:T(8,128)S(1)}, f32[16,128,256]{2,1,0:T(8,128)S(1)}, u32[]{:S(2)}, u32[]{:S(2)}) %collective-permute-start) | collective-permute-done | bytes 2097184 | tf_op jit(solution)/shard_map/ppermute | solution.py:146
  83.6 0.4 fusion.part_ref
  84.0 0.0 copy-start.1
  84.0 0.0 copy-start.2
  84.1 0.0 copy-start.3
  84.1 0.0 copy-start.4
  84.1 52.7 %shard_map.105 = f32[128,256]{1,0:T(8,128)S(1)} custom-call(f32[16,128,256]{2,1,0:T(8,128)S(1)} %fusion.part_ref), custom_call_target="tpu_custom_call" | custom-call | tf_op jit(solution)/shard_map/pallas_call | solution.py:67
  136.8 0.0 copy-done.1
  136.8 0.0 copy-done.2
  136.9 0.0 copy-done.3
  136.9 0.0 copy-done.4
  136.9 1.3 divide_subtract_fusion
  138.2 0.7 copy.13
Async XLA Ops:
  7.2 61.6 %all-gather.2.cloned.1.call-start = ((), (), s32[]{:S(2)}) async-start(), calls=%async_computation | async-start | bytes 4718592 | tf_op jit(solution)/shard_map/all_gather | solution.py:141
  68.7 0.7 copy-start
  79.4 4.2 %collective-permute-start = (f32[16,128,256]{2,1,0:T(8,128)S(1)}, f32[16,128,256]{2,1,0:T(8,128)S(1)}, u32[]{:S(2)}, u32[]{:S(2)}) collective-permute-start(f32[16,128,256]{2,1,0:T(8,128)S(1)} %slice_bitcast_fusion), channel_id=1, source_target_pairs={{0,1},{1,0},{2,3},{3,2},{4,5},{5,4},{6,7},{7,6},{8,9},{9,8},{10,11... | collective-permute-start | bytes 6291464 | tf_op jit(solution)/shard_map/ppermute | solution.py:146
  84.0 52.8 %copy-start.1 = (f32[128,256]{1,0:T(8,128)S(1)}, f32[128,256]{1,0:T(8,128)}, u32[]{:S(2)}) copy-start(f32[128,256]{1,0:T(8,128)} %param.16) | copy-start | bytes 393220
  84.0 52.8 %copy-start.2 = (f32[128,256]{1,0:T(8,128)S(1)}, f32[128,256]{1,0:T(8,128)}, u32[]{:S(2)}) copy-start(f32[128,256]{1,0:T(8,128)} %param.15) | copy-start | bytes 393220
  84.1 52.8 %copy-start.3 = (f32[128,256]{1,0:T(8,128)S(1)}, f32[128,256]{1,0:T(8,128)}, u32[]{:S(2)}) copy-start(f32[128,256]{1,0:T(8,128)} %param.14) | copy-start | bytes 393220
  84.1 52.8 %copy-start.4 = (f32[128,256]{1,0:T(8,128)S(1)}, f32[128,256]{1,0:T(8,128)}, u32[]{:S(2)}) copy-start(f32[128,256]{1,0:T(8,128)} %param.17) | copy-start | bytes 393220
Sparse Core Ops, SparseCore 0:
  9.8 58.9 all-gather.1

commit v5 on v4

--- a/solution.py
+++ b/solution.py
@@ -62,7 +62,7 @@
         copy.wait_send()
 
 
-def reduce_scatter(part, n_col):
+def reduce_scatter(part, n_col, collective_id):
     group, sims, tile = part.shape
     return pl.pallas_call(
         functools.partial(scatter_kernel, n_col),
@@ -75,12 +75,13 @@
             pltpu.SemaphoreType.DMA((group,)),
         ],
         compiler_params=pltpu.CompilerParams(
-            collective_id=0, has_side_effects=True, vmem_limit_bytes=48 * 1024 * 1024
+            collective_id=collective_id, has_side_effects=True, vmem_limit_bytes=48 * 1024 * 1024
         ),
     )(part)
 
 
-def parts_kernel(n_lag, rows_ref, cols_ref, count_ref, lag_ref, hist_ref, tiles_ref, out_ref):
+def parts_kernel(n_lag, rows_ref, cols_ref, count_ref, lag_ref, hist_ref, tiles_ref, *rest):
+    out_ref = rest[-1]
     lag = pl.program_id(0)
     slots = tiles_ref.shape[1]
     side = tiles_ref.shape[2]
@@ -104,7 +105,7 @@
             out_ref[half, row // n_lag] += contrib
 
 
-def stress_parts(history, tiles, rows, cols, count, n_col, n_lag):
+def stress_parts(history, tiles, rows, cols, count, n_col, n_lag, after=()):
     lags, sims, sources = history.shape
     _, slots, side, _ = tiles.shape
     lag = lax.axis_index("lag").astype(jnp.int32).reshape(1)
@@ -114,7 +115,7 @@
         in_specs=[
             pl.BlockSpec((1, sims, sources), lambda l, *_: (l, 0, 0)),
             pl.BlockSpec((1, slots, side, side), lambda l, *_: (l, 0, 0, 0)),
-        ],
+        ] + [pl.BlockSpec(memory_space=pl.ANY) for _ in after],
         out_specs=pl.BlockSpec((2, n_col, sims, side), lambda l, *_: (0, 0, 0, 0)),
     )
     return pl.pallas_call(
@@ -122,7 +123,7 @@
         out_shape=jax.ShapeDtypeStruct((2, n_col, sims, side), jnp.float32),
         grid_spec=grid_spec,
         compiler_params=pltpu.CompilerParams(vmem_limit_bytes=48 * 1024 * 1024),
-    )(rows.reshape(-1), cols.reshape(-1), count, lag, history, tiles)
+    )(rows.reshape(-1), cols.reshape(-1), count, lag, history, tiles, *after)
 
 
 def local(
@@ -138,13 +139,18 @@
     direct_effect,
     state_var,
 ):
-    gathered = lax.all_gather(history, "row", axis=3, tiled=True)
-    tile_side = kernel_tiles.shape[4]
-    parts = stress_parts(gathered[:, 0], kernel_tiles[0, 0], tile_rows[0, 0],
-                         tile_cols[0, 0], tile_count[0, 0], n_col, n_lag)
-    own, other = parts[0], parts[1]
-    from_partner = lax.ppermute(other, "lag", perm=[(0, 1), (1, 0)])
-    stress_change = reduce_scatter(own + from_partner, n_col)
+    n_chunks = 2
+    chunk = history.shape[2] // n_chunks
+    pieces = []
+    for index in range(n_chunks):
+        sims = slice(index * chunk, (index + 1) * chunk)
+        gathered = lax.all_gather(history[:, :, sims], "row", axis=3, tiled=True)
+        parts = stress_parts(gathered[:, 0], kernel_tiles[0, 0], tile_rows[0, 0],
+                             tile_cols[0, 0], tile_count[0, 0], n_col, n_lag,
+                             after=tuple(pieces[-1:]))
+        from_partner = lax.ppermute(parts[1], "lag", perm=[(0, 1), (1, 0)])
+        pieces.append(reduce_scatter(parts[0] + from_partner, n_col, index))
+    stress_change = jnp.concatenate(pieces, axis=0)
     driving = base_stress + stress_change
     factor = jnp.exp(state_var) / 2.0
     velocity = prev_rate

time: 148 us -> 161 us (1.088)
  Pallas kernels: 62.6 us -> 81.5 us
  waiting for transfers between devices: 64.1 us -> 46.8 us
  starting transfers between devices: 0.13 us -> 6.04 us
  local copies, waits for them, and re-layouts: 3 us -> 7.52 us
    all_gather x1 -> x2, waiting for transfers between devices: 59.3 us -> 41.5 us  [local(): gathered = lax.all_gather(history[:, :, sims], 'row', axis=3, tiled=True)]
    pallas_call x1 -> x2, Pallas kernels: 52.7 us -> 62.5 us  [reduce_scatter(): pl.pallas_call(functools.partial(scatter_kernel, n_col), out_shape=jax.Sh...]
    pallas_call x1 -> x2, Pallas kernels: 9.81 us -> 19 us  [stress_parts(): pl.pallas_call(functools.partial(parts_kernel, n_lag), out_shape=jax.Shap...]
    ppermute x1 -> x2, starting transfers between devices: 0.09 us -> 5.96 us  [local(): from_partner = lax.ppermute(parts[1], 'lag', perm=[(0, 1), (1, 0)])]
    unnamed x11 -> x16, local copies, waits for them, and re-layouts: 1.33 us -> 3.86 us
    slice x0 -> x1, local copies, waits for them, and re-layouts: none -> 1.87 us  [local(): gathered = lax.all_gather(history[:, :, sims], 'row', axis=3, tiled=True)]
    ppermute x1 -> x2, waiting for transfers between devices: 4.15 us -> 4.66 us  [local(): from_partner = lax.ppermute(parts[1], 'lag', perm=[(0, 1), (1, 0)])]
  transfers between devices with their start and end apart: 2 -> 4, of which waited for: 2 -> 3; matrix products, arithmetic and copies ran while one was open for 1% -> 1% of each run, Pallas kernels for 0% -> 27%
where the time goes in v5:
time: 161 us; the launch traced here: 158 us
  Pallas kernels  81.5 us (51%)
  waiting for transfers between devices  46.8 us (29%)
  between operations  14.2 us (9%)
  local copies, waits for them, and re-layouts  7.52 us (5%)
  starting transfers between devices  6.04 us (4%)
    pallas_call x2, Pallas kernels, reduce_scatter(): pl.pallas_call(functools.partial(scatter_kernel, n_col), out_shape=jax.Sh...  62.5 us
    all_gather x2, waiting for transfers between devices, local(): gathered = lax.all_gather(history[:, :, sims], 'row', axis=3, tiled=True)  41.5 us
    pallas_call x2, Pallas kernels, stress_parts(): pl.pallas_call(functools.partial(parts_kernel, n_lag), out_shape=jax.Shap...  19 us
    ppermute x2, starting transfers between devices, local(): from_partner = lax.ppermute(parts[1], 'lag', perm=[(0, 1), (1, 0)])  5.96 us
    ppermute x2, waiting for transfers between devices, local(): from_partner = lax.ppermute(parts[1], 'lag', perm=[(0, 1), (1, 0)])  4.66 us
    unnamed x16, local copies, waits for them, and re-layouts  3.86 us
  transfers between devices with their start and end apart: 4, of which 3 were waited for; matrix products, arithmetic and copies ran while one was open for 1% of the time, Pallas kernels for 27%

profile of v5, /device:TPU:1, one launch (start us, length us, event | category | flops | bytes accessed | tf_op | source)
XLA Modules:
  0.0 157.6 jit_solution(6928161185028401204)
XLA Ops:
  7.2 0.0 all-gather.3.cloned.1.call-start
  7.2 1.9 %fusion.5 = (bf16[4,1,64,512]{3,2,0,1:T(8,128)(2,1)}, bf16[4,1,64,512]{3,2,0,1:T(8,128)(2,1)}) fusion(bf16[4,1,128,512]{3,2,0,1:T(8,128)(2,1)} %bitcast.24), kind=kLoop, calls=%fused_computation.15 | loop fusion | bytes 1048576 | tf_op jit(solution)/shard_map/slice | solution.py:147
  9.1 0.0 all-gather.5.cloned.1.call-start
  9.2 0.7 all-gather.5.cloned.1.call-update
  9.9 0.8 reshape_squeeze.8.rows_ref
  10.6 0.8 reshape_squeeze.9.cols_ref
  11.4 41.5 %all-gather.3.cloned.1.call-done = bf16[4,1,64,4096]{3,2,0,1:T(8,128)(2,1)} async-done(((bf16[4,1,64,512]{3,2,0,1:T(8,128)(2,1)}), bf16[4,1,64,4096]{3,2,0,1:T(8,128)(2,1)}) %all-gather.3.cloned.1.call-update) | async-done | bytes 2097168 | tf_op jit(solution)/shard_map/all_gather | solution.py:147
  52.8 1.6 %copy-done.1 = bf16[4,1,64,4096]{3,2,0,1:T(8,128)(2,1)S(1)} copy-done((bf16[4,1,64,4096]{3,2,0,1:T(8,128)(2,1)S(1)}, bf16[4,1,64,4096]{3,2,0,1:T(8,128)(2,1)}, u32[]{:S(2)}) %copy-start.1) | copy-done | bytes 2097176
  54.4 0.7 copy-done.2
  55.1 9.5 %shard_map.104 = f32[2,16,64,256]{3,2,1,0:T(8,128)S(1)} custom-call(s32[48]{0:T(128)S(1)} %reshape_squeeze.8.rows_ref, s32[48]{0:T(128)S(1)} %reshape_squeeze.9.cols_ref, s32[4]{0:T(128)S(1)} %bitcast.20, s32[1]{0:T(128)} %bitcast.1.lag_ref, bf16[4,64,4096]{2,1,0:T(8,128)(2,1)S(1)} %bitcast.19, bf16[4,12,256,256]{3,2,1,0:T(8,128)(2,1)} %bitcast.22), custom_call_target="tpu_custom_call" | custom-call | tf_op jit(solution)/shard_map/pallas_call | solution.py:121
  64.6 0.1 slice_bitcast_fusion.2
  64.7 5.6 %collective-permute-start = (f32[16,64,256]{2,1,0:T(8,128)S(1)}, f32[16,64,256]{2,1,0:T(8,128)S(1)}, u32[]{:S(2)}, u32[]{:S(2)}) collective-permute-start(f32[16,64,256]{2,1,0:T(8,128)S(1)} %slice_bitcast_fusion.2), channel_id=1, source_target_pairs={{0,1},{1,0},{2,3},{3,2},{4,5},{5,4},{6,7},{7,6},{8,9},{9,8},{10,11... | collective-permute-start | bytes 3145736 | tf_op jit(solution)/shard_map/ppermute | solution.py:151
  70.3 2.3 %collective-permute-done = f32[16,64,256]{2,1,0:T(8,128)S(1)} collective-permute-done((f32[16,64,256]{2,1,0:T(8,128)S(1)}, f32[16,64,256]{2,1,0:T(8,128)S(1)}, u32[]{:S(2)}, u32[]{:S(2)}) %collective-permute-start) | collective-permute-done | bytes 1048608 | tf_op jit(solution)/shard_map/ppermute | solution.py:151
  72.6 0.1 fusion.1.part_ref
  72.8 33.8 %shard_map.105.rest_0_ = f32[64,256]{1,0:T(8,128)S(1)} custom-call(f32[16,64,256]{2,1,0:T(8,128)S(1)} %fusion.1.part_ref), custom_call_target="tpu_custom_call" | custom-call | tf_op jit(solution)/shard_map/pallas_call | solution.py:67
  106.5 0.0 all-gather.5.cloned.1.call-done
  106.6 1.6 %copy-done = bf16[4,1,64,4096]{3,2,0,1:T(8,128)(2,1)S(1)} copy-done((bf16[4,1,64,4096]{3,2,0,1:T(8,128)(2,1)S(1)}, bf16[4,1,64,4096]{3,2,0,1:T(8,128)(2,1)}, u32[]{:S(2)}) %copy-start) | copy-done | bytes 2097176
  108.2 9.5 %shard_map.106 = f32[2,16,64,256]{3,2,1,0:T(8,128)S(1)} custom-call(s32[48]{0:T(128)S(1)} %reshape_squeeze.8.rows_ref, s32[48]{0:T(128)S(1)} %reshape_squeeze.9.cols_ref, s32[4]{0:T(128)S(1)} %bitcast.21, s32[1]{0:T(128)} %bitcast.1.lag_ref, bf16[4,64,4096]{2,1,0:T(8,128)(2,1)S(1)} %bitcast.18, bf16[4,12,256,256]{3,2,1,0:T(8,128)(2,1)} %bitcast.23, ...), custom_call_target="tpu_custom_call" | custom-call | tf_op jit(solution)/shard_map/pallas_call | solution.py:121
  117.7 0.1 slice_bitcast_fusion
  117.8 0.4 collective-permute-start.1
  118.2 2.4 %collective-permute-done.1 = f32[16,64,256]{2,1,0:T(8,128)S(1)} collective-permute-done((f32[16,64,256]{2,1,0:T(8,128)S(1)}, f32[16,64,256]{2,1,0:T(8,128)S(1)}, u32[]{:S(2)}, u32[]{:S(2)}) %collective-permute-start.1) | collective-permute-done | bytes 1048608 | tf_op jit(solution)/shard_map/ppermute | solution.py:151
  120.6 0.1 fusion.part_ref
  120.7 28.7 %shard_map.107 = f32[64,256]{1,0:T(8,128)S(1)} custom-call(f32[16,64,256]{2,1,0:T(8,128)S(1)} %fusion.part_ref), custom_call_target="tpu_custom_call" | custom-call | tf_op jit(solution)/shard_map/pallas_call | solution.py:67
  149.5 1.3 divide_subtract_fusion
  (14 shorter events, 0.1 us)
Async XLA Ops:
  7.2 45.7 %all-gather.3.cloned.1.call-start = ((), (), s32[]{:S(2)}) async-start(), calls=%async_computation | async-start | bytes 2359296 | tf_op jit(solution)/shard_map/all_gather | solution.py:147
  9.1 97.4 %all-gather.5.cloned.1.call-start = ((), (), s32[]{:S(2)}) async-start(), calls=%async_computation.1 | async-start | bytes 2359296 | tf_op jit(solution)/shard_map/all_gather | solution.py:147
  52.8 1.6 %copy-start.1 = (bf16[4,1,64,4096]{3,2,0,1:T(8,128)(2,1)S(1)}, bf16[4,1,64,4096]{3,2,0,1:T(8,128)(2,1)}, u32[]{:S(2)}) copy-start(bf16[4,1,64,4096]{3,2,0,1:T(8,128)(2,1)} %all-gather.3.cloned.1.call-done) | copy-start | bytes 6291460
  54.4 0.7 copy-start.2
  64.7 41.8 %copy-start.3 = (s32[1,1,4]{2,1,0:T(1,128)S(1)}, s32[1,1,4]{2,1,0:T(1,128)}, u32[]{:S(2)}) copy-start(s32[1,1,4]{2,1,0:T(1,128)} %param.13) | copy-start | bytes 52
  64.7 7.9 %collective-permute-start = (f32[16,64,256]{2,1,0:T(8,128)S(1)}, f32[16,64,256]{2,1,0:T(8,128)S(1)}, u32[]{:S(2)}, u32[]{:S(2)}) collective-permute-start(f32[16,64,256]{2,1,0:T(8,128)S(1)} %slice_bitcast_fusion.2), channel_id=1, source_target_pairs={{0,1},{1,0},{2,3},{3,2},{4,5},{5,4},{6,7},{7,6},{8,9},{9,8},{10,11... | collective-permute-start | bytes 3145736 | tf_op jit(solution)/shard_map/ppermute | solution.py:151
  106.6 1.6 %copy-start = (bf16[4,1,64,4096]{3,2,0,1:T(8,128)(2,1)S(1)}, bf16[4,1,64,4096]{3,2,0,1:T(8,128)(2,1)}, u32[]{:S(2)}) copy-start(bf16[4,1,64,4096]{3,2,0,1:T(8,128)(2,1)} %all-gather.5.cloned.1.call-done) | copy-start | bytes 6291460
  117.8 31.7 %copy-start.4 = (f32[128,256]{1,0:T(8,128)S(1)}, f32[128,256]{1,0:T(8,128)}, u32[]{:S(2)}) copy-start(f32[128,256]{1,0:T(8,128)} %param.16) | copy-start | bytes 393220
  117.8 31.7 %copy-start.5 = (f32[128,256]{1,0:T(8,128)S(1)}, f32[128,256]{1,0:T(8,128)}, u32[]{:S(2)}) copy-start(f32[128,256]{1,0:T(8,128)} %param.15) | copy-start | bytes 393220
  117.8 31.7 %copy-start.6 = (f32[128,256]{1,0:T(8,128)S(1)}, f32[128,256]{1,0:T(8,128)}, u32[]{:S(2)}) copy-start(f32[128,256]{1,0:T(8,128)} %param.14) | copy-start | bytes 393220
  117.8 31.7 %copy-start.7 = (f32[128,256]{1,0:T(8,128)S(1)}, f32[128,256]{1,0:T(8,128)}, u32[]{:S(2)}) copy-start(f32[128,256]{1,0:T(8,128)} %param.17) | copy-start | bytes 393220
  117.8 2.7 %collective-permute-start.1 = (f32[16,64,256]{2,1,0:T(8,128)S(1)}, f32[16,64,256]{2,1,0:T(8,128)S(1)}, u32[]{:S(2)}, u32[]{:S(2)}) collective-permute-start(f32[16,64,256]{2,1,0:T(8,128)S(1)} %slice_bitcast_fusion), channel_id=1, source_target_pairs={{0,1},{1,0},{2,3},{3,2},{4,5},{5,4},{6,7},{7,6},{8,9},{9,8},{10,11... | collective-permute-start | bytes 3145736 | tf_op jit(solution)/shard_map/ppermute | solution.py:151
Sparse Core Ops, SparseCore 0:
  9.8 43.0 all-gather.2
  54.6 45.8 all-gather.4

commit v6 on v4

--- a/solution.py
+++ b/solution.py
@@ -16,63 +16,89 @@
     return jnp.sign(value) * jnp.log(magnitude + jnp.sqrt(1.0 + magnitude * magnitude))
 
 
-def scatter_kernel(n_col, part_ref, out_ref, slots, send_sem, recv_sem):
+def ring_kernel(n_z, part_ref, out_ref, recv, forward, final, cross,
+                send_sem, recv_sem, cross_sem):
     row = lax.axis_index("row")
-    me = lax.axis_index("col")
+    col = lax.axis_index("col")
     lag = lax.axis_index("lag")
-
-    def peer(t):
-        return (row, t, lag)
+    z = col // 2
+    y_hi = col % 2
+    up = lax.rem(z + 1, n_z)
+    down = lax.rem(z + n_z - 1, n_z)
+
+    def device(zz, yy):
+        return (row, zz * 2 + yy, lag)
 
     barrier = pltpu.get_barrier_semaphore()
-    for d in range(1, n_col):
-        t = lax.rem(me + d, n_col)
-        pl.semaphore_signal(barrier, inc=1, device_id=peer(t), device_id_type=MESH)
-    pl.semaphore_wait(barrier, n_col - 1)
-
-    sends = []
-    for d in range(1, n_col):
-        t = lax.rem(me + d, n_col)
-        copy = pltpu.make_async_remote_copy(
-            src_ref=part_ref.at[t],
-            dst_ref=slots.at[me],
-            send_sem=send_sem.at[t],
-            recv_sem=recv_sem.at[me],
-            device_id=peer(t),
-            device_id_type=MESH,
-        )
-        copy.start()
-        sends.append(copy)
-
-    total = part_ref[me]
-    for d in range(1, n_col):
-        s = lax.rem(me + n_col - d, n_col)
-        incoming = pltpu.make_async_remote_copy(
-            src_ref=part_ref.at[s],
-            dst_ref=slots.at[s],
-            send_sem=send_sem.at[s],
-            recv_sem=recv_sem.at[s],
-            device_id=peer(s),
-            device_id_type=MESH,
-        )
-        incoming.wait_recv()
-        total = total + slots[s]
-    out_ref[...] = total
-    for copy in sends:
-        copy.wait_send()
+    for peer in (device(up, y_hi), device(down, y_hi), device(z, 1 - y_hi)):
+        pl.semaphore_signal(barrier, inc=1, device_id=peer, device_id_type=MESH)
+    pl.semaphore_wait(barrier, 3)
+
+    steps = n_z - 1
+    copies = [[], []]
+    for step in range(steps):
+        for way in range(2):
+            if way == 0:
+                target = lax.rem(z + n_z - 1 - step, n_z)
+                dest = device(up, y_hi)
+            else:
+                target = lax.rem(z + 1 + step, n_z)
+                dest = device(down, y_hi)
+            block = target * 2 + way
+            if step == 0:
+                source = part_ref.at[block]
+            else:
+                copies[way][step - 1].wait_recv()
+                forward[way, step] = recv[way, step - 1] + part_ref[block]
+                source = forward.at[way, step]
+            copy = pltpu.make_async_remote_copy(
+                src_ref=source,
+                dst_ref=recv.at[way, step],
+                send_sem=send_sem.at[way, step],
+                recv_sem=recv_sem.at[way, step],
+                device_id=dest,
+                device_id_type=MESH,
+            )
+            copy.start()
+            copies[way].append(copy)
+
+    for way in range(2):
+        copies[way][steps - 1].wait_recv()
+        final[way] = recv[way, steps - 1] + part_ref[z * 2 + way]
+    handoff = pltpu.make_async_remote_copy(
+        src_ref=final.at[1 - y_hi],
+        dst_ref=cross,
+        send_sem=cross_sem.at[0],
+        recv_sem=cross_sem.at[1],
+        device_id=device(z, 1 - y_hi),
+        device_id_type=MESH,
+    )
+    handoff.start()
+    handoff.wait_recv()
+    out_ref[...] = final[y_hi] + cross[...]
+    handoff.wait_send()
+    for way in range(2):
+        for copy in copies[way]:
+            copy.wait_send()
 
 
 def reduce_scatter(part, n_col):
     group, sims, tile = part.shape
+    n_z = n_col // 2
+    steps = n_z - 1
     return pl.pallas_call(
-        functools.partial(scatter_kernel, n_col),
+        functools.partial(ring_kernel, n_z),
         out_shape=jax.ShapeDtypeStruct((sims, tile), jnp.float32),
         in_specs=[pl.BlockSpec(memory_space=pltpu.VMEM)],
         out_specs=pl.BlockSpec(memory_space=pltpu.VMEM),
         scratch_shapes=[
-            pltpu.VMEM((group, sims, tile), jnp.float32),
-            pltpu.SemaphoreType.DMA((group,)),
-            pltpu.SemaphoreType.DMA((group,)),
+            pltpu.VMEM((2, steps, sims, tile), jnp.float32),
+            pltpu.VMEM((2, steps, sims, tile), jnp.float32),
+            pltpu.VMEM((2, sims, tile), jnp.float32),
+            pltpu.VMEM((sims, tile), jnp.float32),
+            pltpu.SemaphoreType.DMA((2, steps)),
+            pltpu.SemaphoreType.DMA((2, steps)),
+            pltpu.SemaphoreType.DMA((2,)),
         ],
         compiler_params=pltpu.CompilerParams(
             collective_id=0, has_side_effects=True, vmem_limit_bytes=48 * 1024 * 1024

time: 148 us -> 135 us (0.912)
  the two profiles are of different devices: /device:TPU:1 before, /device:TPU:8 now
where the time goes in v6:
time: 135 us
  waiting for transfers between devices  62.3 us (46%)
  Pallas kernels  53.9 us (40%)
  between operations  14.1 us (10%)
  local copies, waits for them, and re-layouts  3 us (2%)
  other arithmetic  1.69 us (1%)
    all_gather x1, waiting for transfers between devices, local(): gathered = lax.all_gather(history, 'row', axis=3, tiled=True)  57.5 us
    pallas_call x1, Pallas kernels, reduce_scatter(): pl.pallas_call(functools.partial(ring_kernel, n_z), out_shape=jax.ShapeDt...  43.4 us
    pallas_call x1, Pallas kernels, stress_parts(): pl.pallas_call(functools.partial(parts_kernel, n_lag), out_shape=jax.Shap...  10.5 us
    ppermute x1, waiting for transfers between devices, local(): from_partner = lax.ppermute(other, 'lag', perm=[(0, 1), (1, 0)])  4.15 us
  transfers between devices with their start and end apart: 2, of which 2 were waited for; matrix products, arithmetic and copies ran while one was open for 1% of the time, Pallas kernels for 0%

profile of v6, /device:TPU:8, one launch (start us, length us, event | category | flops | bytes accessed | tf_op | source)
XLA Modules:
  0.0 135.2 jit_solution(18153194632302156967)
XLA Ops:
  7.2 0.0 all-gather.2.cloned.1.call-start
  7.2 0.7 all-gather.2.cloned.1.call-update
  7.9 0.8 reshape_squeeze.6.rows_ref
  8.7 0.8 reshape_squeeze.7.cols_ref
  9.4 57.5 %all-gather.2.cloned.1.call-done = bf16[4,1,128,4096]{3,2,0,1:T(8,128)(2,1)} async-done(((bf16[4,1,128,512]{3,2,0,1:T(8,128)(2,1)}), bf16[4,1,128,4096]{3,2,0,1:T(8,128)(2,1)}) %all-gather.2.cloned.1.call-update) | async-done | bytes 4194320 | tf_op jit(solution)/shard_map/all_gather | solution.py:167
  66.9 0.0 copy-start
  66.9 0.7 copy-done
  67.5 10.5 %shard_map.104 = f32[2,16,128,256]{3,2,1,0:T(8,128)S(1)} custom-call(s32[48]{0:T(128)S(1)} %reshape_squeeze.6.rows_ref, s32[48]{0:T(128)S(1)} %reshape_squeeze.7.cols_ref, s32[4]{0:T(128)S(1)} %bitcast.11, s32[1]{0:T(128)} %bitcast.1.lag_ref, bf16[4,128,4096]{2,1,0:T(8,128)(2,1)} %bitcast.13, bf16[4,12,256,256]{3,2,1,0:T(8,128)(2,1)} %bitcast.12), custom_call_target="tpu_custom_call" | custom-call | tf_op jit(solution)/shard_map/pallas_call | solution.py:146
  78.0 0.1 slice_bitcast_fusion
  78.2 0.1 collective-permute-start
  78.3 4.1 %collective-permute-done = f32[16,128,256]{2,1,0:T(8,128)S(1)} collective-permute-done((f32[16,128,256]{2,1,0:T(8,128)S(1)}, f32[16,128,256]{2,1,0:T(8,128)S(1)}, u32[]{:S(2)}, u32[]{:S(2)}) %collective-permute-start) | collective-permute-done | bytes 2097184 | tf_op jit(solution)/shard_map/ppermute | solution.py:172
  82.4 0.4 fusion.part_ref
  82.9 0.0 copy-start.1
  82.9 0.0 copy-start.2
  82.9 0.0 copy-start.3
  82.9 0.0 copy-start.4
  82.9 43.4 %shard_map.105 = f32[128,256]{1,0:T(8,128)S(1)} custom-call(f32[16,128,256]{2,1,0:T(8,128)S(1)} %fusion.part_ref), custom_call_target="tpu_custom_call" | custom-call | tf_op jit(solution)/shard_map/pallas_call | solution.py:89
  126.3 0.0 copy-done.1
  126.3 0.0 copy-done.2
  126.4 0.0 copy-done.3
  126.4 0.0 copy-done.4
  126.4 1.3 divide_subtract_fusion
  127.7 0.7 copy.13
Async XLA Ops:
  7.2 59.7 %all-gather.2.cloned.1.call-start = ((), (), s32[]{:S(2)}) async-start(), calls=%async_computation | async-start | bytes 4718592 | tf_op jit(solution)/shard_map/all_gather | solution.py:167
  66.9 0.7 copy-start
  78.2 4.2 %collective-permute-start = (f32[16,128,256]{2,1,0:T(8,128)S(1)}, f32[16,128,256]{2,1,0:T(8,128)S(1)}, u32[]{:S(2)}, u32[]{:S(2)}) collective-permute-start(f32[16,128,256]{2,1,0:T(8,128)S(1)} %slice_bitcast_fusion), channel_id=1, source_target_pairs={{0,1},{1,0},{2,3},{3,2},{4,5},{5,4},{6,7},{7,6},{8,9},{9,8},{10,11... | collective-permute-start | bytes 6291464 | tf_op jit(solution)/shard_map/ppermute | solution.py:172
  82.9 43.5 %copy-start.1 = (f32[128,256]{1,0:T(8,128)S(1)}, f32[128,256]{1,0:T(8,128)}, u32[]{:S(2)}) copy-start(f32[128,256]{1,0:T(8,128)} %param.16) | copy-start | bytes 393220
  82.9 43.5 %copy-start.2 = (f32[128,256]{1,0:T(8,128)S(1)}, f32[128,256]{1,0:T(8,128)}, u32[]{:S(2)}) copy-start(f32[128,256]{1,0:T(8,128)} %param.15) | copy-start | bytes 393220
  82.9 43.5 %copy-start.3 = (f32[128,256]{1,0:T(8,128)S(1)}, f32[128,256]{1,0:T(8,128)}, u32[]{:S(2)}) copy-start(f32[128,256]{1,0:T(8,128)} %param.14) | copy-start | bytes 393220
  82.9 43.5 %copy-start.4 = (f32[128,256]{1,0:T(8,128)S(1)}, f32[128,256]{1,0:T(8,128)}, u32[]{:S(2)}) copy-start(f32[128,256]{1,0:T(8,128)} %param.17) | copy-start | bytes 393220
Sparse Core Ops, SparseCore 0:
  9.8 57.0 all-gather.1

commit v7 on v6

--- a/solution.py
+++ b/solution.py
@@ -120,8 +120,7 @@
         def _():
             col = cols_ref[lag * slots + k]
             row = rows_ref[lag * slots + k]
-            start = pl.multiple_of(col * side, side)
-            history = hist_ref[0, :, pl.ds(start, side)]
+            history = hist_ref[0, col]
             contrib = lax.dot_general(
                 history, tiles_ref[0, k], (((1,), (1,)), ((), ())),
                 preferred_element_type=jnp.float32,
@@ -131,14 +130,14 @@
 
 
 def stress_parts(history, tiles, rows, cols, count, n_col, n_lag):
-    lags, sims, sources = history.shape
+    lags, n_blocks, sims, _ = history.shape
     _, slots, side, _ = tiles.shape
     lag = lax.axis_index("lag").astype(jnp.int32).reshape(1)
     grid_spec = pltpu.PrefetchScalarGridSpec(
         num_scalar_prefetch=4,
         grid=(lags,),
         in_specs=[
-            pl.BlockSpec((1, sims, sources), lambda l, *_: (l, 0, 0)),
+            pl.BlockSpec((1, n_blocks, sims, side), lambda l, *_: (l, 0, 0, 0)),
             pl.BlockSpec((1, slots, side, side), lambda l, *_: (l, 0, 0, 0)),
         ],
         out_specs=pl.BlockSpec((2, n_col, sims, side), lambda l, *_: (0, 0, 0, 0)),
@@ -164,9 +163,12 @@
     direct_effect,
     state_var,
 ):
-    gathered = lax.all_gather(history, "row", axis=3, tiled=True)
     tile_side = kernel_tiles.shape[4]
-    parts = stress_parts(gathered[:, 0], kernel_tiles[0, 0], tile_rows[0, 0],
+    lag_local, _, sims_count, held = history.shape
+    blocks = history.reshape(lag_local, sims_count, held // tile_side, tile_side)
+    blocks = jnp.transpose(blocks, (0, 2, 1, 3))
+    gathered = lax.all_gather(blocks, "row", axis=1, tiled=True)
+    parts = stress_parts(gathered, kernel_tiles[0, 0], tile_rows[0, 0],
                          tile_cols[0, 0], tile_count[0, 0], n_col, n_lag)
     own, other = parts[0], parts[1]
     from_partner = lax.ppermute(other, "lag", perm=[(0, 1), (1, 0)])

time: 135 us -> 135 us (level)
  the two profiles are of different devices: /device:TPU:8 before, /device:TPU:2 now
where the time goes in v7:
time: 135 us
  waiting for transfers between devices  59.8 us (44%)
  Pallas kernels  54.8 us (41%)
  between operations  14.2 us (11%)
  local copies, waits for them, and re-layouts  3.34 us (2%)
  other arithmetic  1.69 us (1%)
    all_gather x1, waiting for transfers between devices, local(): gathered = lax.all_gather(blocks, 'row', axis=1, tiled=True)  56 us
    pallas_call x1, Pallas kernels, reduce_scatter(): pl.pallas_call(functools.partial(ring_kernel, n_z), out_shape=jax.ShapeDt...  46 us
    pallas_call x1, Pallas kernels, stress_parts(): pl.pallas_call(functools.partial(parts_kernel, n_lag), out_shape=jax.Shap...  8.88 us
    ppermute x1, waiting for transfers between devices, local(): from_partner = lax.ppermute(other, 'lag', perm=[(0, 1), (1, 0)])  3.79 us
  transfers between devices with their start and end apart: 2, of which 2 were waited for; matrix products, arithmetic and copies ran while one was open for 0% of the time, Pallas kernels for 0%

profile of v7, /device:TPU:2, one launch (start us, length us, event | category | flops | bytes accessed | tf_op | source)
XLA Modules:
  0.0 134.7 jit_solution(7496528705163551061)
XLA Ops:
  7.2 0.0 copy-start.1
  7.2 0.0 copy-start.2
  7.2 0.0 copy-start
  7.2 0.0 all-gather.2.cloned.1.call-start
  7.2 1.3 copy.11
  8.6 1.0 copy.12
  9.6 0.0 all-gather.2.cloned.1.call-update
  9.6 0.0 copy-done.1
  9.6 0.1 reshape_squeeze.6.rows_ref
  9.7 0.0 copy-done.2
  9.7 0.1 reshape_squeeze.7.cols_ref
  9.8 56.0 %all-gather.2.cloned.1.call-done.hist_ref = bf16[4,16,128,256]{3,2,1,0:T(8,128)(2,1)} async-done(((bf16[4,2,128,256]{3,2,1,0:T(8,128)(2,1)}), bf16[4,16,128,256]{3,2,1,0:T(8,128)(2,1)}) %all-gather.2.cloned.1.call-update) | async-done | bytes 4194320 | tf_op jit(solution)/shard_map/all_gather | solution.py:170
  65.8 8.9 %shard_map.104 = f32[2,16,128,256]{3,2,1,0:T(8,128)S(1)} custom-call(s32[48]{0:T(128)S(1)} %reshape_squeeze.6.rows_ref, s32[48]{0:T(128)S(1)} %reshape_squeeze.7.cols_ref, s32[4]{0:T(128)S(1)} %bitcast.11, s32[1]{0:T(128)} %bitcast.1.lag_ref, bf16[4,16,128,256]{3,2,1,0:T(8,128)(2,1)} %all-gather.2.cloned.1.call-done.hist_ref, bf16[4,12,256,256]{3,2,1,0:T(8,128)(2,1)} %bitcast.12), custom_call_target="tpu_custom_call" | custom-call | tf_op jit(solution)/shard_map/pallas_call | solution.py:145
  74.6 0.1 slice_bitcast_fusion
  74.8 0.9 collective-permute-start
  75.7 3.8 %collective-permute-done = f32[16,128,256]{2,1,0:T(8,128)S(1)} collective-permute-done((f32[16,128,256]{2,1,0:T(8,128)S(1)}, f32[16,128,256]{2,1,0:T(8,128)S(1)}, u32[]{:S(2)}, u32[]{:S(2)}) %collective-permute-start) | collective-permute-done | bytes 2097184 | tf_op jit(solution)/shard_map/ppermute | solution.py:174
  79.5 0.4 fusion.part_ref
  79.9 0.0 copy-start.3
  79.9 0.0 copy-start.4
  79.9 0.0 copy-start.5
  79.9 0.0 copy-start.6
  79.9 46.0 %shard_map.105 = f32[128,256]{1,0:T(8,128)S(1)} custom-call(f32[16,128,256]{2,1,0:T(8,128)S(1)} %fusion.part_ref), custom_call_target="tpu_custom_call" | custom-call | tf_op jit(solution)/shard_map/pallas_call | solution.py:89
  125.9 1.3 divide_subtract_fusion
  127.2 0.7 copy.14
  (5 shorter events, 0.0 us)
Async XLA Ops:
  7.2 2.5 %copy-start.1 = (s32[1,1,4,12]{3,2,1,0:T(4,128)S(1)}, s32[1,1,4,12]{3,2,1,0:T(4,128)}, u32[]{:S(2)}) copy-start(s32[1,1,4,12]{3,2,1,0:T(4,128)} %param.11) | copy-start | bytes 580
  7.2 2.5 %copy-start.2 = (s32[1,1,4,12]{3,2,1,0:T(4,128)S(1)}, s32[1,1,4,12]{3,2,1,0:T(4,128)}, u32[]{:S(2)}) copy-start(s32[1,1,4,12]{3,2,1,0:T(4,128)} %param.12) | copy-start | bytes 580
  7.2 58.6 %copy-start = (s32[1,1,4]{2,1,0:T(1,128)S(1)}, s32[1,1,4]{2,1,0:T(1,128)}, u32[]{:S(2)}) copy-start(s32[1,1,4]{2,1,0:T(1,128)} %param.13) | copy-start | bytes 52
  7.2 58.6 %all-gather.2.cloned.1.call-start = ((), (), s32[]{:S(2)}) async-start(), calls=%async_computation | async-start | bytes 4718592 | tf_op jit(solution)/shard_map/all_gather | solution.py:170
  74.8 4.7 %collective-permute-start = (f32[16,128,256]{2,1,0:T(8,128)S(1)}, f32[16,128,256]{2,1,0:T(8,128)S(1)}, u32[]{:S(2)}, u32[]{:S(2)}) collective-permute-start(f32[16,128,256]{2,1,0:T(8,128)S(1)} %slice_bitcast_fusion), channel_id=1, source_target_pairs={{0,1},{1,0},{2,3},{3,2},{4,5},{5,4},{6,7},{7,6},{8,9},{9,8},{10,11... | collective-permute-start | bytes 6291464 | tf_op jit(solution)/shard_map/ppermute | solution.py:174
  79.9 46.0 %copy-start.3 = (f32[128,256]{1,0:T(8,128)S(1)}, f32[128,256]{1,0:T(8,128)}, u32[]{:S(2)}) copy-start(f32[128,256]{1,0:T(8,128)} %param.16) | copy-start | bytes 393220
  79.9 46.0 %copy-start.4 = (f32[128,256]{1,0:T(8,128)S(1)}, f32[128,256]{1,0:T(8,128)}, u32[]{:S(2)}) copy-start(f32[128,256]{1,0:T(8,128)} %param.15) | copy-start | bytes 393220
  79.9 46.0 %copy-start.5 = (f32[128,256]{1,0:T(8,128)S(1)}, f32[128,256]{1,0:T(8,128)}, u32[]{:S(2)}) copy-start(f32[128,256]{1,0:T(8,128)} %param.14) | copy-start | bytes 393220
  79.9 46.0 %copy-start.6 = (f32[128,256]{1,0:T(8,128)S(1)}, f32[128,256]{1,0:T(8,128)}, u32[]{:S(2)}) copy-start(f32[128,256]{1,0:T(8,128)} %param.17) | copy-start | bytes 393220
Sparse Core Ops, SparseCore 0:
  9.8 55.8 all-gather.1

commit v8 on v6

--- a/solution.py
+++ b/solution.py
@@ -16,7 +16,7 @@
     return jnp.sign(value) * jnp.log(magnitude + jnp.sqrt(1.0 + magnitude * magnitude))
 
 
-def ring_kernel(n_z, part_ref, out_ref, recv, forward, final, cross,
+def ring_kernel(n_z, n_pieces, part_ref, out_ref, recv, forward, final, cross,
                 send_sem, recv_sem, cross_sem):
     row = lax.axis_index("row")
     col = lax.axis_index("col")
@@ -25,6 +25,7 @@
     y_hi = col % 2
     up = lax.rem(z + 1, n_z)
     down = lax.rem(z + n_z - 1, n_z)
+    rows = part_ref.shape[1] // n_pieces
 
     def device(zz, yy):
         return (row, zz * 2 + yy, lag)
@@ -35,70 +36,80 @@
     pl.semaphore_wait(barrier, 3)
 
     steps = n_z - 1
-    copies = [[], []]
+    copies = {}
     for step in range(steps):
+        for piece in range(n_pieces):
+            span = pl.ds(piece * rows, rows)
+            for way in range(2):
+                if way == 0:
+                    target = lax.rem(z + n_z - 1 - step, n_z)
+                    dest = device(up, y_hi)
+                else:
+                    target = lax.rem(z + 1 + step, n_z)
+                    dest = device(down, y_hi)
+                block = target * 2 + way
+                if step == 0:
+                    source = part_ref.at[block, span]
+                else:
+                    copies[way, step - 1, piece].wait_recv()
+                    forward[way, step, piece] = (
+                        recv[way, step - 1, piece] + part_ref[block, span]
+                    )
+                    source = forward.at[way, step, piece]
+                copy = pltpu.make_async_remote_copy(
+                    src_ref=source,
+                    dst_ref=recv.at[way, step, piece],
+                    send_sem=send_sem.at[way, step, piece],
+                    recv_sem=recv_sem.at[way, step, piece],
+                    device_id=dest,
+                    device_id_type=MESH,
+                )
+                copy.start()
+                copies[way, step, piece] = copy
+
+    handoffs = []
+    for piece in range(n_pieces):
+        span = pl.ds(piece * rows, rows)
         for way in range(2):
-            if way == 0:
-                target = lax.rem(z + n_z - 1 - step, n_z)
-                dest = device(up, y_hi)
-            else:
-                target = lax.rem(z + 1 + step, n_z)
-                dest = device(down, y_hi)
-            block = target * 2 + way
-            if step == 0:
-                source = part_ref.at[block]
-            else:
-                copies[way][step - 1].wait_recv()
-                forward[way, step] = recv[way, step - 1] + part_ref[block]
-                source = forward.at[way, step]
-            copy = pltpu.make_async_remote_copy(
-                src_ref=source,
-                dst_ref=recv.at[way, step],
-                send_sem=send_sem.at[way, step],
-                recv_sem=recv_sem.at[way, step],
-                device_id=dest,
-                device_id_type=MESH,
-            )
-            copy.start()
-            copies[way].append(copy)
-
-    for way in range(2):
-        copies[way][steps - 1].wait_recv()
-        final[way] = recv[way, steps - 1] + part_ref[z * 2 + way]
-    handoff = pltpu.make_async_remote_copy(
-        src_ref=final.at[1 - y_hi],
-        dst_ref=cross,
-        send_sem=cross_sem.at[0],
-        recv_sem=cross_sem.at[1],
-        device_id=device(z, 1 - y_hi),
-        device_id_type=MESH,
-    )
-    handoff.start()
-    handoff.wait_recv()
-    out_ref[...] = final[y_hi] + cross[...]
-    handoff.wait_send()
-    for way in range(2):
-        for copy in copies[way]:
-            copy.wait_send()
-
-
-def reduce_scatter(part, n_col):
+            copies[way, steps - 1, piece].wait_recv()
+            final[way, piece] = recv[way, steps - 1, piece] + part_ref[z * 2 + way, span]
+        handoff = pltpu.make_async_remote_copy(
+            src_ref=final.at[1 - y_hi, piece],
+            dst_ref=cross.at[piece],
+            send_sem=cross_sem.at[0, piece],
+            recv_sem=cross_sem.at[1, piece],
+            device_id=device(z, 1 - y_hi),
+            device_id_type=MESH,
+        )
+        handoff.start()
+        handoffs.append(handoff)
+    for piece in range(n_pieces):
+        handoffs[piece].wait_recv()
+        out_ref[pl.ds(piece * rows, rows), :] = final[y_hi, piece] + cross[piece]
+    for handoff in handoffs:
+        handoff.wait_send()
+    for copy in copies.values():
+        copy.wait_send()
+
+
+def reduce_scatter(part, n_col, n_pieces=2):
     group, sims, tile = part.shape
     n_z = n_col // 2
     steps = n_z - 1
+    rows = sims // n_pieces
     return pl.pallas_call(
-        functools.partial(ring_kernel, n_z),
+        functools.partial(ring_kernel, n_z, n_pieces),
         out_shape=jax.ShapeDtypeStruct((sims, tile), jnp.float32),
         in_specs=[pl.BlockSpec(memory_space=pltpu.VMEM)],
         out_specs=pl.BlockSpec(memory_space=pltpu.VMEM),
         scratch_shapes=[
-            pltpu.VMEM((2, steps, sims, tile), jnp.float32),
-            pltpu.VMEM((2, steps, sims, tile), jnp.float32),
-            pltpu.VMEM((2, sims, tile), jnp.float32),
-            pltpu.VMEM((sims, tile), jnp.float32),
-            pltpu.SemaphoreType.DMA((2, steps)),
-            pltpu.SemaphoreType.DMA((2, steps)),
-            pltpu.SemaphoreType.DMA((2,)),
+            pltpu.VMEM((2, steps, n_pieces, rows, tile), jnp.float32),
+            pltpu.VMEM((2, steps, n_pieces, rows, tile), jnp.float32),
+            pltpu.VMEM((2, n_pieces, rows, tile), jnp.float32),
+            pltpu.VMEM((n_pieces, rows, tile), jnp.float32),
+            pltpu.SemaphoreType.DMA((2, steps, n_pieces)),
+            pltpu.SemaphoreType.DMA((2, steps, n_pieces)),
+            pltpu.SemaphoreType.DMA((2, n_pieces)),
         ],
         compiler_params=pltpu.CompilerParams(
             collective_id=0, has_side_effects=True, vmem_limit_bytes=48 * 1024 * 1024

time: 135 us -> 129 us (0.956)
  the two profiles are of different devices: /device:TPU:8 before, /device:TPU:16 now
where the time goes in v8:
time: 129 us
  waiting for transfers between devices  62.8 us (49%)
  Pallas kernels  46.9 us (36%)
  between operations  14.1 us (11%)
  local copies, waits for them, and re-layouts  3 us (2%)
  other arithmetic  1.69 us (1%)
    all_gather x1, waiting for transfers between devices, local(): gathered = lax.all_gather(history, 'row', axis=3, tiled=True)  58 us
    pallas_call x1, Pallas kernels, reduce_scatter(): pl.pallas_call(functools.partial(ring_kernel, n_z, n_pieces), out_shape=j...  35.3 us
    pallas_call x1, Pallas kernels, stress_parts(): pl.pallas_call(functools.partial(parts_kernel, n_lag), out_shape=jax.Shap...  11.6 us
    ppermute x1, waiting for transfers between devices, local(): from_partner = lax.ppermute(other, 'lag', perm=[(0, 1), (1, 0)])  4.15 us
  transfers between devices with their start and end apart: 2, of which 2 were waited for; matrix products, arithmetic and copies ran while one was open for 1% of the time, Pallas kernels for 0%

profile of v8, /device:TPU:16, one launch (start us, length us, event | category | flops | bytes accessed | tf_op | source)
XLA Modules:
  0.0 128.7 jit_solution(8681421774437696552)
XLA Ops:
  7.2 0.0 all-gather.2.cloned.1.call-start
  7.2 0.7 all-gather.2.cloned.1.call-update
  7.9 0.8 reshape_squeeze.6.rows_ref
  8.7 0.8 reshape_squeeze.7.cols_ref
  9.4 58.0 %all-gather.2.cloned.1.call-done = bf16[4,1,128,4096]{3,2,0,1:T(8,128)(2,1)} async-done(((bf16[4,1,128,512]{3,2,0,1:T(8,128)(2,1)}), bf16[4,1,128,4096]{3,2,0,1:T(8,128)(2,1)}) %all-gather.2.cloned.1.call-update) | async-done | bytes 4194320 | tf_op jit(solution)/shard_map/all_gather | solution.py:178
  67.4 0.0 copy-start
  67.4 0.7 copy-done
  68.1 11.6 %shard_map.104 = f32[2,16,128,256]{3,2,1,0:T(8,128)S(1)} custom-call(s32[48]{0:T(128)S(1)} %reshape_squeeze.6.rows_ref, s32[48]{0:T(128)S(1)} %reshape_squeeze.7.cols_ref, s32[4]{0:T(128)S(1)} %bitcast.11, s32[1]{0:T(128)} %bitcast.1.lag_ref, bf16[4,128,4096]{2,1,0:T(8,128)(2,1)} %bitcast.13, bf16[4,12,256,256]{3,2,1,0:T(8,128)(2,1)} %bitcast.12), custom_call_target="tpu_custom_call" | custom-call | tf_op jit(solution)/shard_map/pallas_call | solution.py:157
  79.7 0.1 slice_bitcast_fusion
  79.8 0.1 collective-permute-start
  79.9 4.1 %collective-permute-done = f32[16,128,256]{2,1,0:T(8,128)S(1)} collective-permute-done((f32[16,128,256]{2,1,0:T(8,128)S(1)}, f32[16,128,256]{2,1,0:T(8,128)S(1)}, u32[]{:S(2)}, u32[]{:S(2)}) %collective-permute-start) | collective-permute-done | bytes 2097184 | tf_op jit(solution)/shard_map/ppermute | solution.py:183
  84.1 0.4 fusion.part_ref
  84.5 0.0 copy-start.1
  84.5 0.0 copy-start.2
  84.5 0.0 copy-start.3
  84.5 0.0 copy-start.4
  84.6 35.3 %shard_map.105 = f32[128,256]{1,0:T(8,128)S(1)} custom-call(f32[16,128,256]{2,1,0:T(8,128)S(1)} %fusion.part_ref), custom_call_target="tpu_custom_call" | custom-call | tf_op jit(solution)/shard_map/pallas_call | solution.py:100
  119.8 0.0 copy-done.1
  119.8 0.0 copy-done.2
  119.9 0.0 copy-done.3
  119.9 0.0 copy-done.4
  119.9 1.3 divide_subtract_fusion
  121.2 0.7 copy.13
Async XLA Ops:
  7.2 60.3 %all-gather.2.cloned.1.call-start = ((), (), s32[]{:S(2)}) async-start(), calls=%async_computation | async-start | bytes 4718592 | tf_op jit(solution)/shard_map/all_gather | solution.py:178
  67.4 0.7 copy-start
  79.8 4.2 %collective-permute-start = (f32[16,128,256]{2,1,0:T(8,128)S(1)}, f32[16,128,256]{2,1,0:T(8,128)S(1)}, u32[]{:S(2)}, u32[]{:S(2)}) collective-permute-start(f32[16,128,256]{2,1,0:T(8,128)S(1)} %slice_bitcast_fusion), channel_id=1, source_target_pairs={{0,1},{1,0},{2,3},{3,2},{4,5},{5,4},{6,7},{7,6},{8,9},{9,8},{10,11... | collective-permute-start | bytes 6291464 | tf_op jit(solution)/shard_map/ppermute | solution.py:183
  84.5 35.3 %copy-start.1 = (f32[128,256]{1,0:T(8,128)S(1)}, f32[128,256]{1,0:T(8,128)}, u32[]{:S(2)}) copy-start(f32[128,256]{1,0:T(8,128)} %param.16) | copy-start | bytes 393220
  84.5 35.3 %copy-start.2 = (f32[128,256]{1,0:T(8,128)S(1)}, f32[128,256]{1,0:T(8,128)}, u32[]{:S(2)}) copy-start(f32[128,256]{1,0:T(8,128)} %param.15) | copy-start | bytes 393220
  84.5 35.3 %copy-start.3 = (f32[128,256]{1,0:T(8,128)S(1)}, f32[128,256]{1,0:T(8,128)}, u32[]{:S(2)}) copy-start(f32[128,256]{1,0:T(8,128)} %param.14) | copy-start | bytes 393220
  84.5 35.3 %copy-start.4 = (f32[128,256]{1,0:T(8,128)S(1)}, f32[128,256]{1,0:T(8,128)}, u32[]{:S(2)}) copy-start(f32[128,256]{1,0:T(8,128)} %param.17) | copy-start | bytes 393220
Sparse Core Ops, SparseCore 0:
  9.8 57.6 all-gather.1

commit v9 on v8

--- a/solution.py
+++ b/solution.py
@@ -92,7 +92,7 @@
         copy.wait_send()
 
 
-def reduce_scatter(part, n_col, n_pieces=2):
+def reduce_scatter(part, n_col, n_pieces=4):
     group, sims, tile = part.shape
     n_z = n_col // 2
     steps = n_z - 1

time: 129 us -> 128 us (level)
  the two profiles are of different devices: /device:TPU:16 before, /device:TPU:32 now
where the time goes in v9:
time: 128 us
  waiting for transfers between devices  63 us (49%)
  Pallas kernels  45.8 us (36%)
  between operations  14.1 us (11%)
  local copies, waits for them, and re-layouts  3 us (2%)
  other arithmetic  1.69 us (1%)
    all_gather x1, waiting for transfers between devices, local(): gathered = lax.all_gather(history, 'row', axis=3, tiled=True)  58.1 us
    pallas_call x1, Pallas kernels, reduce_scatter(): pl.pallas_call(functools.partial(ring_kernel, n_z, n_pieces), out_shape=j...  35.2 us
    pallas_call x1, Pallas kernels, stress_parts(): pl.pallas_call(functools.partial(parts_kernel, n_lag), out_shape=jax.Shap...  10.6 us
    ppermute x1, waiting for transfers between devices, local(): from_partner = lax.ppermute(other, 'lag', perm=[(0, 1), (1, 0)])  4.15 us
  transfers between devices with their start and end apart: 2, of which 2 were waited for; matrix products, arithmetic and copies ran while one was open for 1% of the time, Pallas kernels for 0%

profile of v9, /device:TPU:32, one launch (start us, length us, event | category | flops | bytes accessed | tf_op | source)
XLA Modules:
  0.0 127.7 jit_solution(5670619382252405267)
XLA Ops:
  7.2 0.0 all-gather.2.cloned.1.call-start
  7.2 0.7 all-gather.2.cloned.1.call-update
  7.9 0.8 reshape_squeeze.6.rows_ref
  8.7 0.8 reshape_squeeze.7.cols_ref
  9.4 58.1 %all-gather.2.cloned.1.call-done = bf16[4,1,128,4096]{3,2,0,1:T(8,128)(2,1)} async-done(((bf16[4,1,128,512]{3,2,0,1:T(8,128)(2,1)}), bf16[4,1,128,4096]{3,2,0,1:T(8,128)(2,1)}) %all-gather.2.cloned.1.call-update) | async-done | bytes 4194320 | tf_op jit(solution)/shard_map/all_gather | solution.py:178
  67.6 0.0 copy-start
  67.6 0.7 copy-done
  68.2 10.6 %shard_map.104 = f32[2,16,128,256]{3,2,1,0:T(8,128)S(1)} custom-call(s32[48]{0:T(128)S(1)} %reshape_squeeze.6.rows_ref, s32[48]{0:T(128)S(1)} %reshape_squeeze.7.cols_ref, s32[4]{0:T(128)S(1)} %bitcast.11, s32[1]{0:T(128)} %bitcast.1.lag_ref, bf16[4,128,4096]{2,1,0:T(8,128)(2,1)} %bitcast.13, bf16[4,12,256,256]{3,2,1,0:T(8,128)(2,1)} %bitcast.12), custom_call_target="tpu_custom_call" | custom-call | tf_op jit(solution)/shard_map/pallas_call | solution.py:157
  78.8 0.1 slice_bitcast_fusion
  79.0 0.1 collective-permute-start
  79.1 4.1 %collective-permute-done = f32[16,128,256]{2,1,0:T(8,128)S(1)} collective-permute-done((f32[16,128,256]{2,1,0:T(8,128)S(1)}, f32[16,128,256]{2,1,0:T(8,128)S(1)}, u32[]{:S(2)}, u32[]{:S(2)}) %collective-permute-start) | collective-permute-done | bytes 2097184 | tf_op jit(solution)/shard_map/ppermute | solution.py:183
  83.2 0.4 fusion.part_ref
  83.7 0.0 copy-start.1
  83.7 0.0 copy-start.2
  83.7 0.0 copy-start.3
  83.7 0.0 copy-start.4
  83.7 35.2 %shard_map.105 = f32[128,256]{1,0:T(8,128)S(1)} custom-call(f32[16,128,256]{2,1,0:T(8,128)S(1)} %fusion.part_ref), custom_call_target="tpu_custom_call" | custom-call | tf_op jit(solution)/shard_map/pallas_call | solution.py:100
  118.9 0.0 copy-done.1
  118.9 0.0 copy-done.2
  118.9 0.0 copy-done.3
  118.9 0.0 copy-done.4
  118.9 1.3 divide_subtract_fusion
  120.2 0.7 copy.13
Async XLA Ops:
  7.2 60.4 %all-gather.2.cloned.1.call-start = ((), (), s32[]{:S(2)}) async-start(), calls=%async_computation | async-start | bytes 4718592 | tf_op jit(solution)/shard_map/all_gather | solution.py:178
  67.6 0.7 copy-start
  79.0 4.2 %collective-permute-start = (f32[16,128,256]{2,1,0:T(8,128)S(1)}, f32[16,128,256]{2,1,0:T(8,128)S(1)}, u32[]{:S(2)}, u32[]{:S(2)}) collective-permute-start(f32[16,128,256]{2,1,0:T(8,128)S(1)} %slice_bitcast_fusion), channel_id=1, source_target_pairs={{0,1},{1,0},{2,3},{3,2},{4,5},{5,4},{6,7},{7,6},{8,9},{9,8},{10,11... | collective-permute-start | bytes 6291464 | tf_op jit(solution)/shard_map/ppermute | solution.py:183
  83.7 35.2 %copy-start.1 = (f32[128,256]{1,0:T(8,128)S(1)}, f32[128,256]{1,0:T(8,128)}, u32[]{:S(2)}) copy-start(f32[128,256]{1,0:T(8,128)} %param.16) | copy-start | bytes 393220
  83.7 35.2 %copy-start.2 = (f32[128,256]{1,0:T(8,128)S(1)}, f32[128,256]{1,0:T(8,128)}, u32[]{:S(2)}) copy-start(f32[128,256]{1,0:T(8,128)} %param.15) | copy-start | bytes 393220
  83.7 35.2 %copy-start.3 = (f32[128,256]{1,0:T(8,128)S(1)}, f32[128,256]{1,0:T(8,128)}, u32[]{:S(2)}) copy-start(f32[128,256]{1,0:T(8,128)} %param.14) | copy-start | bytes 393220
  83.7 35.2 %copy-start.4 = (f32[128,256]{1,0:T(8,128)S(1)}, f32[128,256]{1,0:T(8,128)}, u32[]{:S(2)}) copy-start(f32[128,256]{1,0:T(8,128)} %param.17) | copy-start | bytes 393220
Sparse Core Ops, SparseCore 0:
  9.8 57.7 all-gather.1

commit v10 on v9

--- a/solution.py
+++ b/solution.py
@@ -117,10 +117,71 @@
     )(part)
 
 
+def gather_kernel(n_row, piece_ref, out_ref, local_sem, send_sem, recv_sem):
+    me = lax.axis_index("row")
+    col = lax.axis_index("col")
+    lag = lax.axis_index("lag")
+
+    def peer(t):
+        return (t, col, lag)
+
+    barrier = pltpu.get_barrier_semaphore()
+    for d in range(1, n_row):
+        t = lax.rem(me + d, n_row)
+        pl.semaphore_signal(barrier, inc=1, device_id=peer(t), device_id_type=MESH)
+    pl.semaphore_wait(barrier, n_row - 1)
+
+    own = pltpu.make_async_copy(piece_ref, out_ref.at[me], local_sem)
+    own.start()
+    sends = []
+    for d in range(1, n_row):
+        t = lax.rem(me + d, n_row)
+        copy = pltpu.make_async_remote_copy(
+            src_ref=piece_ref,
+            dst_ref=out_ref.at[me],
+            send_sem=send_sem.at[t],
+            recv_sem=recv_sem.at[me],
+            device_id=peer(t),
+            device_id_type=MESH,
+        )
+        copy.start()
+        sends.append(copy)
+    for d in range(1, n_row):
+        s = lax.rem(me + n_row - d, n_row)
+        incoming = pltpu.make_async_remote_copy(
+            src_ref=piece_ref,
+            dst_ref=out_ref.at[s],
+            send_sem=send_sem.at[s],
+            recv_sem=recv_sem.at[s],
+            device_id=peer(s),
+            device_id_type=MESH,
+        )
+        incoming.wait_recv()
+    own.wait()
+    for copy in sends:
+        copy.wait_send()
+
+
+def all_gather_rows(piece, n_row):
+    return pl.pallas_call(
+        functools.partial(gather_kernel, n_row),
+        out_shape=jax.ShapeDtypeStruct((n_row,) + piece.shape, piece.dtype),
+        in_specs=[pl.BlockSpec(memory_space=pltpu.VMEM)],
+        out_specs=pl.BlockSpec(memory_space=pl.ANY),
+        scratch_shapes=[
+            pltpu.SemaphoreType.DMA(()),
+            pltpu.SemaphoreType.DMA((n_row,)),
+            pltpu.SemaphoreType.DMA((n_row,)),
+        ],
+        compiler_params=pltpu.CompilerParams(collective_id=1, has_side_effects=True),
+    )(piece)
+
+
 def parts_kernel(n_lag, rows_ref, cols_ref, count_ref, lag_ref, hist_ref, tiles_ref, out_ref):
     lag = pl.program_id(0)
     slots = tiles_ref.shape[1]
     side = tiles_ref.shape[2]
+    halves = hist_ref.shape[3] // side
 
     @pl.when(lag == 0)
     def _():
@@ -131,8 +192,8 @@
         def _():
             col = cols_ref[lag * slots + k]
             row = rows_ref[lag * slots + k]
-            start = pl.multiple_of(col * side, side)
-            history = hist_ref[0, :, pl.ds(start, side)]
+            start = pl.multiple_of((col % halves) * side, side)
+            history = hist_ref[col // halves, 0, :, pl.ds(start, side)]
             contrib = lax.dot_general(
                 history, tiles_ref[0, k], (((1,), (1,)), ((), ())),
                 preferred_element_type=jnp.float32,
@@ -142,14 +203,14 @@
 
 
 def stress_parts(history, tiles, rows, cols, count, n_col, n_lag):
-    lags, sims, sources = history.shape
+    n_row, lags, sims, held = history.shape
     _, slots, side, _ = tiles.shape
     lag = lax.axis_index("lag").astype(jnp.int32).reshape(1)
     grid_spec = pltpu.PrefetchScalarGridSpec(
         num_scalar_prefetch=4,
         grid=(lags,),
         in_specs=[
-            pl.BlockSpec((1, sims, sources), lambda l, *_: (l, 0, 0)),
+            pl.BlockSpec((n_row, 1, sims, held), lambda l, *_: (0, l, 0, 0)),
             pl.BlockSpec((1, slots, side, side), lambda l, *_: (l, 0, 0, 0)),
         ],
         out_specs=pl.BlockSpec((2, n_col, sims, side), lambda l, *_: (0, 0, 0, 0)),
@@ -163,6 +224,7 @@
 
 
 def local(
+    n_row,
     n_col,
     n_lag,
     history,
@@ -175,9 +237,9 @@
     direct_effect,
     state_var,
 ):
-    gathered = lax.all_gather(history, "row", axis=3, tiled=True)
+    gathered = all_gather_rows(history[:, 0], n_row)
     tile_side = kernel_tiles.shape[4]
-    parts = stress_parts(gathered[:, 0], kernel_tiles[0, 0], tile_rows[0, 0],
+    parts = stress_parts(gathered, kernel_tiles[0, 0], tile_rows[0, 0],
                          tile_cols[0, 0], tile_count[0, 0], n_col, n_lag)
     own, other = parts[0], parts[1]
     from_partner = lax.ppermute(other, "lag", perm=[(0, 1), (1, 0)])
@@ -195,7 +257,7 @@
 
 def solution(mesh):
     return jax.shard_map(
-        functools.partial(local, mesh.shape["col"], mesh.shape["lag"]),
+        functools.partial(local, mesh.shape["row"], mesh.shape["col"], mesh.shape["lag"]),
         mesh=mesh,
         in_specs=(
             P("lag", "col", None, "row"),

time: 128 us -> 126 us (0.984)
  the two profiles are of different devices: /device:TPU:32 before, /device:TPU:16 now
where the time goes in v10:
time: 126 us
  Pallas kernels  117 us (93%)
  waiting for transfers between devices  4.15 us (3%)
  local copies, waits for them, and re-layouts  2.35 us (2%)
  other arithmetic  1.69 us (1%)
    pallas_call x1, Pallas kernels, all_gather_rows(): pl.pallas_call(functools.partial(gather_kernel, n_row), out_shape=jax.Sha...  70.6 us
    pallas_call x1, Pallas kernels, reduce_scatter(): pl.pallas_call(functools.partial(ring_kernel, n_z, n_pieces), out_shape=j...  37.7 us
    pallas_call x1, Pallas kernels, stress_parts(): pl.pallas_call(functools.partial(parts_kernel, n_lag), out_shape=jax.Shap...  8.7 us
    ppermute x1, waiting for transfers between devices, local(): from_partner = lax.ppermute(other, 'lag', perm=[(0, 1), (1, 0)])  4.15 us
  transfers between devices with their start and end apart: 1, of which 1 were waited for; matrix products, arithmetic and copies ran while one was open for 0% of the time, Pallas kernels for 0%

profile of v10, /device:TPU:16, one launch (start us, length us, event | category | flops | bytes accessed | tf_op | source)
XLA Modules:
  0.0 126.0 jit_solution(6550910756719777135)
XLA Ops:
  0.6 0.8 reshape_squeeze.6.rows_ref
  1.4 0.8 reshape_squeeze.7.cols_ref
  2.2 0.0 copy-start
  2.2 70.6 %shard_map.104.hist_ref = bf16[8,4,128,512]{3,2,1,0:T(8,128)(2,1)} custom-call(bf16[4,128,512]{2,1,0:T(8,128)(2,1)} %bitcast.12), custom_call_target="tpu_custom_call" | custom-call | tf_op jit(solution)/shard_map/pallas_call | solution.py:166
  72.8 0.0 copy-done
  72.8 8.7 %shard_map.105 = f32[2,16,128,256]{3,2,1,0:T(8,128)S(1)} custom-call(s32[48]{0:T(128)S(1)} %reshape_squeeze.6.rows_ref, s32[48]{0:T(128)S(1)} %reshape_squeeze.7.cols_ref, s32[4]{0:T(128)S(1)} %bitcast.10, s32[1]{0:T(128)} %bitcast.1.lag_ref, bf16[8,4,128,512]{3,2,1,0:T(8,128)(2,1)} %shard_map.104.hist_ref, bf16[4,12,256,256]{3,2,1,0:T(8,128)(2,1)} %bitcast.11), custom_call_target="tpu_custom_call" | custom-call | tf_op jit(solution)/shard_map/pallas_call | solution.py:218
  81.5 0.1 slice_bitcast_fusion
  81.6 0.1 collective-permute-start
  81.7 4.1 %collective-permute-done = f32[16,128,256]{2,1,0:T(8,128)S(1)} collective-permute-done((f32[16,128,256]{2,1,0:T(8,128)S(1)}, f32[16,128,256]{2,1,0:T(8,128)S(1)}, u32[]{:S(2)}, u32[]{:S(2)}) %collective-permute-start) | collective-permute-done | bytes 2097184 | tf_op jit(solution)/shard_map/ppermute | solution.py:245
  85.9 0.4 fusion.part_ref
  86.3 0.0 copy-start.1
  86.3 0.0 copy-start.2
  86.3 0.0 copy-start.3
  86.3 0.0 copy-start.4
  86.3 37.7 %shard_map.106 = f32[128,256]{1,0:T(8,128)S(1)} custom-call(f32[16,128,256]{2,1,0:T(8,128)S(1)} %fusion.part_ref), custom_call_target="tpu_custom_call" | custom-call | tf_op jit(solution)/shard_map/pallas_call | solution.py:100
  124.0 0.0 copy-done.1
  124.0 0.0 copy-done.2
  124.1 0.0 copy-done.3
  124.1 0.0 copy-done.4
  124.1 1.3 %divide_subtract_fusion = f32[128,256]{1,0:T(8,128)} fusion(f32[128,256]{1,0:T(8,128)S(1)} %copy-done.1, f32[128,256]{1,0:T(8,128)S(1)} %copy-done.2, f32[128,256]{1,0:T(8,128)S(1)} %copy-done.3, f32[128,256]{1,0:T(8,128)S(1)} %shard_map.106, f32[128,256]{1,0:T(8,128)S(1)} %copy-done.4), kind=kLoop, calls=%fused_computation.3 | loop fusion | flops 2064384 | bytes 786432 | tf_op jit(solution)/shard_map/sub | solution.py:254
  125.4 0.7 copy.12
Async XLA Ops:
  2.2 70.6 %copy-start = (s32[1,1,4]{2,1,0:T(1,128)S(1)}, s32[1,1,4]{2,1,0:T(1,128)}, u32[]{:S(2)}) copy-start(s32[1,1,4]{2,1,0:T(1,128)} %param.13) | copy-start | bytes 52
  81.6 4.2 %collective-permute-start = (f32[16,128,256]{2,1,0:T(8,128)S(1)}, f32[16,128,256]{2,1,0:T(8,128)S(1)}, u32[]{:S(2)}, u32[]{:S(2)}) collective-permute-start(f32[16,128,256]{2,1,0:T(8,128)S(1)} %slice_bitcast_fusion), channel_id=1, source_target_pairs={{0,1},{1,0},{2,3},{3,2},{4,5},{5,4},{6,7},{7,6},{8,9},{9,8},{10,11... | collective-permute-start | bytes 6291464 | tf_op jit(solution)/shard_map/ppermute | solution.py:245
  86.3 37.8 %copy-start.1 = (f32[128,256]{1,0:T(8,128)S(1)}, f32[128,256]{1,0:T(8,128)}, u32[]{:S(2)}) copy-start(f32[128,256]{1,0:T(8,128)} %param.16) | copy-start | bytes 393220
  86.3 37.8 %copy-start.2 = (f32[128,256]{1,0:T(8,128)S(1)}, f32[128,256]{1,0:T(8,128)}, u32[]{:S(2)}) copy-start(f32[128,256]{1,0:T(8,128)} %param.15) | copy-start | bytes 393220
  86.3 37.8 %copy-start.3 = (f32[128,256]{1,0:T(8,128)S(1)}, f32[128,256]{1,0:T(8,128)}, u32[]{:S(2)}) copy-start(f32[128,256]{1,0:T(8,128)} %param.14) | copy-start | bytes 393220
  86.3 37.7 %copy-start.4 = (f32[128,256]{1,0:T(8,128)S(1)}, f32[128,256]{1,0:T(8,128)}, u32[]{:S(2)}) copy-start(f32[128,256]{1,0:T(8,128)} %param.17) | copy-start | bytes 393220

commit v11 on v10

--- a/solution.py
+++ b/solution.py
@@ -117,61 +117,101 @@
     )(part)
 
 
-def gather_kernel(n_row, piece_ref, out_ref, local_sem, send_sem, recv_sem):
+def gather_kernel(n_x, piece_ref, out_ref, local_sem, send_sem, recv_sem):
     me = lax.axis_index("row")
     col = lax.axis_index("col")
     lag = lax.axis_index("lag")
-
-    def peer(t):
-        return (t, col, lag)
+    y = me // n_x
+    x = me % n_x
+    right = x + 1
+    left = x + n_x - 1
+    across = 1 - y
+    half = piece_ref.shape[0] // 2
+
+    def slot(yy, xx):
+        return yy * n_x + lax.rem(xx, n_x)
+
+    def device(yy, xx):
+        return (slot(yy, xx), col, lag)
+
+    def region(index, part):
+        if part is None:
+            return out_ref.at[index], recv_sem.at[index, 0]
+        return out_ref.at[index, pl.ds(part * half, half)], recv_sem.at[index, part]
 
     barrier = pltpu.get_barrier_semaphore()
-    for d in range(1, n_row):
-        t = lax.rem(me + d, n_row)
-        pl.semaphore_signal(barrier, inc=1, device_id=peer(t), device_id_type=MESH)
-    pl.semaphore_wait(barrier, n_row - 1)
-
-    own = pltpu.make_async_copy(piece_ref, out_ref.at[me], local_sem)
+    for peer in (device(y, right), device(y, left), device(across, x)):
+        pl.semaphore_signal(barrier, inc=1, device_id=peer, device_id_type=MESH)
+    pl.semaphore_wait(barrier, 3)
+
+    mine = slot(y, x)
+    own = pltpu.make_async_copy(piece_ref, out_ref.at[mine], local_sem)
     own.start()
     sends = []
-    for d in range(1, n_row):
-        t = lax.rem(me + d, n_row)
+
+    def send(index, part, dest, from_input=False):
+        target, sem = region(index, part)
+        if from_input:
+            source = piece_ref
+        else:
+            source = region(index, part)[0]
         copy = pltpu.make_async_remote_copy(
-            src_ref=piece_ref,
-            dst_ref=out_ref.at[me],
-            send_sem=send_sem.at[t],
-            recv_sem=recv_sem.at[me],
-            device_id=peer(t),
+            src_ref=source,
+            dst_ref=target,
+            send_sem=send_sem.at[len(sends)],
+            recv_sem=sem,
+            device_id=dest,
             device_id_type=MESH,
         )
         copy.start()
         sends.append(copy)
-    for d in range(1, n_row):
-        s = lax.rem(me + n_row - d, n_row)
-        incoming = pltpu.make_async_remote_copy(
-            src_ref=piece_ref,
-            dst_ref=out_ref.at[s],
-            send_sem=send_sem.at[s],
-            recv_sem=recv_sem.at[s],
-            device_id=peer(s),
+
+    def arrive(index, part):
+        target, sem = region(index, part)
+        source = piece_ref if part is None else piece_ref.at[pl.ds(part * half, half)]
+        pltpu.make_async_remote_copy(
+            src_ref=source,
+            dst_ref=target,
+            send_sem=send_sem.at[0],
+            recv_sem=sem,
+            device_id=device(y, right),
             device_id_type=MESH,
-        )
-        incoming.wait_recv()
+        ).wait_recv()
+
+    send(mine, None, device(y, right), from_input=True)
+    send(mine, None, device(y, left), from_input=True)
+    send(mine, None, device(across, x), from_input=True)
+    arrive(slot(y, left), None)
+    send(slot(y, left), 0, device(y, right))
+    arrive(slot(y, right), None)
+    send(slot(y, right), 1, device(y, left))
+    arrive(slot(across, x), None)
+    send(slot(across, x), None, device(y, right))
+    send(slot(across, x), None, device(y, left))
+    arrive(slot(across, left), None)
+    send(slot(across, left), 0, device(y, right))
+    arrive(slot(across, right), None)
+    send(slot(across, right), 1, device(y, left))
+    for yy in (y, across):
+        arrive(slot(yy, x + 2), 0)
+        arrive(slot(yy, x + 2), 1)
     own.wait()
     for copy in sends:
         copy.wait_send()
 
 
 def all_gather_rows(piece, n_row):
+    n_x = n_row // 2
+    assert n_x == 4
     return pl.pallas_call(
-        functools.partial(gather_kernel, n_row),
+        functools.partial(gather_kernel, n_x),
         out_shape=jax.ShapeDtypeStruct((n_row,) + piece.shape, piece.dtype),
         in_specs=[pl.BlockSpec(memory_space=pltpu.VMEM)],
         out_specs=pl.BlockSpec(memory_space=pl.ANY),
         scratch_shapes=[
             pltpu.SemaphoreType.DMA(()),
-            pltpu.SemaphoreType.DMA((n_row,)),
-            pltpu.SemaphoreType.DMA((n_row,)),
+            pltpu.SemaphoreType.DMA((9,)),
+            pltpu.SemaphoreType.DMA((n_row, 2)),
         ],
         compiler_params=pltpu.CompilerParams(collective_id=1, has_side_effects=True),
     )(piece)

time: 126 us -> 97.8 us (0.78)
  the two profiles are of different devices: /device:TPU:16 before, /device:TPU:14 now
where the time goes in v11:
time: 97.8 us; the launch traced here: 97.6 us
  Pallas kernels  88.6 us (91%)
  waiting for transfers between devices  4.15 us (4%)
  local copies, waits for them, and re-layouts  2.35 us (2%)
  other arithmetic  1.69 us (2%)
    pallas_call x1, Pallas kernels, all_gather_rows(): pl.pallas_call(functools.partial(gather_kernel, n_x), out_shape=jax.Shape...  40.4 us
    pallas_call x1, Pallas kernels, reduce_scatter(): pl.pallas_call(functools.partial(ring_kernel, n_z, n_pieces), out_shape=j...  37.3 us
    pallas_call x1, Pallas kernels, stress_parts(): pl.pallas_call(functools.partial(parts_kernel, n_lag), out_shape=jax.Shap...  10.8 us
    ppermute x1, waiting for transfers between devices, local(): from_partner = lax.ppermute(other, 'lag', perm=[(0, 1), (1, 0)])  4.15 us
  transfers between devices with their start and end apart: 1, of which 1 were waited for; matrix products, arithmetic and copies ran while one was open for 0% of the time, Pallas kernels for 0%

profile of v11, /device:TPU:14, one launch (start us, length us, event | category | flops | bytes accessed | tf_op | source)
XLA Modules:
  0.0 97.6 jit_solution(1897531357858416705)
XLA Ops:
  0.6 0.8 reshape_squeeze.6.rows_ref
  1.4 0.8 reshape_squeeze.7.cols_ref
  2.2 0.0 copy-start
  2.2 40.4 %shard_map.104.hist_ref = bf16[8,4,128,512]{3,2,1,0:T(8,128)(2,1)} custom-call(bf16[4,128,512]{2,1,0:T(8,128)(2,1)} %bitcast.12), custom_call_target="tpu_custom_call" | custom-call | tf_op jit(solution)/shard_map/pallas_call | solution.py:206
  42.6 0.0 copy-done
  42.6 10.8 %shard_map.105 = f32[2,16,128,256]{3,2,1,0:T(8,128)S(1)} custom-call(s32[48]{0:T(128)S(1)} %reshape_squeeze.6.rows_ref, s32[48]{0:T(128)S(1)} %reshape_squeeze.7.cols_ref, s32[4]{0:T(128)S(1)} %bitcast.10, s32[1]{0:T(128)} %bitcast.1.lag_ref, bf16[8,4,128,512]{3,2,1,0:T(8,128)(2,1)} %shard_map.104.hist_ref, bf16[4,12,256,256]{3,2,1,0:T(8,128)(2,1)} %bitcast.11), custom_call_target="tpu_custom_call" | custom-call | tf_op jit(solution)/shard_map/pallas_call | solution.py:258
  53.5 0.1 slice_bitcast_fusion
  53.6 0.1 collective-permute-start
  53.7 4.1 %collective-permute-done = f32[16,128,256]{2,1,0:T(8,128)S(1)} collective-permute-done((f32[16,128,256]{2,1,0:T(8,128)S(1)}, f32[16,128,256]{2,1,0:T(8,128)S(1)}, u32[]{:S(2)}, u32[]{:S(2)}) %collective-permute-start) | collective-permute-done | bytes 2097184 | tf_op jit(solution)/shard_map/ppermute | solution.py:285
  57.9 0.4 fusion.part_ref
  58.3 0.0 copy-start.1
  58.3 0.0 copy-start.2
  58.3 0.0 copy-start.3
  58.3 0.0 copy-start.4
  58.3 37.3 %shard_map.106 = f32[128,256]{1,0:T(8,128)S(1)} custom-call(f32[16,128,256]{2,1,0:T(8,128)S(1)} %fusion.part_ref), custom_call_target="tpu_custom_call" | custom-call | tf_op jit(solution)/shard_map/pallas_call | solution.py:100
  95.6 0.0 copy-done.1
  95.6 0.0 copy-done.2
  95.6 0.0 copy-done.3
  95.7 0.0 copy-done.4
  95.7 1.3 %divide_subtract_fusion = f32[128,256]{1,0:T(8,128)} fusion(f32[128,256]{1,0:T(8,128)S(1)} %copy-done.1, f32[128,256]{1,0:T(8,128)S(1)} %copy-done.2, f32[128,256]{1,0:T(8,128)S(1)} %copy-done.3, f32[128,256]{1,0:T(8,128)S(1)} %shard_map.106, f32[128,256]{1,0:T(8,128)S(1)} %copy-done.4), kind=kLoop, calls=%fused_computation.3 | loop fusion | flops 2064384 | bytes 786432 | tf_op jit(solution)/shard_map/sub | solution.py:294
  96.9 0.7 copy.12
Async XLA Ops:
  2.2 40.5 %copy-start = (s32[1,1,4]{2,1,0:T(1,128)S(1)}, s32[1,1,4]{2,1,0:T(1,128)}, u32[]{:S(2)}) copy-start(s32[1,1,4]{2,1,0:T(1,128)} %param.13) | copy-start | bytes 52
  53.6 4.2 %collective-permute-start = (f32[16,128,256]{2,1,0:T(8,128)S(1)}, f32[16,128,256]{2,1,0:T(8,128)S(1)}, u32[]{:S(2)}, u32[]{:S(2)}) collective-permute-start(f32[16,128,256]{2,1,0:T(8,128)S(1)} %slice_bitcast_fusion), channel_id=1, source_target_pairs={{0,1},{1,0},{2,3},{3,2},{4,5},{5,4},{6,7},{7,6},{8,9},{9,8},{10,11... | collective-permute-start | bytes 6291464 | tf_op jit(solution)/shard_map/ppermute | solution.py:285
  58.3 37.4 %copy-start.1 = (f32[128,256]{1,0:T(8,128)S(1)}, f32[128,256]{1,0:T(8,128)}, u32[]{:S(2)}) copy-start(f32[128,256]{1,0:T(8,128)} %param.16) | copy-start | bytes 393220
  58.3 37.4 %copy-start.2 = (f32[128,256]{1,0:T(8,128)S(1)}, f32[128,256]{1,0:T(8,128)}, u32[]{:S(2)}) copy-start(f32[128,256]{1,0:T(8,128)} %param.15) | copy-start | bytes 393220
  58.3 37.3 %copy-start.3 = (f32[128,256]{1,0:T(8,128)S(1)}, f32[128,256]{1,0:T(8,128)}, u32[]{:S(2)}) copy-start(f32[128,256]{1,0:T(8,128)} %param.14) | copy-start | bytes 393220
  58.3 37.3 %copy-start.4 = (f32[128,256]{1,0:T(8,128)S(1)}, f32[128,256]{1,0:T(8,128)}, u32[]{:S(2)}) copy-start(f32[128,256]{1,0:T(8,128)} %param.17) | copy-start | bytes 393220

commit v12 on v11

--- a/solution.py
+++ b/solution.py
@@ -117,7 +117,7 @@
     )(part)
 
 
-def gather_kernel(n_x, piece_ref, out_ref, local_sem, send_sem, recv_sem):
+def gather_kernel(n_x, n_pieces, piece_ref, out_ref, local_sem, send_sem, recv_sem):
     me = lax.axis_index("row")
     col = lax.axis_index("col")
     lag = lax.axis_index("lag")
@@ -127,6 +127,7 @@
     left = x + n_x - 1
     across = 1 - y
     half = piece_ref.shape[0] // 2
+    rows = piece_ref.shape[1] // n_pieces
 
     def slot(yy, xx):
         return yy * n_x + lax.rem(xx, n_x)
@@ -134,10 +135,14 @@
     def device(yy, xx):
         return (slot(yy, xx), col, lag)
 
-    def region(index, part):
-        if part is None:
-            return out_ref.at[index], recv_sem.at[index, 0]
-        return out_ref.at[index, pl.ds(part * half, half)], recv_sem.at[index, part]
+    def span(part):
+        return slice(None) if part is None else pl.ds(part * half, half)
+
+    def region(ref, part, piece):
+        return ref.at[span(part), pl.ds(piece * rows, rows)]
+
+    def semaphore(index, part, piece):
+        return recv_sem.at[index, 0 if part is None else part, piece]
 
     barrier = pltpu.get_barrier_semaphore()
     for peer in (device(y, right), device(y, left), device(across, x)):
@@ -150,68 +155,73 @@
     sends = []
 
     def send(index, part, dest, from_input=False):
-        target, sem = region(index, part)
-        if from_input:
-            source = piece_ref
-        else:
-            source = region(index, part)[0]
-        copy = pltpu.make_async_remote_copy(
-            src_ref=source,
-            dst_ref=target,
-            send_sem=send_sem.at[len(sends)],
-            recv_sem=sem,
-            device_id=dest,
-            device_id_type=MESH,
-        )
-        copy.start()
-        sends.append(copy)
-
-    def arrive(index, part):
-        target, sem = region(index, part)
-        source = piece_ref if part is None else piece_ref.at[pl.ds(part * half, half)]
+        for piece in range(n_pieces):
+            source = piece_ref if from_input else out_ref.at[index]
+            copy = pltpu.make_async_remote_copy(
+                src_ref=region(source, part, piece),
+                dst_ref=region(out_ref.at[index], part, piece),
+                send_sem=send_sem.at[len(sends)],
+                recv_sem=semaphore(index, part, piece),
+                device_id=dest,
+                device_id_type=MESH,
+            )
+            copy.start()
+            sends.append(copy)
+
+    def arrive(index, part, piece):
         pltpu.make_async_remote_copy(
-            src_ref=source,
-            dst_ref=target,
+            src_ref=region(piece_ref, part, piece),
+            dst_ref=region(out_ref.at[index], part, piece),
             send_sem=send_sem.at[0],
-            recv_sem=sem,
+            recv_sem=semaphore(index, part, piece),
             device_id=device(y, right),
             device_id_type=MESH,
         ).wait_recv()
 
+    def relay(index, part, dests):
+        for piece in range(n_pieces):
+            arrive(index, None, piece)
+            for dest in dests:
+                for_piece = pltpu.make_async_remote_copy(
+                    src_ref=region(out_ref.at[index], part, piece),
+                    dst_ref=region(out_ref.at[index], part, piece),
+                    send_sem=send_sem.at[len(sends)],
+                    recv_sem=semaphore(index, part, piece),
+                    device_id=dest,
+                    device_id_type=MESH,
+                )
+                for_piece.start()
+                sends.append(for_piece)
+
     send(mine, None, device(y, right), from_input=True)
     send(mine, None, device(y, left), from_input=True)
     send(mine, None, device(across, x), from_input=True)
-    arrive(slot(y, left), None)
-    send(slot(y, left), 0, device(y, right))
-    arrive(slot(y, right), None)
-    send(slot(y, right), 1, device(y, left))
-    arrive(slot(across, x), None)
-    send(slot(across, x), None, device(y, right))
-    send(slot(across, x), None, device(y, left))
-    arrive(slot(across, left), None)
-    send(slot(across, left), 0, device(y, right))
-    arrive(slot(across, right), None)
-    send(slot(across, right), 1, device(y, left))
+    relay(slot(y, left), 0, [device(y, right)])
+    relay(slot(y, right), 1, [device(y, left)])
+    relay(slot(across, x), None, [device(y, right), device(y, left)])
+    relay(slot(across, left), 0, [device(y, right)])
+    relay(slot(across, right), 1, [device(y, left)])
     for yy in (y, across):
-        arrive(slot(yy, x + 2), 0)
-        arrive(slot(yy, x + 2), 1)
+        for piece in range(n_pieces):
+            arrive(slot(yy, x + 2), 0, piece)
+            arrive(slot(yy, x + 2), 1, piece)
     own.wait()
     for copy in sends:
         copy.wait_send()
 
 
-def all_gather_rows(piece, n_row):
+def all_gather_rows(piece, n_row, n_pieces=2):
     n_x = n_row // 2
     assert n_x == 4
     return pl.pallas_call(
-        functools.partial(gather_kernel, n_x),
+        functools.partial(gather_kernel, n_x, n_pieces),
         out_shape=jax.ShapeDtypeStruct((n_row,) + piece.shape, piece.dtype),
         in_specs=[pl.BlockSpec(memory_space=pltpu.VMEM)],
         out_specs=pl.BlockSpec(memory_space=pl.ANY),
         scratch_shapes=[
             pltpu.SemaphoreType.DMA(()),
-            pltpu.SemaphoreType.DMA((9,)),
-            pltpu.SemaphoreType.DMA((n_row, 2)),
+            pltpu.SemaphoreType.DMA((9 * n_pieces,)),
+            pltpu.SemaphoreType.DMA((n_row, 2, n_pieces)),
         ],
         compiler_params=pltpu.CompilerParams(collective_id=1, has_side_effects=True),
     )(piece)

time: 97.8 us -> 97.7 us (level)
  the two profiles are of different devices: /device:TPU:14 before, /device:TPU:8 now
where the time goes in v12:
time: 97.7 us; the launch traced here: 97.5 us
  Pallas kernels  88.5 us (91%)
  waiting for transfers between devices  4.15 us (4%)
  local copies, waits for them, and re-layouts  2.35 us (2%)
  other arithmetic  1.69 us (2%)
    pallas_call x1, Pallas kernels, all_gather_rows(): pl.pallas_call(functools.partial(gather_kernel, n_x, n_pieces), out_shape...  40.8 us
    pallas_call x1, Pallas kernels, reduce_scatter(): pl.pallas_call(functools.partial(ring_kernel, n_z, n_pieces), out_shape=j...  37.6 us
    pallas_call x1, Pallas kernels, stress_parts(): pl.pallas_call(functools.partial(parts_kernel, n_lag), out_shape=jax.Shap...  10.1 us
    ppermute x1, waiting for transfers between devices, local(): from_partner = lax.ppermute(other, 'lag', perm=[(0, 1), (1, 0)])  4.15 us
  transfers between devices with their start and end apart: 1, of which 1 were waited for; matrix products, arithmetic and copies ran while one was open for 0% of the time, Pallas kernels for 0%

profile of v12, /device:TPU:8, one launch (start us, length us, event | category | flops | bytes accessed | tf_op | source)
XLA Modules:
  0.0 97.5 jit_solution(6341507226441675972)
XLA Ops:
  0.6 0.8 reshape_squeeze.6.rows_ref
  1.4 0.8 reshape_squeeze.7.cols_ref
  2.2 0.0 copy-start
  2.2 40.8 %shard_map.104.hist_ref = bf16[8,4,128,512]{3,2,1,0:T(8,128)(2,1)} custom-call(bf16[4,128,512]{2,1,0:T(8,128)(2,1)} %bitcast.12), custom_call_target="tpu_custom_call" | custom-call | tf_op jit(solution)/shard_map/pallas_call | solution.py:216
  43.0 0.0 copy-done
  43.0 10.1 %shard_map.105 = f32[2,16,128,256]{3,2,1,0:T(8,128)S(1)} custom-call(s32[48]{0:T(128)S(1)} %reshape_squeeze.6.rows_ref, s32[48]{0:T(128)S(1)} %reshape_squeeze.7.cols_ref, s32[4]{0:T(128)S(1)} %bitcast.10, s32[1]{0:T(128)} %bitcast.1.lag_ref, bf16[8,4,128,512]{3,2,1,0:T(8,128)(2,1)} %shard_map.104.hist_ref, bf16[4,12,256,256]{3,2,1,0:T(8,128)(2,1)} %bitcast.11), custom_call_target="tpu_custom_call" | custom-call | tf_op jit(solution)/shard_map/pallas_call | solution.py:268
  53.0 0.1 slice_bitcast_fusion
  53.2 0.1 collective-permute-start
  53.3 4.1 %collective-permute-done = f32[16,128,256]{2,1,0:T(8,128)S(1)} collective-permute-done((f32[16,128,256]{2,1,0:T(8,128)S(1)}, f32[16,128,256]{2,1,0:T(8,128)S(1)}, u32[]{:S(2)}, u32[]{:S(2)}) %collective-permute-start) | collective-permute-done | bytes 2097184 | tf_op jit(solution)/shard_map/ppermute | solution.py:295
  57.4 0.4 fusion.part_ref
  57.8 0.0 copy-start.1
  57.9 0.0 copy-start.2
  57.9 0.0 copy-start.3
  57.9 0.0 copy-start.4
  57.9 37.6 %shard_map.106 = f32[128,256]{1,0:T(8,128)S(1)} custom-call(f32[16,128,256]{2,1,0:T(8,128)S(1)} %fusion.part_ref), custom_call_target="tpu_custom_call" | custom-call | tf_op jit(solution)/shard_map/pallas_call | solution.py:100
  95.5 0.0 copy-done.1
  95.5 0.0 copy-done.2
  95.5 0.0 copy-done.3
  95.6 0.0 copy-done.4
  95.6 1.3 %divide_subtract_fusion = f32[128,256]{1,0:T(8,128)} fusion(f32[128,256]{1,0:T(8,128)S(1)} %copy-done.1, f32[128,256]{1,0:T(8,128)S(1)} %copy-done.2, f32[128,256]{1,0:T(8,128)S(1)} %copy-done.3, f32[128,256]{1,0:T(8,128)S(1)} %shard_map.106, f32[128,256]{1,0:T(8,128)S(1)} %copy-done.4), kind=kLoop, calls=%fused_computation.3 | loop fusion | flops 2064384 | bytes 786432 | tf_op jit(solution)/shard_map/sub | solution.py:304
  96.8 0.7 copy.12
Async XLA Ops:
  2.2 40.8 %copy-start = (s32[1,1,4]{2,1,0:T(1,128)S(1)}, s32[1,1,4]{2,1,0:T(1,128)}, u32[]{:S(2)}) copy-start(s32[1,1,4]{2,1,0:T(1,128)} %param.13) | copy-start | bytes 52
  53.2 4.2 %collective-permute-start = (f32[16,128,256]{2,1,0:T(8,128)S(1)}, f32[16,128,256]{2,1,0:T(8,128)S(1)}, u32[]{:S(2)}, u32[]{:S(2)}) collective-permute-start(f32[16,128,256]{2,1,0:T(8,128)S(1)} %slice_bitcast_fusion), channel_id=1, source_target_pairs={{0,1},{1,0},{2,3},{3,2},{4,5},{5,4},{6,7},{7,6},{8,9},{9,8},{10,11... | collective-permute-start | bytes 6291464 | tf_op jit(solution)/shard_map/ppermute | solution.py:295
  57.8 37.7 %copy-start.1 = (f32[128,256]{1,0:T(8,128)S(1)}, f32[128,256]{1,0:T(8,128)}, u32[]{:S(2)}) copy-start(f32[128,256]{1,0:T(8,128)} %param.16) | copy-start | bytes 393220
  57.9 37.7 %copy-start.2 = (f32[128,256]{1,0:T(8,128)S(1)}, f32[128,256]{1,0:T(8,128)}, u32[]{:S(2)}) copy-start(f32[128,256]{1,0:T(8,128)} %param.15) | copy-start | bytes 393220
  57.9 37.7 %copy-start.3 = (f32[128,256]{1,0:T(8,128)S(1)}, f32[128,256]{1,0:T(8,128)}, u32[]{:S(2)}) copy-start(f32[128,256]{1,0:T(8,128)} %param.14) | copy-start | bytes 393220
  57.9 37.7 %copy-start.4 = (f32[128,256]{1,0:T(8,128)S(1)}, f32[128,256]{1,0:T(8,128)}, u32[]{:S(2)}) copy-start(f32[128,256]{1,0:T(8,128)} %param.17) | copy-start | bytes 393220

commit v13 on v11

--- a/solution.py
+++ b/solution.py
@@ -230,10 +230,10 @@
     for k in range(slots):
         @pl.when(k < count_ref[lag])
         def _():
-            col = cols_ref[lag * slots + k]
-            row = rows_ref[lag * slots + k]
-            start = pl.multiple_of((col % halves) * side, side)
-            history = hist_ref[col // halves, 0, :, pl.ds(start, side)]
+            col = cols_ref[lag, k]
+            row = rows_ref[lag, k]
+            both = hist_ref[col // halves, 0]
+            history = jnp.where(col % halves == 0, both[:, :side], both[:, side:])
             contrib = lax.dot_general(
                 history, tiles_ref[0, k], (((1,), (1,)), ((), ())),
                 preferred_element_type=jnp.float32,
@@ -260,7 +260,7 @@
         out_shape=jax.ShapeDtypeStruct((2, n_col, sims, side), jnp.float32),
         grid_spec=grid_spec,
         compiler_params=pltpu.CompilerParams(vmem_limit_bytes=48 * 1024 * 1024),
-    )(rows.reshape(-1), cols.reshape(-1), count, lag, history, tiles)
+    )(rows, cols, count, lag, history, tiles)
 
 
 def local(

time: 97.8 us -> 97.2 us (level)
  the two profiles are of different devices: /device:TPU:14 before, /device:TPU:6 now
where the time goes in v13:
time: 97.2 us; the launch traced here: 97 us
  Pallas kernels  89.5 us (92%)
  waiting for transfers between devices  4.15 us (4%)
  other arithmetic  1.69 us (2%)
    pallas_call x1, Pallas kernels, all_gather_rows(): pl.pallas_call(functools.partial(gather_kernel, n_x), out_shape=jax.Shape...  41.7 us
    pallas_call x1, Pallas kernels, reduce_scatter(): pl.pallas_call(functools.partial(ring_kernel, n_z, n_pieces), out_shape=j...  38.1 us
    pallas_call x1, Pallas kernels, stress_parts(): pl.pallas_call(functools.partial(parts_kernel, n_lag), out_shape=jax.Shap...  9.69 us
    ppermute x1, waiting for transfers between devices, local(): from_partner = lax.ppermute(other, 'lag', perm=[(0, 1), (1, 0)])  4.15 us
  transfers between devices with their start and end apart: 1, of which 1 were waited for; matrix products, arithmetic and copies ran while one was open for 0% of the time, Pallas kernels for 0%

profile of v13, /device:TPU:6, one launch (start us, length us, event | category | flops | bytes accessed | tf_op | source)
XLA Modules:
  0.0 97.0 jit_solution(753954174033615060)
XLA Ops:
  0.6 0.0 copy-start
  0.6 0.0 copy-start.1
  0.7 0.0 copy-start.2
  0.7 41.7 %shard_map.104.hist_ref = bf16[8,4,128,512]{3,2,1,0:T(8,128)(2,1)} custom-call(bf16[4,128,512]{2,1,0:T(8,128)(2,1)} %bitcast.16), custom_call_target="tpu_custom_call" | custom-call | tf_op jit(solution)/shard_map/pallas_call | solution.py:206
  42.4 0.0 copy-done
  42.4 0.0 copy-done.1
  42.4 0.0 copy-done.2
  42.4 9.7 %shard_map.105 = f32[2,16,128,256]{3,2,1,0:T(8,128)S(1)} custom-call(s32[4,12]{1,0:T(4,128)S(1)} %bitcast.12, s32[4,12]{1,0:T(4,128)S(1)} %bitcast.13, s32[4]{0:T(128)S(1)} %bitcast.14, s32[1]{0:T(128)} %bitcast.3.lag_ref, bf16[8,4,128,512]{3,2,1,0:T(8,128)(2,1)} %shard_map.104.hist_ref, bf16[4,12,256,256]{3,2,1,0:T(8,128)(2,1)} %bitcast.15), custom_call_target="tpu_custom_call" | custom-call | tf_op jit(solution)/shard_map/pallas_call | solution.py:258
  52.1 0.1 slice_bitcast_fusion
  52.2 0.1 collective-permute-start
  52.3 4.1 %collective-permute-done = f32[16,128,256]{2,1,0:T(8,128)S(1)} collective-permute-done((f32[16,128,256]{2,1,0:T(8,128)S(1)}, f32[16,128,256]{2,1,0:T(8,128)S(1)}, u32[]{:S(2)}, u32[]{:S(2)}) %collective-permute-start) | collective-permute-done | bytes 2097184 | tf_op jit(solution)/shard_map/ppermute | solution.py:285
  56.5 0.4 fusion.part_ref
  56.9 0.0 copy-start.3
  56.9 0.0 copy-start.4
  56.9 0.0 copy-start.5
  56.9 0.0 copy-start.6
  57.0 38.1 %shard_map.106 = f32[128,256]{1,0:T(8,128)S(1)} custom-call(f32[16,128,256]{2,1,0:T(8,128)S(1)} %fusion.part_ref), custom_call_target="tpu_custom_call" | custom-call | tf_op jit(solution)/shard_map/pallas_call | solution.py:100
  95.0 0.0 copy-done.3
  95.0 0.0 copy-done.4
  95.1 0.0 copy-done.5
  95.1 0.0 copy-done.6
  95.1 1.3 %divide_subtract_fusion = f32[128,256]{1,0:T(8,128)} fusion(f32[128,256]{1,0:T(8,128)S(1)} %copy-done.3, f32[128,256]{1,0:T(8,128)S(1)} %copy-done.4, f32[128,256]{1,0:T(8,128)S(1)} %copy-done.5, f32[128,256]{1,0:T(8,128)S(1)} %shard_map.106, f32[128,256]{1,0:T(8,128)S(1)} %copy-done.6), kind=kLoop, calls=%fused_computation.3 | loop fusion | flops 2064384 | bytes 786432 | tf_op jit(solution)/shard_map/sub | solution.py:294
  96.4 0.7 copy.12
Async XLA Ops:
  0.6 41.7 %copy-start = (s32[1,1,4,12]{3,2,1,0:T(4,128)S(1)}, s32[1,1,4,12]{3,2,1,0:T(4,128)}, u32[]{:S(2)}) copy-start(s32[1,1,4,12]{3,2,1,0:T(4,128)} %param.11) | copy-start | bytes 580
  0.6 41.7 %copy-start.1 = (s32[1,1,4,12]{3,2,1,0:T(4,128)S(1)}, s32[1,1,4,12]{3,2,1,0:T(4,128)}, u32[]{:S(2)}) copy-start(s32[1,1,4,12]{3,2,1,0:T(4,128)} %param.12) | copy-start | bytes 580
  0.7 41.7 %copy-start.2 = (s32[1,1,4]{2,1,0:T(1,128)S(1)}, s32[1,1,4]{2,1,0:T(1,128)}, u32[]{:S(2)}) copy-start(s32[1,1,4]{2,1,0:T(1,128)} %param.13) | copy-start | bytes 52
  52.2 4.2 %collective-permute-start = (f32[16,128,256]{2,1,0:T(8,128)S(1)}, f32[16,128,256]{2,1,0:T(8,128)S(1)}, u32[]{:S(2)}, u32[]{:S(2)}) collective-permute-start(f32[16,128,256]{2,1,0:T(8,128)S(1)} %slice_bitcast_fusion), channel_id=1, source_target_pairs={{0,1},{1,0},{2,3},{3,2},{4,5},{5,4},{6,7},{7,6},{8,9},{9,8},{10,11... | collective-permute-start | bytes 6291464 | tf_op jit(solution)/shard_map/ppermute | solution.py:285
  56.9 38.1 %copy-start.3 = (f32[128,256]{1,0:T(8,128)S(1)}, f32[128,256]{1,0:T(8,128)}, u32[]{:S(2)}) copy-start(f32[128,256]{1,0:T(8,128)} %param.16) | copy-start | bytes 393220
  56.9 38.1 %copy-start.4 = (f32[128,256]{1,0:T(8,128)S(1)}, f32[128,256]{1,0:T(8,128)}, u32[]{:S(2)}) copy-start(f32[128,256]{1,0:T(8,128)} %param.15) | copy-start | bytes 393220
  56.9 38.1 %copy-start.5 = (f32[128,256]{1,0:T(8,128)S(1)}, f32[128,256]{1,0:T(8,128)}, u32[]{:S(2)}) copy-start(f32[128,256]{1,0:T(8,128)} %param.14) | copy-start | bytes 393220
  56.9 38.1 %copy-start.6 = (f32[128,256]{1,0:T(8,128)S(1)}, f32[128,256]{1,0:T(8,128)}, u32[]{:S(2)}) copy-start(f32[128,256]{1,0:T(8,128)} %param.17) | copy-start | bytes 393220

commit v14 on v13

--- a/solution.py
+++ b/solution.py
@@ -26,53 +26,65 @@
     up = lax.rem(z + 1, n_z)
     down = lax.rem(z + n_z - 1, n_z)
     rows = part_ref.shape[1] // n_pieces
+    longer = n_z // 2
+    shorter = n_z - 1 - longer
 
     def device(zz, yy):
         return (row, zz * 2 + yy, lag)
+
+    def length(way, side):
+        return longer if way == side else shorter
 
     barrier = pltpu.get_barrier_semaphore()
     for peer in (device(up, y_hi), device(down, y_hi), device(z, 1 - y_hi)):
         pl.semaphore_signal(barrier, inc=1, device_id=peer, device_id_type=MESH)
     pl.semaphore_wait(barrier, 3)
 
-    steps = n_z - 1
     copies = {}
-    for step in range(steps):
+    for step in range(longer):
         for piece in range(n_pieces):
             span = pl.ds(piece * rows, rows)
-            for way in range(2):
-                if way == 0:
-                    target = lax.rem(z + n_z - 1 - step, n_z)
-                    dest = device(up, y_hi)
-                else:
-                    target = lax.rem(z + 1 + step, n_z)
-                    dest = device(down, y_hi)
-                block = target * 2 + way
-                if step == 0:
-                    source = part_ref.at[block, span]
-                else:
-                    copies[way, step - 1, piece].wait_recv()
-                    forward[way, step, piece] = (
-                        recv[way, step - 1, piece] + part_ref[block, span]
+            for side in range(2):
+                for way in range(2):
+                    chain = length(way, side)
+                    if step >= chain:
+                        continue
+                    if side == 0:
+                        target = lax.rem(z + chain - step, n_z)
+                        dest = device(up, y_hi)
+                    else:
+                        target = lax.rem(z + n_z - chain + step, n_z)
+                        dest = device(down, y_hi)
+                    block = target * 2 + way
+                    if step == 0:
+                        source = part_ref.at[block, span]
+                    else:
+                        copies[side, way, step - 1, piece].wait_recv()
+                        forward[side, way, step, piece] = (
+                            recv[side, way, step - 1, piece] + part_ref[block, span]
+                        )
+                        source = forward.at[side, way, step, piece]
+                    copy = pltpu.make_async_remote_copy(
+                        src_ref=source,
+                        dst_ref=recv.at[side, way, step, piece],
+                        send_sem=send_sem.at[side, way, step, piece],
+                        recv_sem=recv_sem.at[side, way, step, piece],
+                        device_id=dest,
+                        device_id_type=MESH,
                     )
-                    source = forward.at[way, step, piece]
-                copy = pltpu.make_async_remote_copy(
-                    src_ref=source,
-                    dst_ref=recv.at[way, step, piece],
-                    send_sem=send_sem.at[way, step, piece],
-                    recv_sem=recv_sem.at[way, step, piece],
-                    device_id=dest,
-                    device_id_type=MESH,
-                )
-                copy.start()
-                copies[way, step, piece] = copy
+                    copy.start()
+                    copies[side, way, step, piece] = copy
 
     handoffs = []
     for piece in range(n_pieces):
         span = pl.ds(piece * rows, rows)
         for way in range(2):
-            copies[way, steps - 1, piece].wait_recv()
-            final[way, piece] = recv[way, steps - 1, piece] + part_ref[z * 2 + way, span]
+            total = part_ref[z * 2 + way, span]
+            for side in range(2):
+                last = length(way, side) - 1
+                copies[side, way, last, piece].wait_recv()
+                total = total + recv[side, way, last, piece]
+            final[way, piece] = total
         handoff = pltpu.make_async_remote_copy(
             src_ref=final.at[1 - y_hi, piece],
             dst_ref=cross.at[piece],
@@ -95,7 +107,7 @@
 def reduce_scatter(part, n_col, n_pieces=4):
     group, sims, tile = part.shape
     n_z = n_col // 2
-    steps = n_z - 1
+    longer = n_z // 2
     rows = sims // n_pieces
     return pl.pallas_call(
         functools.partial(ring_kernel, n_z, n_pieces),
@@ -103,12 +115,12 @@
         in_specs=[pl.BlockSpec(memory_space=pltpu.VMEM)],
         out_specs=pl.BlockSpec(memory_space=pltpu.VMEM),
         scratch_shapes=[
-            pltpu.VMEM((2, steps, n_pieces, rows, tile), jnp.float32),
-            pltpu.VMEM((2, steps, n_pieces, rows, tile), jnp.float32),
+            pltpu.VMEM((2, 2, longer, n_pieces, rows, tile), jnp.float32),
+            pltpu.VMEM((2, 2, longer, n_pieces, rows, tile), jnp.float32),
             pltpu.VMEM((2, n_pieces, rows, tile), jnp.float32),
             pltpu.VMEM((n_pieces, rows, tile), jnp.float32),
-            pltpu.SemaphoreType.DMA((2, steps, n_pieces)),
-            pltpu.SemaphoreType.DMA((2, steps, n_pieces)),
+            pltpu.SemaphoreType.DMA((2, 2, longer, n_pieces)),
+            pltpu.SemaphoreType.DMA((2, 2, longer, n_pieces)),
             pltpu.SemaphoreType.DMA((2, n_pieces)),
         ],
         compiler_params=pltpu.CompilerParams(

time: 97.2 us -> 94.3 us (0.970)
  the two profiles are of different devices: /device:TPU:6 before, /device:TPU:1 now
where the time goes in v14:
time: 94.3 us; the launch traced here: 93.1 us
  Pallas kernels  83.9 us (89%)
  waiting for transfers between devices  3.79 us (4%)
  starting transfers between devices  2.07 us (2%)
  other arithmetic  1.69 us (2%)
    pallas_call x1, Pallas kernels, all_gather_rows(): pl.pallas_call(functools.partial(gather_kernel, n_x), out_shape=jax.Shape...  40.2 us
    pallas_call x1, Pallas kernels, reduce_scatter(): pl.pallas_call(functools.partial(ring_kernel, n_z, n_pieces), out_shape=j...  34.3 us
    pallas_call x1, Pallas kernels, stress_parts(): pl.pallas_call(functools.partial(parts_kernel, n_lag), out_shape=jax.Shap...  9.35 us
    ppermute x1, waiting for transfers between devices, local(): from_partner = lax.ppermute(other, 'lag', perm=[(0, 1), (1, 0)])  3.79 us
    ppermute x1, starting transfers between devices, local(): from_partner = lax.ppermute(other, 'lag', perm=[(0, 1), (1, 0)])  2.07 us
  transfers between devices with their start and end apart: 1, of which 1 were waited for; matrix products, arithmetic and copies ran while one was open for 0% of the time, Pallas kernels for 0%

profile of v14, /device:TPU:1, one launch (start us, length us, event | category | flops | bytes accessed | tf_op | source)
XLA Modules:
  0.0 93.1 jit_solution(13569993996860384908)
XLA Ops:
  0.6 0.0 copy-start
  0.6 0.0 copy-start.1
  0.7 0.0 copy-start.2
  0.7 40.2 %shard_map.104.hist_ref = bf16[8,4,128,512]{3,2,1,0:T(8,128)(2,1)} custom-call(bf16[4,128,512]{2,1,0:T(8,128)(2,1)} %bitcast.16), custom_call_target="tpu_custom_call" | custom-call | tf_op jit(solution)/shard_map/pallas_call | solution.py:218
  40.9 0.0 copy-done
  40.9 0.0 copy-done.1
  40.9 0.0 copy-done.2
  40.9 9.3 %shard_map.105 = f32[2,16,128,256]{3,2,1,0:T(8,128)S(1)} custom-call(s32[4,12]{1,0:T(4,128)S(1)} %bitcast.12, s32[4,12]{1,0:T(4,128)S(1)} %bitcast.13, s32[4]{0:T(128)S(1)} %bitcast.14, s32[1]{0:T(128)} %bitcast.3.lag_ref, bf16[8,4,128,512]{3,2,1,0:T(8,128)(2,1)} %shard_map.104.hist_ref, bf16[4,12,256,256]{3,2,1,0:T(8,128)(2,1)} %bitcast.15), custom_call_target="tpu_custom_call" | custom-call | tf_op jit(solution)/shard_map/pallas_call | solution.py:270
  50.3 0.1 slice_bitcast_fusion
  50.4 2.1 %collective-permute-start = (f32[16,128,256]{2,1,0:T(8,128)S(1)}, f32[16,128,256]{2,1,0:T(8,128)S(1)}, u32[]{:S(2)}, u32[]{:S(2)}) collective-permute-start(f32[16,128,256]{2,1,0:T(8,128)S(1)} %slice_bitcast_fusion), channel_id=1, source_target_pairs={{0,1},{1,0},{2,3},{3,2},{4,5},{5,4},{6,7},{7,6},{8,9},{9,8},{10,11... | collective-permute-start | bytes 6291464 | tf_op jit(solution)/shard_map/ppermute | solution.py:297
  52.5 3.8 %collective-permute-done = f32[16,128,256]{2,1,0:T(8,128)S(1)} collective-permute-done((f32[16,128,256]{2,1,0:T(8,128)S(1)}, f32[16,128,256]{2,1,0:T(8,128)S(1)}, u32[]{:S(2)}, u32[]{:S(2)}) %collective-permute-start) | collective-permute-done | bytes 2097184 | tf_op jit(solution)/shard_map/ppermute | solution.py:297
  56.3 0.4 fusion.part_ref
  56.7 0.0 copy-start.3
  56.7 0.0 copy-start.4
  56.7 0.0 copy-start.5
  56.8 0.0 copy-start.6
  56.8 34.3 %shard_map.106 = f32[128,256]{1,0:T(8,128)S(1)} custom-call(f32[16,128,256]{2,1,0:T(8,128)S(1)} %fusion.part_ref), custom_call_target="tpu_custom_call" | custom-call | tf_op jit(solution)/shard_map/pallas_call | solution.py:112
  91.1 0.0 copy-done.3
  91.1 0.0 copy-done.4
  91.1 0.0 copy-done.5
  91.1 0.0 copy-done.6
  91.2 1.3 %divide_subtract_fusion = f32[128,256]{1,0:T(8,128)} fusion(f32[128,256]{1,0:T(8,128)S(1)} %copy-done.3, f32[128,256]{1,0:T(8,128)S(1)} %copy-done.4, f32[128,256]{1,0:T(8,128)S(1)} %copy-done.5, f32[128,256]{1,0:T(8,128)S(1)} %shard_map.106, f32[128,256]{1,0:T(8,128)S(1)} %copy-done.6), kind=kLoop, calls=%fused_computation.3 | loop fusion | flops 2064384 | bytes 786432 | tf_op jit(solution)/shard_map/sub | solution.py:306
  92.4 0.7 copy.12
Async XLA Ops:
  0.6 40.3 %copy-start = (s32[1,1,4,12]{3,2,1,0:T(4,128)S(1)}, s32[1,1,4,12]{3,2,1,0:T(4,128)}, u32[]{:S(2)}) copy-start(s32[1,1,4,12]{3,2,1,0:T(4,128)} %param.11) | copy-start | bytes 580
  0.6 40.3 %copy-start.1 = (s32[1,1,4,12]{3,2,1,0:T(4,128)S(1)}, s32[1,1,4,12]{3,2,1,0:T(4,128)}, u32[]{:S(2)}) copy-start(s32[1,1,4,12]{3,2,1,0:T(4,128)} %param.12) | copy-start | bytes 580
  0.7 40.3 %copy-start.2 = (s32[1,1,4]{2,1,0:T(1,128)S(1)}, s32[1,1,4]{2,1,0:T(1,128)}, u32[]{:S(2)}) copy-start(s32[1,1,4]{2,1,0:T(1,128)} %param.13) | copy-start | bytes 52
  50.4 5.9 %collective-permute-start = (f32[16,128,256]{2,1,0:T(8,128)S(1)}, f32[16,128,256]{2,1,0:T(8,128)S(1)}, u32[]{:S(2)}, u32[]{:S(2)}) collective-permute-start(f32[16,128,256]{2,1,0:T(8,128)S(1)} %slice_bitcast_fusion), channel_id=1, source_target_pairs={{0,1},{1,0},{2,3},{3,2},{4,5},{5,4},{6,7},{7,6},{8,9},{9,8},{10,11... | collective-permute-start | bytes 6291464 | tf_op jit(solution)/shard_map/ppermute | solution.py:297
  56.7 34.4 %copy-start.3 = (f32[128,256]{1,0:T(8,128)S(1)}, f32[128,256]{1,0:T(8,128)}, u32[]{:S(2)}) copy-start(f32[128,256]{1,0:T(8,128)} %param.16) | copy-start | bytes 393220
  56.7 34.4 %copy-start.4 = (f32[128,256]{1,0:T(8,128)S(1)}, f32[128,256]{1,0:T(8,128)}, u32[]{:S(2)}) copy-start(f32[128,256]{1,0:T(8,128)} %param.15) | copy-start | bytes 393220
  56.7 34.4 %copy-start.5 = (f32[128,256]{1,0:T(8,128)S(1)}, f32[128,256]{1,0:T(8,128)}, u32[]{:S(2)}) copy-start(f32[128,256]{1,0:T(8,128)} %param.14) | copy-start | bytes 393220
  56.8 34.4 %copy-start.6 = (f32[128,256]{1,0:T(8,128)S(1)}, f32[128,256]{1,0:T(8,128)}, u32[]{:S(2)}) copy-start(f32[128,256]{1,0:T(8,128)} %param.17) | copy-start | bytes 393220

commit v15 on v14

--- a/solution.py
+++ b/solution.py
@@ -16,8 +16,8 @@
     return jnp.sign(value) * jnp.log(magnitude + jnp.sqrt(1.0 + magnitude * magnitude))
 
 
-def ring_kernel(n_z, n_pieces, part_ref, out_ref, recv, forward, final, cross,
-                send_sem, recv_sem, cross_sem):
+def ring_kernel(n_z, n_pieces, part_ref, out_ref, recv, forward, final, cross, mate,
+                send_sem, recv_sem, cross_sem, mate_sem):
     row = lax.axis_index("row")
     col = lax.axis_index("col")
     lag = lax.axis_index("lag")
@@ -25,7 +25,7 @@
     y_hi = col % 2
     up = lax.rem(z + 1, n_z)
     down = lax.rem(z + n_z - 1, n_z)
-    rows = part_ref.shape[1] // n_pieces
+    rows = part_ref.shape[2] // n_pieces
     longer = n_z // 2
     shorter = n_z - 1 - longer
 
@@ -35,10 +35,47 @@
     def length(way, side):
         return longer if way == side else shorter
 
+    partner = (row, col, 1 - lag)
     barrier = pltpu.get_barrier_semaphore()
-    for peer in (device(up, y_hi), device(down, y_hi), device(z, 1 - y_hi)):
+    for peer in (device(up, y_hi), device(down, y_hi), device(z, 1 - y_hi), partner):
         pl.semaphore_signal(barrier, inc=1, device_id=peer, device_id_type=MESH)
-    pl.semaphore_wait(barrier, 3)
+    pl.semaphore_wait(barrier, 4)
+
+    def chain_block(step, side, way):
+        chain = length(way, side)
+        if side == 0:
+            target = lax.rem(z + chain - step, n_z)
+        else:
+            target = lax.rem(z + n_z - chain + step, n_z)
+        return target * 2 + way
+
+    order = []
+    for step in range(longer):
+        for side in range(2):
+            for way in range(2):
+                if step < length(way, side):
+                    order.append(chain_block(step, side, way))
+    order += [z * 2 + way for way in range(2)]
+    handed = {}
+    for index, block in enumerate(order):
+        copy = pltpu.make_async_remote_copy(
+            src_ref=part_ref.at[1, block],
+            dst_ref=mate.at[block],
+            send_sem=mate_sem.at[0, index],
+            recv_sem=mate_sem.at[1, index],
+            device_id=partner,
+            device_id_type=MESH,
+        )
+        copy.start()
+        handed[index] = copy
+    ready = set()
+
+    def own(index, span):
+        if index not in ready:
+            handed[index].wait_recv()
+            ready.add(index)
+        block = order[index]
+        return part_ref[0, block, span] + mate[block, span]
 
     copies = {}
     for step in range(longer):
@@ -46,24 +83,22 @@
             span = pl.ds(piece * rows, rows)
             for side in range(2):
                 for way in range(2):
-                    chain = length(way, side)
-                    if step >= chain:
+                    if step >= length(way, side):
                         continue
-                    if side == 0:
-                        target = lax.rem(z + chain - step, n_z)
-                        dest = device(up, y_hi)
-                    else:
-                        target = lax.rem(z + n_z - chain + step, n_z)
-                        dest = device(down, y_hi)
-                    block = target * 2 + way
+                    dest = device(up, y_hi) if side == 0 else device(down, y_hi)
+                    index = len([1 for st in range(step) for sd in range(2) for w in range(2)
+                                 if st < length(w, sd)])
+                    index += len([1 for sd in range(side) for w in range(2)
+                                  if step < length(w, sd)])
+                    index += len([1 for w in range(way) if step < length(w, side)])
                     if step == 0:
-                        source = part_ref.at[block, span]
+                        forward[side, way, step, piece] = own(index, span)
                     else:
                         copies[side, way, step - 1, piece].wait_recv()
                         forward[side, way, step, piece] = (
-                            recv[side, way, step - 1, piece] + part_ref[block, span]
+                            recv[side, way, step - 1, piece] + own(index, span)
                         )
-                        source = forward.at[side, way, step, piece]
+                    source = forward.at[side, way, step, piece]
                     copy = pltpu.make_async_remote_copy(
                         src_ref=source,
                         dst_ref=recv.at[side, way, step, piece],
@@ -79,7 +114,7 @@
     for piece in range(n_pieces):
         span = pl.ds(piece * rows, rows)
         for way in range(2):
-            total = part_ref[z * 2 + way, span]
+            total = own(len(order) - 2 + way, span)
             for side in range(2):
                 last = length(way, side) - 1
                 copies[side, way, last, piece].wait_recv()
@@ -102,10 +137,12 @@
         handoff.wait_send()
     for copy in copies.values():
         copy.wait_send()
+    for copy in handed.values():
+        copy.wait_send()
 
 
 def reduce_scatter(part, n_col, n_pieces=4):
-    group, sims, tile = part.shape
+    _, group, sims, tile = part.shape
     n_z = n_col // 2
     longer = n_z // 2
     rows = sims // n_pieces
@@ -119,9 +156,11 @@
             pltpu.VMEM((2, 2, longer, n_pieces, rows, tile), jnp.float32),
             pltpu.VMEM((2, n_pieces, rows, tile), jnp.float32),
             pltpu.VMEM((n_pieces, rows, tile), jnp.float32),
+            pltpu.VMEM((group, sims, tile), jnp.float32),
             pltpu.SemaphoreType.DMA((2, 2, longer, n_pieces)),
             pltpu.SemaphoreType.DMA((2, 2, longer, n_pieces)),
             pltpu.SemaphoreType.DMA((2, n_pieces)),
+            pltpu.SemaphoreType.DMA((2, group)),
         ],
         compiler_params=pltpu.CompilerParams(
             collective_id=0, has_side_effects=True, vmem_limit_bytes=48 * 1024 * 1024
@@ -293,9 +332,7 @@
     tile_side = kernel_tiles.shape[4]
     parts = stress_parts(gathered, kernel_tiles[0, 0], tile_rows[0, 0],
                          tile_cols[0, 0], tile_count[0, 0], n_col, n_lag)
-    own, other = parts[0], parts[1]
-    from_partner = lax.ppermute(other, "lag", perm=[(0, 1), (1, 0)])
-    stress_change = reduce_scatter(own + from_partner, n_col)
+    stress_change = reduce_scatter(parts, n_col)
     driving = base_stress + stress_change
     factor = jnp.exp(state_var) / 2.0
     velocity = prev_rate

time: 94.3 us -> 89.6 us (0.950)
  waiting for transfers between devices: 3.79 us -> 0 us
  Pallas kernels: 83.9 us -> 86.3 us
  starting transfers between devices: 2.07 us -> 0 us
    ppermute x1 -> x0, waiting for transfers between devices: 3.79 us -> none  [local(): from_partner = lax.ppermute(other, 'lag', perm=[(0, 1), (1, 0)])]
    ppermute x1 -> x0, starting transfers between devices: 2.07 us -> none  [local(): from_partner = lax.ppermute(other, 'lag', perm=[(0, 1), (1, 0)])]
    pallas_call x1, Pallas kernels: 9.35 us -> 11.1 us  [stress_parts(): pl.pallas_call(functools.partial(parts_kernel, n_lag), out_shape=jax.Shap...]
  transfers between devices with their start and end apart: 1 -> 0, of which waited for: 1 -> 0; matrix products, arithmetic and copies ran while one was open for 0% -> 0% of each run, Pallas kernels for 0% -> 0%
where the time goes in v15:
time: 89.6 us; the launch traced here: 89.1 us
  Pallas kernels  86.3 us (96%)
  other arithmetic  1.27 us (1%)
    pallas_call x1, Pallas kernels, all_gather_rows(): pl.pallas_call(functools.partial(gather_kernel, n_x), out_shape=jax.Shape...  40.2 us
    pallas_call x1, Pallas kernels, reduce_scatter(): pl.pallas_call(functools.partial(ring_kernel, n_z, n_pieces), out_shape=j...  35 us
    pallas_call x1, Pallas kernels, stress_parts(): pl.pallas_call(functools.partial(parts_kernel, n_lag), out_shape=jax.Shap...  11.1 us

profile of v15, /device:TPU:1, one launch (start us, length us, event | category | flops | bytes accessed | tf_op | source)
XLA Modules:
  0.0 89.1 jit_solution(4594666269449047046)
XLA Ops:
  0.6 0.0 copy-start.2
  0.6 0.0 copy-start.1
  0.7 0.0 copy-start
  0.7 40.2 %shard_map.104.hist_ref = bf16[8,4,128,512]{3,2,1,0:T(8,128)(2,1)} custom-call(bf16[4,128,512]{2,1,0:T(8,128)(2,1)} %bitcast.10), custom_call_target="tpu_custom_call" | custom-call | tf_op jit(solution)/shard_map/pallas_call | solution.py:257
  40.9 0.0 copy-done.2
  40.9 0.0 copy-done.1
  40.9 0.0 copy-done
  40.9 11.1 %shard_map.105.part_ref = f32[2,16,128,256]{3,2,1,0:T(8,128)S(1)} custom-call(s32[4,12]{1,0:T(4,128)S(1)} %bitcast.6, s32[4,12]{1,0:T(4,128)S(1)} %bitcast.7, s32[4]{0:T(128)S(1)} %bitcast.8, s32[1]{0:T(128)} %bitcast.3.lag_ref, bf16[8,4,128,512]{3,2,1,0:T(8,128)(2,1)} %shard_map.104.hist_ref, bf16[4,12,256,256]{3,2,1,0:T(8,128)(2,1)} %bitcast.9), custom_call_target="tpu_custom_call" | custom-call | tf_op jit(solution)/shard_map/pallas_call | solution.py:309
  52.0 0.0 copy-start.3
  52.1 0.0 copy-start.4
  52.1 0.0 copy-start.5
  52.1 0.0 copy-start.6
  52.1 35.0 %shard_map.106 = f32[128,256]{1,0:T(8,128)S(1)} custom-call(f32[2,16,128,256]{3,2,1,0:T(8,128)S(1)} %shard_map.105.part_ref), custom_call_target="tpu_custom_call" | custom-call | tf_op jit(solution)/shard_map/pallas_call | solution.py:149
  87.1 0.0 copy-done.3
  87.1 0.0 copy-done.4
  87.1 0.0 copy-done.5
  87.1 0.0 copy-done.6
  87.1 1.3 %divide_subtract_fusion = f32[128,256]{1,0:T(8,128)} fusion(f32[128,256]{1,0:T(8,128)S(1)} %copy-done.3, f32[128,256]{1,0:T(8,128)S(1)} %copy-done.4, f32[128,256]{1,0:T(8,128)S(1)} %copy-done.5, f32[128,256]{1,0:T(8,128)S(1)} %shard_map.106, f32[128,256]{1,0:T(8,128)S(1)} %copy-done.6), kind=kLoop, calls=%fused_computation | loop fusion | flops 2064384 | bytes 786432 | tf_op jit(solution)/shard_map/sub | solution.py:343
  88.4 0.7 copy.12
Async XLA Ops:
  0.6 40.3 %copy-start.2 = (s32[1,1,4]{2,1,0:T(1,128)S(1)}, s32[1,1,4]{2,1,0:T(1,128)}, u32[]{:S(2)}) copy-start(s32[1,1,4]{2,1,0:T(1,128)} %param.13) | copy-start | bytes 52
  0.6 40.3 %copy-start.1 = (s32[1,1,4,12]{3,2,1,0:T(4,128)S(1)}, s32[1,1,4,12]{3,2,1,0:T(4,128)}, u32[]{:S(2)}) copy-start(s32[1,1,4,12]{3,2,1,0:T(4,128)} %param.12) | copy-start | bytes 580
  0.7 40.3 %copy-start = (s32[1,1,4,12]{3,2,1,0:T(4,128)S(1)}, s32[1,1,4,12]{3,2,1,0:T(4,128)}, u32[]{:S(2)}) copy-start(s32[1,1,4,12]{3,2,1,0:T(4,128)} %param.11) | copy-start | bytes 580
  52.0 35.0 %copy-start.3 = (f32[128,256]{1,0:T(8,128)S(1)}, f32[128,256]{1,0:T(8,128)}, u32[]{:S(2)}) copy-start(f32[128,256]{1,0:T(8,128)} %param.16) | copy-start | bytes 393220
  52.1 35.0 %copy-start.4 = (f32[128,256]{1,0:T(8,128)S(1)}, f32[128,256]{1,0:T(8,128)}, u32[]{:S(2)}) copy-start(f32[128,256]{1,0:T(8,128)} %param.15) | copy-start | bytes 393220
  52.1 35.0 %copy-start.5 = (f32[128,256]{1,0:T(8,128)S(1)}, f32[128,256]{1,0:T(8,128)}, u32[]{:S(2)}) copy-start(f32[128,256]{1,0:T(8,128)} %param.14) | copy-start | bytes 393220
  52.1 35.0 %copy-start.6 = (f32[128,256]{1,0:T(8,128)S(1)}, f32[128,256]{1,0:T(8,128)}, u32[]{:S(2)}) copy-start(f32[128,256]{1,0:T(8,128)} %param.17) | copy-start | bytes 393220

commit v16 on v15

--- a/solution.py
+++ b/solution.py
@@ -141,7 +141,7 @@
         copy.wait_send()
 
 
-def reduce_scatter(part, n_col, n_pieces=4):
+def reduce_scatter(part, n_col, n_pieces=8):
     _, group, sims, tile = part.shape
     n_z = n_col // 2
     longer = n_z // 2

time: 89.6 us -> 92 us (1.027)
  Pallas kernels: 86.3 us -> 88.3 us
    pallas_call x1, Pallas kernels: 35 us -> 39.3 us  [reduce_scatter(): pl.pallas_call(functools.partial(ring_kernel, n_z, n_pieces), out_shape=j...]
    pallas_call x1, Pallas kernels: 11.1 us -> 8.77 us  [stress_parts(): pl.pallas_call(functools.partial(parts_kernel, n_lag), out_shape=jax.Shap...]
where the time goes in v16:
time: 92 us; the launch traced here: 91.1 us
  Pallas kernels  88.3 us (96%)
  other arithmetic  1.27 us (1%)
    pallas_call x1, Pallas kernels, all_gather_rows(): pl.pallas_call(functools.partial(gather_kernel, n_x), out_shape=jax.Shape...  40.2 us
    pallas_call x1, Pallas kernels, reduce_scatter(): pl.pallas_call(functools.partial(ring_kernel, n_z, n_pieces), out_shape=j...  39.3 us
    pallas_call x1, Pallas kernels, stress_parts(): pl.pallas_call(functools.partial(parts_kernel, n_lag), out_shape=jax.Shap...  8.77 us

profile of v16, /device:TPU:1, one launch (start us, length us, event | category | flops | bytes accessed | tf_op | source)
XLA Modules:
  0.0 91.1 jit_solution(11423159071497911812)
XLA Ops:
  0.6 0.0 copy-start.2
  0.6 0.0 copy-start.1
  0.7 0.0 copy-start
  0.7 40.2 %shard_map.104.hist_ref = bf16[8,4,128,512]{3,2,1,0:T(8,128)(2,1)} custom-call(bf16[4,128,512]{2,1,0:T(8,128)(2,1)} %bitcast.10), custom_call_target="tpu_custom_call" | custom-call | tf_op jit(solution)/shard_map/pallas_call | solution.py:257
  40.9 0.0 copy-done.2
  40.9 0.0 copy-done.1
  40.9 0.0 copy-done
  40.9 8.8 %shard_map.105.part_ref = f32[2,16,128,256]{3,2,1,0:T(8,128)S(1)} custom-call(s32[4,12]{1,0:T(4,128)S(1)} %bitcast.6, s32[4,12]{1,0:T(4,128)S(1)} %bitcast.7, s32[4]{0:T(128)S(1)} %bitcast.8, s32[1]{0:T(128)} %bitcast.3.lag_ref, bf16[8,4,128,512]{3,2,1,0:T(8,128)(2,1)} %shard_map.104.hist_ref, bf16[4,12,256,256]{3,2,1,0:T(8,128)(2,1)} %bitcast.9), custom_call_target="tpu_custom_call" | custom-call | tf_op jit(solution)/shard_map/pallas_call | solution.py:309
  49.7 0.0 copy-start.3
  49.7 0.0 copy-start.4
  49.8 0.0 copy-start.5
  49.8 0.0 copy-start.6
  49.8 39.3 %shard_map.106 = f32[128,256]{1,0:T(8,128)S(1)} custom-call(f32[2,16,128,256]{3,2,1,0:T(8,128)S(1)} %shard_map.105.part_ref), custom_call_target="tpu_custom_call" | custom-call | tf_op jit(solution)/shard_map/pallas_call | solution.py:149
  89.1 0.0 copy-done.3
  89.1 0.0 copy-done.4
  89.1 0.0 copy-done.5
  89.1 0.0 copy-done.6
  89.1 1.3 %divide_subtract_fusion = f32[128,256]{1,0:T(8,128)} fusion(f32[128,256]{1,0:T(8,128)S(1)} %copy-done.3, f32[128,256]{1,0:T(8,128)S(1)} %copy-done.4, f32[128,256]{1,0:T(8,128)S(1)} %copy-done.5, f32[128,256]{1,0:T(8,128)S(1)} %shard_map.106, f32[128,256]{1,0:T(8,128)S(1)} %copy-done.6), kind=kLoop, calls=%fused_computation | loop fusion | flops 2064384 | bytes 786432 | tf_op jit(solution)/shard_map/sub | solution.py:343
  90.4 0.7 copy.12
Async XLA Ops:
  0.6 40.3 %copy-start.2 = (s32[1,1,4]{2,1,0:T(1,128)S(1)}, s32[1,1,4]{2,1,0:T(1,128)}, u32[]{:S(2)}) copy-start(s32[1,1,4]{2,1,0:T(1,128)} %param.13) | copy-start | bytes 52
  0.6 40.3 %copy-start.1 = (s32[1,1,4,12]{3,2,1,0:T(4,128)S(1)}, s32[1,1,4,12]{3,2,1,0:T(4,128)}, u32[]{:S(2)}) copy-start(s32[1,1,4,12]{3,2,1,0:T(4,128)} %param.12) | copy-start | bytes 580
  0.7 40.3 %copy-start = (s32[1,1,4,12]{3,2,1,0:T(4,128)S(1)}, s32[1,1,4,12]{3,2,1,0:T(4,128)}, u32[]{:S(2)}) copy-start(s32[1,1,4,12]{3,2,1,0:T(4,128)} %param.11) | copy-start | bytes 580
  49.7 39.4 %copy-start.3 = (f32[128,256]{1,0:T(8,128)S(1)}, f32[128,256]{1,0:T(8,128)}, u32[]{:S(2)}) copy-start(f32[128,256]{1,0:T(8,128)} %param.16) | copy-start | bytes 393220
  49.7 39.4 %copy-start.4 = (f32[128,256]{1,0:T(8,128)S(1)}, f32[128,256]{1,0:T(8,128)}, u32[]{:S(2)}) copy-start(f32[128,256]{1,0:T(8,128)} %param.15) | copy-start | bytes 393220
  49.8 39.4 %copy-start.5 = (f32[128,256]{1,0:T(8,128)S(1)}, f32[128,256]{1,0:T(8,128)}, u32[]{:S(2)}) copy-start(f32[128,256]{1,0:T(8,128)} %param.14) | copy-start | bytes 393220
  49.8 39.4 %copy-start.6 = (f32[128,256]{1,0:T(8,128)S(1)}, f32[128,256]{1,0:T(8,128)}, u32[]{:S(2)}) copy-start(f32[128,256]{1,0:T(8,128)} %param.17) | copy-start | bytes 393220

commit v17 on v15

--- a/solution.py
+++ b/solution.py
@@ -239,13 +239,13 @@
     arrive(slot(across, x), None)
     send(slot(across, x), None, device(y, right))
     send(slot(across, x), None, device(y, left))
+    for part in range(2):
+        arrive(slot(y, x + 2), part)
+        send(slot(y, x + 2), part, device(across, x))
     arrive(slot(across, left), None)
-    send(slot(across, left), 0, device(y, right))
     arrive(slot(across, right), None)
-    send(slot(across, right), 1, device(y, left))
-    for yy in (y, across):
-        arrive(slot(yy, x + 2), 0)
-        arrive(slot(yy, x + 2), 1)
+    for part in range(2):
+        arrive(slot(across, x + 2), part)
     own.wait()
     for copy in sends:
         copy.wait_send()

time: 89.6 us -> 84.4 us (0.942)
  Pallas kernels: 86.3 us -> 81.5 us
    pallas_call x1, Pallas kernels: 40.2 us -> 34.6 us  [all_gather_rows(): pl.pallas_call(functools.partial(gather_kernel, n_x), out_shape=jax.Shape...]
    pallas_call x1, Pallas kernels: 35 us -> 37.3 us  [reduce_scatter(): pl.pallas_call(functools.partial(ring_kernel, n_z, n_pieces), out_shape=j...]
    pallas_call x1, Pallas kernels: 11.1 us -> 9.54 us  [stress_parts(): pl.pallas_call(functools.partial(parts_kernel, n_lag), out_shape=jax.Shap...]
where the time goes in v17:
time: 84.4 us; the launch traced here: 84.2 us
  Pallas kernels  81.5 us (97%)
  other arithmetic  1.27 us (2%)
    pallas_call x1, Pallas kernels, reduce_scatter(): pl.pallas_call(functools.partial(ring_kernel, n_z, n_pieces), out_shape=j...  37.3 us
    pallas_call x1, Pallas kernels, all_gather_rows(): pl.pallas_call(functools.partial(gather_kernel, n_x), out_shape=jax.Shape...  34.6 us
    pallas_call x1, Pallas kernels, stress_parts(): pl.pallas_call(functools.partial(parts_kernel, n_lag), out_shape=jax.Shap...  9.54 us

profile of v17, /device:TPU:1, one launch (start us, length us, event | category | flops | bytes accessed | tf_op | source)
XLA Modules:
  0.0 84.2 jit_solution(12710267488359892843)
XLA Ops:
  0.6 0.0 copy-start.2
  0.6 0.0 copy-start.1
  0.7 0.0 copy-start
  0.7 34.6 %shard_map.104.hist_ref = bf16[8,4,128,512]{3,2,1,0:T(8,128)(2,1)} custom-call(bf16[4,128,512]{2,1,0:T(8,128)(2,1)} %bitcast.10), custom_call_target="tpu_custom_call" | custom-call | tf_op jit(solution)/shard_map/pallas_call | solution.py:257
  35.3 0.0 copy-done.2
  35.3 0.0 copy-done.1
  35.3 0.0 copy-done
  35.3 9.5 %shard_map.105.part_ref = f32[2,16,128,256]{3,2,1,0:T(8,128)S(1)} custom-call(s32[4,12]{1,0:T(4,128)S(1)} %bitcast.6, s32[4,12]{1,0:T(4,128)S(1)} %bitcast.7, s32[4]{0:T(128)S(1)} %bitcast.8, s32[1]{0:T(128)} %bitcast.3.lag_ref, bf16[8,4,128,512]{3,2,1,0:T(8,128)(2,1)} %shard_map.104.hist_ref, bf16[4,12,256,256]{3,2,1,0:T(8,128)(2,1)} %bitcast.9), custom_call_target="tpu_custom_call" | custom-call | tf_op jit(solution)/shard_map/pallas_call | solution.py:309
  44.9 0.0 copy-start.3
  44.9 0.0 copy-start.4
  44.9 0.0 copy-start.5
  44.9 0.0 copy-start.6
  44.9 37.3 %shard_map.106 = f32[128,256]{1,0:T(8,128)S(1)} custom-call(f32[2,16,128,256]{3,2,1,0:T(8,128)S(1)} %shard_map.105.part_ref), custom_call_target="tpu_custom_call" | custom-call | tf_op jit(solution)/shard_map/pallas_call | solution.py:149
  82.2 0.0 copy-done.3
  82.2 0.0 copy-done.4
  82.2 0.0 copy-done.5
  82.3 0.0 copy-done.6
  82.3 1.3 %divide_subtract_fusion = f32[128,256]{1,0:T(8,128)} fusion(f32[128,256]{1,0:T(8,128)S(1)} %copy-done.3, f32[128,256]{1,0:T(8,128)S(1)} %copy-done.4, f32[128,256]{1,0:T(8,128)S(1)} %copy-done.5, f32[128,256]{1,0:T(8,128)S(1)} %shard_map.106, f32[128,256]{1,0:T(8,128)S(1)} %copy-done.6), kind=kLoop, calls=%fused_computation | loop fusion | flops 2064384 | bytes 786432 | tf_op jit(solution)/shard_map/sub | solution.py:343
  83.5 0.7 copy.12
Async XLA Ops:
  0.6 34.7 %copy-start.2 = (s32[1,1,4]{2,1,0:T(1,128)S(1)}, s32[1,1,4]{2,1,0:T(1,128)}, u32[]{:S(2)}) copy-start(s32[1,1,4]{2,1,0:T(1,128)} %param.13) | copy-start | bytes 52
  0.6 34.7 %copy-start.1 = (s32[1,1,4,12]{3,2,1,0:T(4,128)S(1)}, s32[1,1,4,12]{3,2,1,0:T(4,128)}, u32[]{:S(2)}) copy-start(s32[1,1,4,12]{3,2,1,0:T(4,128)} %param.12) | copy-start | bytes 580
  0.7 34.7 %copy-start = (s32[1,1,4,12]{3,2,1,0:T(4,128)S(1)}, s32[1,1,4,12]{3,2,1,0:T(4,128)}, u32[]{:S(2)}) copy-start(s32[1,1,4,12]{3,2,1,0:T(4,128)} %param.11) | copy-start | bytes 580
  44.9 37.4 %copy-start.3 = (f32[128,256]{1,0:T(8,128)S(1)}, f32[128,256]{1,0:T(8,128)}, u32[]{:S(2)}) copy-start(f32[128,256]{1,0:T(8,128)} %param.16) | copy-start | bytes 393220
  44.9 37.4 %copy-start.4 = (f32[128,256]{1,0:T(8,128)S(1)}, f32[128,256]{1,0:T(8,128)}, u32[]{:S(2)}) copy-start(f32[128,256]{1,0:T(8,128)} %param.15) | copy-start | bytes 393220
  44.9 37.4 %copy-start.5 = (f32[128,256]{1,0:T(8,128)S(1)}, f32[128,256]{1,0:T(8,128)}, u32[]{:S(2)}) copy-start(f32[128,256]{1,0:T(8,128)} %param.14) | copy-start | bytes 393220
  44.9 37.4 %copy-start.6 = (f32[128,256]{1,0:T(8,128)S(1)}, f32[128,256]{1,0:T(8,128)}, u32[]{:S(2)}) copy-start(f32[128,256]{1,0:T(8,128)} %param.17) | copy-start | bytes 393220

commit v18 on v17

--- a/solution.py
+++ b/solution.py
@@ -229,9 +229,9 @@
             device_id_type=MESH,
         ).wait_recv()
 
+    send(mine, None, device(across, x), from_input=True)
     send(mine, None, device(y, right), from_input=True)
     send(mine, None, device(y, left), from_input=True)
-    send(mine, None, device(across, x), from_input=True)
     arrive(slot(y, left), None)
     send(slot(y, left), 0, device(y, right))
     arrive(slot(y, right), None)

time: 84.4 us -> 84.9 us (level)
    pallas_call x1, Pallas kernels: 37.3 us -> 38.5 us  [reduce_scatter(): pl.pallas_call(functools.partial(ring_kernel, n_z, n_pieces), out_shape=j...]
where the time goes in v18:
time: 84.9 us; the launch traced here: 84.8 us
  Pallas kernels  82 us (97%)
  other arithmetic  1.27 us (1%)
    pallas_call x1, Pallas kernels, reduce_scatter(): pl.pallas_call(functools.partial(ring_kernel, n_z, n_pieces), out_shape=j...  38.5 us
    pallas_call x1, Pallas kernels, all_gather_rows(): pl.pallas_call(functools.partial(gather_kernel, n_x), out_shape=jax.Shape...  34.6 us
    pallas_call x1, Pallas kernels, stress_parts(): pl.pallas_call(functools.partial(parts_kernel, n_lag), out_shape=jax.Shap...  8.95 us

profile of v18, /device:TPU:1, one launch (start us, length us, event | category | flops | bytes accessed | tf_op | source)
XLA Modules:
  0.0 84.8 jit_solution(13276117950914239874)
XLA Ops:
  0.6 0.0 copy-start.2
  0.6 0.0 copy-start.1
  0.7 0.0 copy-start
  0.7 34.6 %shard_map.104.hist_ref = bf16[8,4,128,512]{3,2,1,0:T(8,128)(2,1)} custom-call(bf16[4,128,512]{2,1,0:T(8,128)(2,1)} %bitcast.10), custom_call_target="tpu_custom_call" | custom-call | tf_op jit(solution)/shard_map/pallas_call | solution.py:257
  35.3 0.0 copy-done.2
  35.3 0.0 copy-done.1
  35.3 0.0 copy-done
  35.3 8.9 %shard_map.105.part_ref = f32[2,16,128,256]{3,2,1,0:T(8,128)S(1)} custom-call(s32[4,12]{1,0:T(4,128)S(1)} %bitcast.6, s32[4,12]{1,0:T(4,128)S(1)} %bitcast.7, s32[4]{0:T(128)S(1)} %bitcast.8, s32[1]{0:T(128)} %bitcast.3.lag_ref, bf16[8,4,128,512]{3,2,1,0:T(8,128)(2,1)} %shard_map.104.hist_ref, bf16[4,12,256,256]{3,2,1,0:T(8,128)(2,1)} %bitcast.9), custom_call_target="tpu_custom_call" | custom-call | tf_op jit(solution)/shard_map/pallas_call | solution.py:309
  44.3 0.0 copy-start.3
  44.3 0.0 copy-start.4
  44.3 0.0 copy-start.5
  44.3 0.0 copy-start.6
  44.3 38.5 %shard_map.106 = f32[128,256]{1,0:T(8,128)S(1)} custom-call(f32[2,16,128,256]{3,2,1,0:T(8,128)S(1)} %shard_map.105.part_ref), custom_call_target="tpu_custom_call" | custom-call | tf_op jit(solution)/shard_map/pallas_call | solution.py:149
  82.8 0.0 copy-done.3
  82.8 0.0 copy-done.4
  82.8 0.0 copy-done.5
  82.8 0.0 copy-done.6
  82.8 1.3 %divide_subtract_fusion = f32[128,256]{1,0:T(8,128)} fusion(f32[128,256]{1,0:T(8,128)S(1)} %copy-done.3, f32[128,256]{1,0:T(8,128)S(1)} %copy-done.4, f32[128,256]{1,0:T(8,128)S(1)} %copy-done.5, f32[128,256]{1,0:T(8,128)S(1)} %shard_map.106, f32[128,256]{1,0:T(8,128)S(1)} %copy-done.6), kind=kLoop, calls=%fused_computation | loop fusion | flops 2064384 | bytes 786432 | tf_op jit(solution)/shard_map/sub | solution.py:343
  84.1 0.7 copy.12
Async XLA Ops:
  0.6 34.7 %copy-start.2 = (s32[1,1,4]{2,1,0:T(1,128)S(1)}, s32[1,1,4]{2,1,0:T(1,128)}, u32[]{:S(2)}) copy-start(s32[1,1,4]{2,1,0:T(1,128)} %param.13) | copy-start | bytes 52
  0.6 34.7 %copy-start.1 = (s32[1,1,4,12]{3,2,1,0:T(4,128)S(1)}, s32[1,1,4,12]{3,2,1,0:T(4,128)}, u32[]{:S(2)}) copy-start(s32[1,1,4,12]{3,2,1,0:T(4,128)} %param.12) | copy-start | bytes 580
  0.7 34.7 %copy-start = (s32[1,1,4,12]{3,2,1,0:T(4,128)S(1)}, s32[1,1,4,12]{3,2,1,0:T(4,128)}, u32[]{:S(2)}) copy-start(s32[1,1,4,12]{3,2,1,0:T(4,128)} %param.11) | copy-start | bytes 580
  44.3 38.5 %copy-start.3 = (f32[128,256]{1,0:T(8,128)S(1)}, f32[128,256]{1,0:T(8,128)}, u32[]{:S(2)}) copy-start(f32[128,256]{1,0:T(8,128)} %param.16) | copy-start | bytes 393220
  44.3 38.5 %copy-start.4 = (f32[128,256]{1,0:T(8,128)S(1)}, f32[128,256]{1,0:T(8,128)}, u32[]{:S(2)}) copy-start(f32[128,256]{1,0:T(8,128)} %param.15) | copy-start | bytes 393220
  44.3 38.5 %copy-start.5 = (f32[128,256]{1,0:T(8,128)S(1)}, f32[128,256]{1,0:T(8,128)}, u32[]{:S(2)}) copy-start(f32[128,256]{1,0:T(8,128)} %param.14) | copy-start | bytes 393220
  44.3 38.5 %copy-start.6 = (f32[128,256]{1,0:T(8,128)S(1)}, f32[128,256]{1,0:T(8,128)}, u32[]{:S(2)}) copy-start(f32[128,256]{1,0:T(8,128)} %param.17) | copy-start | bytes 393220

commit v19 on v18

--- a/solution.py
+++ b/solution.py
@@ -17,7 +17,7 @@
 
 
 def ring_kernel(n_z, n_pieces, part_ref, out_ref, recv, forward, final, cross, mate,
-                send_sem, recv_sem, cross_sem, mate_sem):
+                own_buf, send_sem, recv_sem, cross_sem, mate_sem, own_sem):
     row = lax.axis_index("row")
     col = lax.axis_index("col")
     lag = lax.axis_index("lag")
@@ -36,6 +36,8 @@
         return longer if way == side else shorter
 
     partner = (row, col, 1 - lag)
+    own_copy = pltpu.make_async_copy(part_ref.at[0], own_buf, own_sem)
+    own_copy.start()
     barrier = pltpu.get_barrier_semaphore()
     for peer in (device(up, y_hi), device(down, y_hi), device(z, 1 - y_hi), partner):
         pl.semaphore_signal(barrier, inc=1, device_id=peer, device_id_type=MESH)
@@ -71,11 +73,13 @@
     ready = set()
 
     def own(index, span):
+        if not ready:
+            own_copy.wait()
         if index not in ready:
             handed[index].wait_recv()
             ready.add(index)
         block = order[index]
-        return part_ref[0, block, span] + mate[block, span]
+        return own_buf[block, span] + mate[block, span]
 
     copies = {}
     for step in range(longer):
@@ -149,7 +153,7 @@
     return pl.pallas_call(
         functools.partial(ring_kernel, n_z, n_pieces),
         out_shape=jax.ShapeDtypeStruct((sims, tile), jnp.float32),
-        in_specs=[pl.BlockSpec(memory_space=pltpu.VMEM)],
+        in_specs=[pl.BlockSpec(memory_space=pl.ANY)],
         out_specs=pl.BlockSpec(memory_space=pltpu.VMEM),
         scratch_shapes=[
             pltpu.VMEM((2, 2, longer, n_pieces, rows, tile), jnp.float32),
@@ -157,10 +161,12 @@
             pltpu.VMEM((2, n_pieces, rows, tile), jnp.float32),
             pltpu.VMEM((n_pieces, rows, tile), jnp.float32),
             pltpu.VMEM((group, sims, tile), jnp.float32),
+            pltpu.VMEM((group, sims, tile), jnp.float32),
             pltpu.SemaphoreType.DMA((2, 2, longer, n_pieces)),
             pltpu.SemaphoreType.DMA((2, 2, longer, n_pieces)),
             pltpu.SemaphoreType.DMA((2, n_pieces)),
             pltpu.SemaphoreType.DMA((2, group)),
+            pltpu.SemaphoreType.DMA(()),
         ],
         compiler_params=pltpu.CompilerParams(
             collective_id=0, has_side_effects=True, vmem_limit_bytes=48 * 1024 * 1024

time: 84.9 us -> 84.4 us (level)
    pallas_call x1, Pallas kernels: 38.5 us -> 36.8 us  [reduce_scatter(): pl.pallas_call(functools.partial(ring_kernel, n_z, n_pieces), out_shape=j...]
    pallas_call x1, Pallas kernels: 8.95 us -> 10.1 us  [stress_parts(): pl.pallas_call(functools.partial(parts_kernel, n_lag), out_shape=jax.Shap...]
where the time goes in v19:
time: 84.4 us; the launch traced here: 84.3 us
  Pallas kernels  81.5 us (97%)
  other arithmetic  1.27 us (2%)
    pallas_call x1, Pallas kernels, reduce_scatter(): pl.pallas_call(functools.partial(ring_kernel, n_z, n_pieces), out_shape=j...  36.8 us
    pallas_call x1, Pallas kernels, all_gather_rows(): pl.pallas_call(functools.partial(gather_kernel, n_x), out_shape=jax.Shape...  34.6 us
    pallas_call x1, Pallas kernels, stress_parts(): pl.pallas_call(functools.partial(parts_kernel, n_lag), out_shape=jax.Shap...  10.1 us

profile of v19, /device:TPU:1, one launch (start us, length us, event | category | flops | bytes accessed | tf_op | source)
XLA Modules:
  0.0 84.3 jit_solution(9130115494898121477)
XLA Ops:
  0.6 0.0 copy-start.2
  0.6 0.0 copy-start.1
  0.7 0.0 copy-start
  0.7 34.6 %shard_map.104.hist_ref = bf16[8,4,128,512]{3,2,1,0:T(8,128)(2,1)} custom-call(bf16[4,128,512]{2,1,0:T(8,128)(2,1)} %bitcast.10), custom_call_target="tpu_custom_call" | custom-call | tf_op jit(solution)/shard_map/pallas_call | solution.py:263
  35.3 0.0 copy-done.2
  35.3 0.0 copy-done.1
  35.3 0.0 copy-done
  35.3 10.1 %shard_map.105.part_ref = f32[2,16,128,256]{3,2,1,0:T(8,128)S(1)} custom-call(s32[4,12]{1,0:T(4,128)S(1)} %bitcast.6, s32[4,12]{1,0:T(4,128)S(1)} %bitcast.7, s32[4]{0:T(128)S(1)} %bitcast.8, s32[1]{0:T(128)} %bitcast.3.lag_ref, bf16[8,4,128,512]{3,2,1,0:T(8,128)(2,1)} %shard_map.104.hist_ref, bf16[4,12,256,256]{3,2,1,0:T(8,128)(2,1)} %bitcast.9), custom_call_target="tpu_custom_call" | custom-call | tf_op jit(solution)/shard_map/pallas_call | solution.py:315
  45.4 0.0 copy-start.3
  45.5 0.0 copy-start.4
  45.5 0.0 copy-start.5
  45.5 0.0 copy-start.6
  45.5 36.8 %shard_map.106 = f32[128,256]{1,0:T(8,128)S(1)} custom-call(f32[2,16,128,256]{3,2,1,0:T(8,128)S(1)} %shard_map.105.part_ref), custom_call_target="tpu_custom_call" | custom-call | tf_op jit(solution)/shard_map/pallas_call | solution.py:153
  82.3 0.0 copy-done.3
  82.3 0.0 copy-done.4
  82.3 0.0 copy-done.5
  82.3 0.0 copy-done.6
  82.3 1.3 %divide_subtract_fusion = f32[128,256]{1,0:T(8,128)} fusion(f32[128,256]{1,0:T(8,128)S(1)} %copy-done.3, f32[128,256]{1,0:T(8,128)S(1)} %copy-done.4, f32[128,256]{1,0:T(8,128)S(1)} %copy-done.5, f32[128,256]{1,0:T(8,128)S(1)} %shard_map.106, f32[128,256]{1,0:T(8,128)S(1)} %copy-done.6), kind=kLoop, calls=%fused_computation | loop fusion | flops 2064384 | bytes 786432 | tf_op jit(solution)/shard_map/sub | solution.py:349
  83.6 0.7 copy.12
Async XLA Ops:
  0.6 34.7 %copy-start.2 = (s32[1,1,4]{2,1,0:T(1,128)S(1)}, s32[1,1,4]{2,1,0:T(1,128)}, u32[]{:S(2)}) copy-start(s32[1,1,4]{2,1,0:T(1,128)} %param.13) | copy-start | bytes 52
  0.6 34.7 %copy-start.1 = (s32[1,1,4,12]{3,2,1,0:T(4,128)S(1)}, s32[1,1,4,12]{3,2,1,0:T(4,128)}, u32[]{:S(2)}) copy-start(s32[1,1,4,12]{3,2,1,0:T(4,128)} %param.12) | copy-start | bytes 580
  0.7 34.7 %copy-start = (s32[1,1,4,12]{3,2,1,0:T(4,128)S(1)}, s32[1,1,4,12]{3,2,1,0:T(4,128)}, u32[]{:S(2)}) copy-start(s32[1,1,4,12]{3,2,1,0:T(4,128)} %param.11) | copy-start | bytes 580
  45.4 36.9 %copy-start.3 = (f32[128,256]{1,0:T(8,128)S(1)}, f32[128,256]{1,0:T(8,128)}, u32[]{:S(2)}) copy-start(f32[128,256]{1,0:T(8,128)} %param.16) | copy-start | bytes 393220
  45.5 36.9 %copy-start.4 = (f32[128,256]{1,0:T(8,128)S(1)}, f32[128,256]{1,0:T(8,128)}, u32[]{:S(2)}) copy-start(f32[128,256]{1,0:T(8,128)} %param.15) | copy-start | bytes 393220
  45.5 36.9 %copy-start.5 = (f32[128,256]{1,0:T(8,128)S(1)}, f32[128,256]{1,0:T(8,128)}, u32[]{:S(2)}) copy-start(f32[128,256]{1,0:T(8,128)} %param.14) | copy-start | bytes 393220
  45.5 36.9 %copy-start.6 = (f32[128,256]{1,0:T(8,128)S(1)}, f32[128,256]{1,0:T(8,128)}, u32[]{:S(2)}) copy-start(f32[128,256]{1,0:T(8,128)} %param.17) | copy-start | bytes 393220

commit v20 on v18

--- a/solution.py
+++ b/solution.py
@@ -16,7 +16,7 @@
     return jnp.sign(value) * jnp.log(magnitude + jnp.sqrt(1.0 + magnitude * magnitude))
 
 
-def ring_kernel(n_z, n_pieces, part_ref, out_ref, recv, forward, final, cross, mate,
+def ring_kernel(n_z, n_pieces, part_ref, out_ref, cross_ref, recv, forward, final, cross, mate,
                 send_sem, recv_sem, cross_sem, mate_sem):
     row = lax.axis_index("row")
     col = lax.axis_index("col")
@@ -132,7 +132,8 @@
         handoffs.append(handoff)
     for piece in range(n_pieces):
         handoffs[piece].wait_recv()
-        out_ref[pl.ds(piece * rows, rows), :] = final[y_hi, piece] + cross[piece]
+        out_ref[pl.ds(piece * rows, rows), :] = final[y_hi, piece]
+        cross_ref[pl.ds(piece * rows, rows), :] = cross[piece]
     for handoff in handoffs:
         handoff.wait_send()
     for copy in copies.values():
@@ -148,9 +149,9 @@
     rows = sims // n_pieces
     return pl.pallas_call(
         functools.partial(ring_kernel, n_z, n_pieces),
-        out_shape=jax.ShapeDtypeStruct((sims, tile), jnp.float32),
+        out_shape=[jax.ShapeDtypeStruct((sims, tile), jnp.float32)] * 2,
         in_specs=[pl.BlockSpec(memory_space=pltpu.VMEM)],
-        out_specs=pl.BlockSpec(memory_space=pltpu.VMEM),
+        out_specs=[pl.BlockSpec(memory_space=pltpu.VMEM)] * 2,
         scratch_shapes=[
             pltpu.VMEM((2, 2, longer, n_pieces, rows, tile), jnp.float32),
             pltpu.VMEM((2, 2, longer, n_pieces, rows, tile), jnp.float32),
@@ -332,7 +333,8 @@
     tile_side = kernel_tiles.shape[4]
     parts = stress_parts(gathered, kernel_tiles[0, 0], tile_rows[0, 0],
                          tile_cols[0, 0], tile_count[0, 0], n_col, n_lag)
-    stress_change = reduce_scatter(parts, n_col)
+    held, handed_over = reduce_scatter(parts, n_col)
+    stress_change = held + handed_over
     driving = base_stress + stress_change
     factor = jnp.exp(state_var) / 2.0
     velocity = prev_rate

time: 84.9 us -> 84.7 us (level)
  no operation moved by 1% of the time
where the time goes in v20:
time: 84.7 us; the launch traced here: 84.5 us
  Pallas kernels  82.4 us (97%)
  other arithmetic  1.28 us (2%)
    pallas_call x1, Pallas kernels, reduce_scatter(): pl.pallas_call(functools.partial(ring_kernel, n_z, n_pieces), out_shape=[...  38.7 us
    pallas_call x1, Pallas kernels, all_gather_rows(): pl.pallas_call(functools.partial(gather_kernel, n_x), out_shape=jax.Shape...  34.6 us
    pallas_call x1, Pallas kernels, stress_parts(): pl.pallas_call(functools.partial(parts_kernel, n_lag), out_shape=jax.Shap...  9.15 us

profile of v20, /device:TPU:1, one launch (start us, length us, event | category | flops | bytes accessed | tf_op | source)
XLA Modules:
  0.0 84.5 jit_solution(13693019718178676367)
XLA Ops:
  0.6 0.0 copy-start.2
  0.6 0.0 copy-start.1
  0.7 0.0 copy-start
  0.7 34.6 %shard_map.104.hist_ref = bf16[8,4,128,512]{3,2,1,0:T(8,128)(2,1)} custom-call(bf16[4,128,512]{2,1,0:T(8,128)(2,1)} %bitcast.10), custom_call_target="tpu_custom_call" | custom-call | tf_op jit(solution)/shard_map/pallas_call | solution.py:258
  35.3 0.0 copy-done.2
  35.3 0.0 copy-done.1
  35.3 0.0 copy-done
  35.3 9.1 %shard_map.105.part_ref = f32[2,16,128,256]{3,2,1,0:T(8,128)S(1)} custom-call(s32[4,12]{1,0:T(4,128)S(1)} %bitcast.6, s32[4,12]{1,0:T(4,128)S(1)} %bitcast.7, s32[4]{0:T(128)S(1)} %bitcast.8, s32[1]{0:T(128)} %bitcast.3.lag_ref, bf16[8,4,128,512]{3,2,1,0:T(8,128)(2,1)} %shard_map.104.hist_ref, bf16[4,12,256,256]{3,2,1,0:T(8,128)(2,1)} %bitcast.9), custom_call_target="tpu_custom_call" | custom-call | tf_op jit(solution)/shard_map/pallas_call | solution.py:310
  44.5 0.0 copy-start.3
  44.5 0.0 copy-start.4
  44.5 0.0 copy-start.5
  44.5 0.0 copy-start.6
  44.5 38.7 %shard_map.106 = (f32[128,256]{1,0:T(8,128)S(1)}, f32[128,256]{1,0:T(8,128)S(1)}) custom-call(f32[2,16,128,256]{3,2,1,0:T(8,128)S(1)} %shard_map.105.part_ref), custom_call_target="tpu_custom_call" | custom-call | tf_op jit(solution)/shard_map/pallas_call | solution.py:150
  83.2 0.0 copy-done.3
  83.2 0.0 copy-done.4
  83.2 0.0 copy-done.5
  83.2 0.0 copy-done.6
  83.2 1.3 %divide_subtract_fusion = (f32[128,256]{1,0:T(8,128)}, f32[128,256]{1,0:T(8,128)}) fusion(f32[128,256]{1,0:T(8,128)S(1)} %copy-done.3, f32[128,256]{1,0:T(8,128)S(1)} %copy-done.4, f32[128,256]{1,0:T(8,128)S(1)} %copy-done.5, f32[128,256]{1,0:T(8,128)S(1)} %copy-done.6, f32[128,256]{1,0:T(8,128)S(1)} %get-tuple-element.4, f32[128,256]{1,0:T(8,128)S(1)} %get-tuple-element.5), kind=kLoop, calls=%fused_computation | loop fusion | flops 2097152 | bytes 1048576 | tf_op jit(solution)/shard_map/sub | solution.py:345
Async XLA Ops:
  0.6 34.7 %copy-start.2 = (s32[1,1,4]{2,1,0:T(1,128)S(1)}, s32[1,1,4]{2,1,0:T(1,128)}, u32[]{:S(2)}) copy-start(s32[1,1,4]{2,1,0:T(1,128)} %param.13) | copy-start | bytes 52
  0.6 34.7 %copy-start.1 = (s32[1,1,4,12]{3,2,1,0:T(4,128)S(1)}, s32[1,1,4,12]{3,2,1,0:T(4,128)}, u32[]{:S(2)}) copy-start(s32[1,1,4,12]{3,2,1,0:T(4,128)} %param.12) | copy-start | bytes 580
  0.7 34.7 %copy-start = (s32[1,1,4,12]{3,2,1,0:T(4,128)S(1)}, s32[1,1,4,12]{3,2,1,0:T(4,128)}, u32[]{:S(2)}) copy-start(s32[1,1,4,12]{3,2,1,0:T(4,128)} %param.11) | copy-start | bytes 580
  44.5 38.7 %copy-start.3 = (f32[128,256]{1,0:T(8,128)S(1)}, f32[128,256]{1,0:T(8,128)}, u32[]{:S(2)}) copy-start(f32[128,256]{1,0:T(8,128)} %param.16) | copy-start | bytes 393220
  44.5 38.7 %copy-start.4 = (f32[128,256]{1,0:T(8,128)S(1)}, f32[128,256]{1,0:T(8,128)}, u32[]{:S(2)}) copy-start(f32[128,256]{1,0:T(8,128)} %param.15) | copy-start | bytes 393220
  44.5 38.7 %copy-start.5 = (f32[128,256]{1,0:T(8,128)S(1)}, f32[128,256]{1,0:T(8,128)}, u32[]{:S(2)}) copy-start(f32[128,256]{1,0:T(8,128)} %param.14) | copy-start | bytes 393220
  44.5 38.7 %copy-start.6 = (f32[128,256]{1,0:T(8,128)S(1)}, f32[128,256]{1,0:T(8,128)}, u32[]{:S(2)}) copy-start(f32[128,256]{1,0:T(8,128)} %param.17) | copy-start | bytes 393220

commit v21 on v18

--- a/solution.py
+++ b/solution.py
@@ -185,10 +185,21 @@
     def device(yy, xx):
         return (slot(yy, xx), col, lag)
 
+    few = 16
+    sims = piece_ref.shape[1]
+
+    def span(part):
+        if part is None:
+            return (slice(None),)
+        if part < 2:
+            return (pl.ds(part * half, half),)
+        if part == 2:
+            return (slice(None), pl.ds(0, few))
+        return (slice(None), pl.ds(few, sims - few))
+
     def region(index, part):
-        if part is None:
-            return out_ref.at[index], recv_sem.at[index, 0]
-        return out_ref.at[index, pl.ds(part * half, half)], recv_sem.at[index, part]
+        sem = recv_sem.at[index, 0 if part is None else part]
+        return out_ref.at[(index,) + span(part)], sem
 
     barrier = pltpu.get_barrier_semaphore()
     for peer in (device(y, right), device(y, left), device(across, x)):
@@ -219,7 +230,7 @@
 
     def arrive(index, part):
         target, sem = region(index, part)
-        source = piece_ref if part is None else piece_ref.at[pl.ds(part * half, half)]
+        source = piece_ref.at[span(part)]
         pltpu.make_async_remote_copy(
             src_ref=source,
             dst_ref=target,
@@ -234,16 +245,19 @@
     send(mine, None, device(y, left), from_input=True)
     arrive(slot(y, left), None)
     send(slot(y, left), 0, device(y, right))
+    send(slot(y, left), 2, device(across, x))
     arrive(slot(y, right), None)
     send(slot(y, right), 1, device(y, left))
+    send(slot(y, right), 2, device(across, x))
     arrive(slot(across, x), None)
-    send(slot(across, x), None, device(y, right))
-    send(slot(across, x), None, device(y, left))
+    send(slot(across, x), 3, device(y, right))
+    send(slot(across, x), 3, device(y, left))
     for part in range(2):
         arrive(slot(y, x + 2), part)
         send(slot(y, x + 2), part, device(across, x))
-    arrive(slot(across, left), None)
-    arrive(slot(across, right), None)
+    for part in (2, 3):
+        arrive(slot(across, left), part)
+        arrive(slot(across, right), part)
     for part in range(2):
         arrive(slot(across, x + 2), part)
     own.wait()
@@ -261,8 +275,8 @@
         out_specs=pl.BlockSpec(memory_space=pl.ANY),
         scratch_shapes=[
             pltpu.SemaphoreType.DMA(()),
-            pltpu.SemaphoreType.DMA((9,)),
-            pltpu.SemaphoreType.DMA((n_row, 2)),
+            pltpu.SemaphoreType.DMA((11,)),
+            pltpu.SemaphoreType.DMA((n_row, 4)),
         ],
         compiler_params=pltpu.CompilerParams(collective_id=1, has_side_effects=True),
     )(piece)

time: 84.9 us -> 84.5 us (level)
    pallas_call x1, Pallas kernels: 34.6 us -> 33.4 us  [all_gather_rows(): pl.pallas_call(functools.partial(gather_kernel, n_x), out_shape=jax.Shape...]
where the time goes in v21:
time: 84.5 us; the launch traced here: 84.4 us
  Pallas kernels  81.6 us (97%)
  other arithmetic  1.27 us (2%)
    pallas_call x1, Pallas kernels, reduce_scatter(): pl.pallas_call(functools.partial(ring_kernel, n_z, n_pieces), out_shape=j...  38.5 us
    pallas_call x1, Pallas kernels, all_gather_rows(): pl.pallas_call(functools.partial(gather_kernel, n_x), out_shape=jax.Shape...  33.4 us
    pallas_call x1, Pallas kernels, stress_parts(): pl.pallas_call(functools.partial(parts_kernel, n_lag), out_shape=jax.Shap...  9.72 us

profile of v21, /device:TPU:1, one launch (start us, length us, event | category | flops | bytes accessed | tf_op | source)
XLA Modules:
  0.0 84.4 jit_solution(2675205965445697204)
XLA Ops:
  0.6 0.0 copy-start.2
  0.6 0.0 copy-start.1
  0.7 0.0 copy-start
  0.7 33.4 %shard_map.104.hist_ref = bf16[8,4,128,512]{3,2,1,0:T(8,128)(2,1)} custom-call(bf16[4,128,512]{2,1,0:T(8,128)(2,1)} %bitcast.10), custom_call_target="tpu_custom_call" | custom-call | tf_op jit(solution)/shard_map/pallas_call | solution.py:271
  34.0 0.0 copy-done.2
  34.1 0.0 copy-done.1
  34.1 0.0 copy-done
  34.1 9.7 %shard_map.105.part_ref = f32[2,16,128,256]{3,2,1,0:T(8,128)S(1)} custom-call(s32[4,12]{1,0:T(4,128)S(1)} %bitcast.6, s32[4,12]{1,0:T(4,128)S(1)} %bitcast.7, s32[4]{0:T(128)S(1)} %bitcast.8, s32[1]{0:T(128)} %bitcast.3.lag_ref, bf16[8,4,128,512]{3,2,1,0:T(8,128)(2,1)} %shard_map.104.hist_ref, bf16[4,12,256,256]{3,2,1,0:T(8,128)(2,1)} %bitcast.9), custom_call_target="tpu_custom_call" | custom-call | tf_op jit(solution)/shard_map/pallas_call | solution.py:323
  43.8 0.0 copy-start.3
  43.8 0.0 copy-start.4
  43.8 0.0 copy-start.5
  43.8 0.0 copy-start.6
  43.9 38.5 %shard_map.106 = f32[128,256]{1,0:T(8,128)S(1)} custom-call(f32[2,16,128,256]{3,2,1,0:T(8,128)S(1)} %shard_map.105.part_ref), custom_call_target="tpu_custom_call" | custom-call | tf_op jit(solution)/shard_map/pallas_call | solution.py:149
  82.4 0.0 copy-done.3
  82.4 0.0 copy-done.4
  82.4 0.0 copy-done.5
  82.4 0.0 copy-done.6
  82.4 1.3 %divide_subtract_fusion = f32[128,256]{1,0:T(8,128)} fusion(f32[128,256]{1,0:T(8,128)S(1)} %copy-done.3, f32[128,256]{1,0:T(8,128)S(1)} %copy-done.4, f32[128,256]{1,0:T(8,128)S(1)} %copy-done.5, f32[128,256]{1,0:T(8,128)S(1)} %shard_map.106, f32[128,256]{1,0:T(8,128)S(1)} %copy-done.6), kind=kLoop, calls=%fused_computation | loop fusion | flops 2064384 | bytes 786432 | tf_op jit(solution)/shard_map/sub | solution.py:357
  83.7 0.7 copy.12
Async XLA Ops:
  0.6 33.4 %copy-start.2 = (s32[1,1,4]{2,1,0:T(1,128)S(1)}, s32[1,1,4]{2,1,0:T(1,128)}, u32[]{:S(2)}) copy-start(s32[1,1,4]{2,1,0:T(1,128)} %param.13) | copy-start | bytes 52
  0.6 33.4 %copy-start.1 = (s32[1,1,4,12]{3,2,1,0:T(4,128)S(1)}, s32[1,1,4,12]{3,2,1,0:T(4,128)}, u32[]{:S(2)}) copy-start(s32[1,1,4,12]{3,2,1,0:T(4,128)} %param.12) | copy-start | bytes 580
  0.7 33.4 %copy-start = (s32[1,1,4,12]{3,2,1,0:T(4,128)S(1)}, s32[1,1,4,12]{3,2,1,0:T(4,128)}, u32[]{:S(2)}) copy-start(s32[1,1,4,12]{3,2,1,0:T(4,128)} %param.11) | copy-start | bytes 580
  43.8 38.6 %copy-start.3 = (f32[128,256]{1,0:T(8,128)S(1)}, f32[128,256]{1,0:T(8,128)}, u32[]{:S(2)}) copy-start(f32[128,256]{1,0:T(8,128)} %param.16) | copy-start | bytes 393220
  43.8 38.6 %copy-start.4 = (f32[128,256]{1,0:T(8,128)S(1)}, f32[128,256]{1,0:T(8,128)}, u32[]{:S(2)}) copy-start(f32[128,256]{1,0:T(8,128)} %param.15) | copy-start | bytes 393220
  43.8 38.6 %copy-start.5 = (f32[128,256]{1,0:T(8,128)S(1)}, f32[128,256]{1,0:T(8,128)}, u32[]{:S(2)}) copy-start(f32[128,256]{1,0:T(8,128)} %param.14) | copy-start | bytes 393220
  43.8 38.6 %copy-start.6 = (f32[128,256]{1,0:T(8,128)S(1)}, f32[128,256]{1,0:T(8,128)}, u32[]{:S(2)}) copy-start(f32[128,256]{1,0:T(8,128)} %param.17) | copy-start | bytes 393220

commit v22 on v21

--- a/solution.py
+++ b/solution.py
@@ -185,7 +185,7 @@
     def device(yy, xx):
         return (slot(yy, xx), col, lag)
 
-    few = 16
+    few = 32
     sims = piece_ref.shape[1]
 
     def span(part):

time: 84.5 us -> 84.7 us (level)
  no operation moved by 1% of the time
where the time goes in v22:
time: 84.7 us; the launch traced here: 84.5 us
  Pallas kernels  81.8 us (97%)
  other arithmetic  1.27 us (1%)
    pallas_call x1, Pallas kernels, reduce_scatter(): pl.pallas_call(functools.partial(ring_kernel, n_z, n_pieces), out_shape=j...  38.8 us
    pallas_call x1, Pallas kernels, all_gather_rows(): pl.pallas_call(functools.partial(gather_kernel, n_x), out_shape=jax.Shape...  33 us
    pallas_call x1, Pallas kernels, stress_parts(): pl.pallas_call(functools.partial(parts_kernel, n_lag), out_shape=jax.Shap...  9.92 us

profile of v22, /device:TPU:1, one launch (start us, length us, event | category | flops | bytes accessed | tf_op | source)
XLA Modules:
  0.0 84.5 jit_solution(13288361060496006253)
XLA Ops:
  0.6 0.0 copy-start.2
  0.6 0.0 copy-start.1
  0.7 0.0 copy-start
  0.7 33.0 %shard_map.104.hist_ref = bf16[8,4,128,512]{3,2,1,0:T(8,128)(2,1)} custom-call(bf16[4,128,512]{2,1,0:T(8,128)(2,1)} %bitcast.10), custom_call_target="tpu_custom_call" | custom-call | tf_op jit(solution)/shard_map/pallas_call | solution.py:271
  33.7 0.0 copy-done.2
  33.7 0.0 copy-done.1
  33.7 0.0 copy-done
  33.7 9.9 %shard_map.105.part_ref = f32[2,16,128,256]{3,2,1,0:T(8,128)S(1)} custom-call(s32[4,12]{1,0:T(4,128)S(1)} %bitcast.6, s32[4,12]{1,0:T(4,128)S(1)} %bitcast.7, s32[4]{0:T(128)S(1)} %bitcast.8, s32[1]{0:T(128)} %bitcast.3.lag_ref, bf16[8,4,128,512]{3,2,1,0:T(8,128)(2,1)} %shard_map.104.hist_ref, bf16[4,12,256,256]{3,2,1,0:T(8,128)(2,1)} %bitcast.9), custom_call_target="tpu_custom_call" | custom-call | tf_op jit(solution)/shard_map/pallas_call | solution.py:323
  43.7 0.0 copy-start.3
  43.7 0.0 copy-start.4
  43.7 0.0 copy-start.5
  43.7 0.0 copy-start.6
  43.7 38.8 %shard_map.106 = f32[128,256]{1,0:T(8,128)S(1)} custom-call(f32[2,16,128,256]{3,2,1,0:T(8,128)S(1)} %shard_map.105.part_ref), custom_call_target="tpu_custom_call" | custom-call | tf_op jit(solution)/shard_map/pallas_call | solution.py:149
  82.6 0.0 copy-done.3
  82.6 0.0 copy-done.4
  82.6 0.0 copy-done.5
  82.6 0.0 copy-done.6
  82.6 1.3 %divide_subtract_fusion = f32[128,256]{1,0:T(8,128)} fusion(f32[128,256]{1,0:T(8,128)S(1)} %copy-done.3, f32[128,256]{1,0:T(8,128)S(1)} %copy-done.4, f32[128,256]{1,0:T(8,128)S(1)} %copy-done.5, f32[128,256]{1,0:T(8,128)S(1)} %shard_map.106, f32[128,256]{1,0:T(8,128)S(1)} %copy-done.6), kind=kLoop, calls=%fused_computation | loop fusion | flops 2064384 | bytes 786432 | tf_op jit(solution)/shard_map/sub | solution.py:357
  83.9 0.7 copy.12
Async XLA Ops:
  0.6 33.1 %copy-start.2 = (s32[1,1,4]{2,1,0:T(1,128)S(1)}, s32[1,1,4]{2,1,0:T(1,128)}, u32[]{:S(2)}) copy-start(s32[1,1,4]{2,1,0:T(1,128)} %param.13) | copy-start | bytes 52
  0.6 33.1 %copy-start.1 = (s32[1,1,4,12]{3,2,1,0:T(4,128)S(1)}, s32[1,1,4,12]{3,2,1,0:T(4,128)}, u32[]{:S(2)}) copy-start(s32[1,1,4,12]{3,2,1,0:T(4,128)} %param.12) | copy-start | bytes 580
  0.7 33.1 %copy-start = (s32[1,1,4,12]{3,2,1,0:T(4,128)S(1)}, s32[1,1,4,12]{3,2,1,0:T(4,128)}, u32[]{:S(2)}) copy-start(s32[1,1,4,12]{3,2,1,0:T(4,128)} %param.11) | copy-start | bytes 580
  43.7 38.9 %copy-start.3 = (f32[128,256]{1,0:T(8,128)S(1)}, f32[128,256]{1,0:T(8,128)}, u32[]{:S(2)}) copy-start(f32[128,256]{1,0:T(8,128)} %param.16) | copy-start | bytes 393220
  43.7 38.9 %copy-start.4 = (f32[128,256]{1,0:T(8,128)S(1)}, f32[128,256]{1,0:T(8,128)}, u32[]{:S(2)}) copy-start(f32[128,256]{1,0:T(8,128)} %param.15) | copy-start | bytes 393220
  43.7 38.9 %copy-start.5 = (f32[128,256]{1,0:T(8,128)S(1)}, f32[128,256]{1,0:T(8,128)}, u32[]{:S(2)}) copy-start(f32[128,256]{1,0:T(8,128)} %param.14) | copy-start | bytes 393220
  43.7 38.9 %copy-start.6 = (f32[128,256]{1,0:T(8,128)S(1)}, f32[128,256]{1,0:T(8,128)}, u32[]{:S(2)}) copy-start(f32[128,256]{1,0:T(8,128)} %param.17) | copy-start | bytes 393220

commit v23 on v21

--- a/solution.py
+++ b/solution.py
@@ -141,7 +141,7 @@
         copy.wait_send()
 
 
-def reduce_scatter(part, n_col, n_pieces=4):
+def reduce_scatter(part, n_col, n_pieces=2):
     _, group, sims, tile = part.shape
     n_z = n_col // 2
     longer = n_z // 2

time: 84.5 us -> 84.2 us (level)
    pallas_call x1, Pallas kernels: 38.5 us -> 39.6 us  [reduce_scatter(): pl.pallas_call(functools.partial(ring_kernel, n_z, n_pieces), out_shape=j...]
where the time goes in v23:
time: 84.2 us; the launch traced here: 84.7 us
  Pallas kernels  81.9 us (97%)
  other arithmetic  1.27 us (2%)
    pallas_call x1, Pallas kernels, reduce_scatter(): pl.pallas_call(functools.partial(ring_kernel, n_z, n_pieces), out_shape=j...  39.6 us
    pallas_call x1, Pallas kernels, all_gather_rows(): pl.pallas_call(functools.partial(gather_kernel, n_x), out_shape=jax.Shape...  33.4 us
    pallas_call x1, Pallas kernels, stress_parts(): pl.pallas_call(functools.partial(parts_kernel, n_lag), out_shape=jax.Shap...  8.96 us

profile of v23, /device:TPU:1, one launch (start us, length us, event | category | flops | bytes accessed | tf_op | source)
XLA Modules:
  0.0 84.7 jit_solution(1473738304443224150)
XLA Ops:
  0.6 0.0 copy-start.2
  0.6 0.0 copy-start.1
  0.7 0.0 copy-start
  0.7 33.4 %shard_map.104.hist_ref = bf16[8,4,128,512]{3,2,1,0:T(8,128)(2,1)} custom-call(bf16[4,128,512]{2,1,0:T(8,128)(2,1)} %bitcast.10), custom_call_target="tpu_custom_call" | custom-call | tf_op jit(solution)/shard_map/pallas_call | solution.py:271
  34.0 0.0 copy-done.2
  34.1 0.0 copy-done.1
  34.1 0.0 copy-done
  34.1 9.0 %shard_map.105.part_ref = f32[2,16,128,256]{3,2,1,0:T(8,128)S(1)} custom-call(s32[4,12]{1,0:T(4,128)S(1)} %bitcast.6, s32[4,12]{1,0:T(4,128)S(1)} %bitcast.7, s32[4]{0:T(128)S(1)} %bitcast.8, s32[1]{0:T(128)} %bitcast.3.lag_ref, bf16[8,4,128,512]{3,2,1,0:T(8,128)(2,1)} %shard_map.104.hist_ref, bf16[4,12,256,256]{3,2,1,0:T(8,128)(2,1)} %bitcast.9), custom_call_target="tpu_custom_call" | custom-call | tf_op jit(solution)/shard_map/pallas_call | solution.py:323
  43.0 0.0 copy-start.3
  43.1 0.0 copy-start.4
  43.1 0.0 copy-start.5
  43.1 0.0 copy-start.6
  43.1 39.6 %shard_map.106 = f32[128,256]{1,0:T(8,128)S(1)} custom-call(f32[2,16,128,256]{3,2,1,0:T(8,128)S(1)} %shard_map.105.part_ref), custom_call_target="tpu_custom_call" | custom-call | tf_op jit(solution)/shard_map/pallas_call | solution.py:149
  82.7 0.0 copy-done.3
  82.7 0.0 copy-done.4
  82.7 0.0 copy-done.5
  82.7 0.0 copy-done.6
  82.7 1.3 %divide_subtract_fusion = f32[128,256]{1,0:T(8,128)} fusion(f32[128,256]{1,0:T(8,128)S(1)} %copy-done.3, f32[128,256]{1,0:T(8,128)S(1)} %copy-done.4, f32[128,256]{1,0:T(8,128)S(1)} %copy-done.5, f32[128,256]{1,0:T(8,128)S(1)} %shard_map.106, f32[128,256]{1,0:T(8,128)S(1)} %copy-done.6), kind=kLoop, calls=%fused_computation | loop fusion | flops 2064384 | bytes 786432 | tf_op jit(solution)/shard_map/sub | solution.py:357
  84.0 0.7 copy.12
Async XLA Ops:
  0.6 33.4 %copy-start.2 = (s32[1,1,4]{2,1,0:T(1,128)S(1)}, s32[1,1,4]{2,1,0:T(1,128)}, u32[]{:S(2)}) copy-start(s32[1,1,4]{2,1,0:T(1,128)} %param.13) | copy-start | bytes 52
  0.6 33.4 %copy-start.1 = (s32[1,1,4,12]{3,2,1,0:T(4,128)S(1)}, s32[1,1,4,12]{3,2,1,0:T(4,128)}, u32[]{:S(2)}) copy-start(s32[1,1,4,12]{3,2,1,0:T(4,128)} %param.12) | copy-start | bytes 580
  0.7 33.4 %copy-start = (s32[1,1,4,12]{3,2,1,0:T(4,128)S(1)}, s32[1,1,4,12]{3,2,1,0:T(4,128)}, u32[]{:S(2)}) copy-start(s32[1,1,4,12]{3,2,1,0:T(4,128)} %param.11) | copy-start | bytes 580
  43.0 39.7 %copy-start.3 = (f32[128,256]{1,0:T(8,128)S(1)}, f32[128,256]{1,0:T(8,128)}, u32[]{:S(2)}) copy-start(f32[128,256]{1,0:T(8,128)} %param.16) | copy-start | bytes 393220
  43.1 39.7 %copy-start.4 = (f32[128,256]{1,0:T(8,128)S(1)}, f32[128,256]{1,0:T(8,128)}, u32[]{:S(2)}) copy-start(f32[128,256]{1,0:T(8,128)} %param.15) | copy-start | bytes 393220
  43.1 39.7 %copy-start.5 = (f32[128,256]{1,0:T(8,128)S(1)}, f32[128,256]{1,0:T(8,128)}, u32[]{:S(2)}) copy-start(f32[128,256]{1,0:T(8,128)} %param.14) | copy-start | bytes 393220
  43.1 39.7 %copy-start.6 = (f32[128,256]{1,0:T(8,128)S(1)}, f32[128,256]{1,0:T(8,128)}, u32[]{:S(2)}) copy-start(f32[128,256]{1,0:T(8,128)} %param.17) | copy-start | bytes 393220

commit v24 on v23

--- a/solution.py
+++ b/solution.py
@@ -141,7 +141,7 @@
         copy.wait_send()
 
 
-def reduce_scatter(part, n_col, n_pieces=2):
+def reduce_scatter(part, n_col, n_pieces=1):
     _, group, sims, tile = part.shape
     n_z = n_col // 2
     longer = n_z // 2

time: 84.2 us -> 87.3 us (1.037)
  the two profiles are of different devices: /device:TPU:1 before, /device:TPU:32 now
where the time goes in v24:
time: 87.3 us; the launch traced here: 87.2 us
  Pallas kernels  84.5 us (97%)
  other arithmetic  1.27 us (1%)
    pallas_call x1, Pallas kernels, reduce_scatter(): pl.pallas_call(functools.partial(ring_kernel, n_z, n_pieces), out_shape=j...  39.2 us
    pallas_call x1, Pallas kernels, all_gather_rows(): pl.pallas_call(functools.partial(gather_kernel, n_x), out_shape=jax.Shape...  36.2 us
    pallas_call x1, Pallas kernels, stress_parts(): pl.pallas_call(functools.partial(parts_kernel, n_lag), out_shape=jax.Shap...  9.14 us

profile of v24, /device:TPU:32, one launch (start us, length us, event | category | flops | bytes accessed | tf_op | source)
XLA Modules:
  0.0 87.2 jit_solution(11239047714642771386)
XLA Ops:
  0.6 0.0 copy-start.2
  0.6 0.0 copy-start.1
  0.7 0.0 copy-start
  0.7 36.2 %shard_map.104.hist_ref = bf16[8,4,128,512]{3,2,1,0:T(8,128)(2,1)} custom-call(bf16[4,128,512]{2,1,0:T(8,128)(2,1)} %bitcast.10), custom_call_target="tpu_custom_call" | custom-call | tf_op jit(solution)/shard_map/pallas_call | solution.py:271
  36.8 0.0 copy-done.2
  36.8 0.0 copy-done.1
  36.8 0.0 copy-done
  36.9 9.1 %shard_map.105.part_ref = f32[2,16,128,256]{3,2,1,0:T(8,128)S(1)} custom-call(s32[4,12]{1,0:T(4,128)S(1)} %bitcast.6, s32[4,12]{1,0:T(4,128)S(1)} %bitcast.7, s32[4]{0:T(128)S(1)} %bitcast.8, s32[1]{0:T(128)} %bitcast.3.lag_ref, bf16[8,4,128,512]{3,2,1,0:T(8,128)(2,1)} %shard_map.104.hist_ref, bf16[4,12,256,256]{3,2,1,0:T(8,128)(2,1)} %bitcast.9), custom_call_target="tpu_custom_call" | custom-call | tf_op jit(solution)/shard_map/pallas_call | solution.py:323
  46.0 0.0 copy-start.3
  46.0 0.0 copy-start.4
  46.0 0.0 copy-start.5
  46.0 0.0 copy-start.6
  46.1 39.2 %shard_map.106 = f32[128,256]{1,0:T(8,128)S(1)} custom-call(f32[2,16,128,256]{3,2,1,0:T(8,128)S(1)} %shard_map.105.part_ref), custom_call_target="tpu_custom_call" | custom-call | tf_op jit(solution)/shard_map/pallas_call | solution.py:149
  85.2 0.0 copy-done.3
  85.2 0.0 copy-done.4
  85.2 0.0 copy-done.5
  85.2 0.0 copy-done.6
  85.3 1.3 %divide_subtract_fusion = f32[128,256]{1,0:T(8,128)} fusion(f32[128,256]{1,0:T(8,128)S(1)} %copy-done.3, f32[128,256]{1,0:T(8,128)S(1)} %copy-done.4, f32[128,256]{1,0:T(8,128)S(1)} %copy-done.5, f32[128,256]{1,0:T(8,128)S(1)} %shard_map.106, f32[128,256]{1,0:T(8,128)S(1)} %copy-done.6), kind=kLoop, calls=%fused_computation | loop fusion | flops 2064384 | bytes 786432 | tf_op jit(solution)/shard_map/sub | solution.py:357
  86.5 0.7 copy.12
Async XLA Ops:
  0.6 36.2 %copy-start.2 = (s32[1,1,4]{2,1,0:T(1,128)S(1)}, s32[1,1,4]{2,1,0:T(1,128)}, u32[]{:S(2)}) copy-start(s32[1,1,4]{2,1,0:T(1,128)} %param.13) | copy-start | bytes 52
  0.6 36.2 %copy-start.1 = (s32[1,1,4,12]{3,2,1,0:T(4,128)S(1)}, s32[1,1,4,12]{3,2,1,0:T(4,128)}, u32[]{:S(2)}) copy-start(s32[1,1,4,12]{3,2,1,0:T(4,128)} %param.12) | copy-start | bytes 580
  0.7 36.2 %copy-start = (s32[1,1,4,12]{3,2,1,0:T(4,128)S(1)}, s32[1,1,4,12]{3,2,1,0:T(4,128)}, u32[]{:S(2)}) copy-start(s32[1,1,4,12]{3,2,1,0:T(4,128)} %param.11) | copy-start | bytes 580
  46.0 39.2 %copy-start.3 = (f32[128,256]{1,0:T(8,128)S(1)}, f32[128,256]{1,0:T(8,128)}, u32[]{:S(2)}) copy-start(f32[128,256]{1,0:T(8,128)} %param.16) | copy-start | bytes 393220
  46.0 39.2 %copy-start.4 = (f32[128,256]{1,0:T(8,128)S(1)}, f32[128,256]{1,0:T(8,128)}, u32[]{:S(2)}) copy-start(f32[128,256]{1,0:T(8,128)} %param.15) | copy-start | bytes 393220
  46.0 39.2 %copy-start.5 = (f32[128,256]{1,0:T(8,128)S(1)}, f32[128,256]{1,0:T(8,128)}, u32[]{:S(2)}) copy-start(f32[128,256]{1,0:T(8,128)} %param.14) | copy-start | bytes 393220
  46.0 39.2 %copy-start.6 = (f32[128,256]{1,0:T(8,128)S(1)}, f32[128,256]{1,0:T(8,128)}, u32[]{:S(2)}) copy-start(f32[128,256]{1,0:T(8,128)} %param.17) | copy-start | bytes 393220

commit v25 on v23

--- a/solution.py
+++ b/solution.py
@@ -185,7 +185,7 @@
     def device(yy, xx):
         return (slot(yy, xx), col, lag)
 
-    few = 16
+    few = 24
     sims = piece_ref.shape[1]
 
     def span(part):

time: 84.2 us -> 84.4 us (level)
    pallas_call x1, Pallas kernels: 39.6 us -> 38.6 us  [reduce_scatter(): pl.pallas_call(functools.partial(ring_kernel, n_z, n_pieces), out_shape=j...]
    pallas_call x1, Pallas kernels: 8.96 us -> 9.88 us  [stress_parts(): pl.pallas_call(functools.partial(parts_kernel, n_lag), out_shape=jax.Shap...]
where the time goes in v25:
time: 84.4 us; the launch traced here: 84.3 us
  Pallas kernels  81.5 us (97%)
  other arithmetic  1.27 us (2%)
    pallas_call x1, Pallas kernels, reduce_scatter(): pl.pallas_call(functools.partial(ring_kernel, n_z, n_pieces), out_shape=j...  38.6 us
    pallas_call x1, Pallas kernels, all_gather_rows(): pl.pallas_call(functools.partial(gather_kernel, n_x), out_shape=jax.Shape...  33 us
    pallas_call x1, Pallas kernels, stress_parts(): pl.pallas_call(functools.partial(parts_kernel, n_lag), out_shape=jax.Shap...  9.88 us

profile of v25, /device:TPU:1, one launch (start us, length us, event | category | flops | bytes accessed | tf_op | source)
XLA Modules:
  0.0 84.3 jit_solution(2287129277707702354)
XLA Ops:
  0.6 0.0 copy-start.2
  0.6 0.0 copy-start.1
  0.7 0.0 copy-start
  0.7 33.0 %shard_map.104.hist_ref = bf16[8,4,128,512]{3,2,1,0:T(8,128)(2,1)} custom-call(bf16[4,128,512]{2,1,0:T(8,128)(2,1)} %bitcast.10), custom_call_target="tpu_custom_call" | custom-call | tf_op jit(solution)/shard_map/pallas_call | solution.py:271
  33.7 0.0 copy-done.2
  33.7 0.0 copy-done.1
  33.7 0.0 copy-done
  33.7 9.9 %shard_map.105.part_ref = f32[2,16,128,256]{3,2,1,0:T(8,128)S(1)} custom-call(s32[4,12]{1,0:T(4,128)S(1)} %bitcast.6, s32[4,12]{1,0:T(4,128)S(1)} %bitcast.7, s32[4]{0:T(128)S(1)} %bitcast.8, s32[1]{0:T(128)} %bitcast.3.lag_ref, bf16[8,4,128,512]{3,2,1,0:T(8,128)(2,1)} %shard_map.104.hist_ref, bf16[4,12,256,256]{3,2,1,0:T(8,128)(2,1)} %bitcast.9), custom_call_target="tpu_custom_call" | custom-call | tf_op jit(solution)/shard_map/pallas_call | solution.py:323
  43.6 0.0 copy-start.3
  43.6 0.0 copy-start.4
  43.7 0.0 copy-start.5
  43.7 0.0 copy-start.6
  43.7 38.6 %shard_map.106 = f32[128,256]{1,0:T(8,128)S(1)} custom-call(f32[2,16,128,256]{3,2,1,0:T(8,128)S(1)} %shard_map.105.part_ref), custom_call_target="tpu_custom_call" | custom-call | tf_op jit(solution)/shard_map/pallas_call | solution.py:149
  82.3 0.0 copy-done.3
  82.3 0.0 copy-done.4
  82.3 0.0 copy-done.5
  82.3 0.0 copy-done.6
  82.3 1.3 %divide_subtract_fusion = f32[128,256]{1,0:T(8,128)} fusion(f32[128,256]{1,0:T(8,128)S(1)} %copy-done.3, f32[128,256]{1,0:T(8,128)S(1)} %copy-done.4, f32[128,256]{1,0:T(8,128)S(1)} %copy-done.5, f32[128,256]{1,0:T(8,128)S(1)} %shard_map.106, f32[128,256]{1,0:T(8,128)S(1)} %copy-done.6), kind=kLoop, calls=%fused_computation | loop fusion | flops 2064384 | bytes 786432 | tf_op jit(solution)/shard_map/sub | solution.py:357
  83.6 0.7 copy.12
Async XLA Ops:
  0.6 33.1 %copy-start.2 = (s32[1,1,4]{2,1,0:T(1,128)S(1)}, s32[1,1,4]{2,1,0:T(1,128)}, u32[]{:S(2)}) copy-start(s32[1,1,4]{2,1,0:T(1,128)} %param.13) | copy-start | bytes 52
  0.6 33.1 %copy-start.1 = (s32[1,1,4,12]{3,2,1,0:T(4,128)S(1)}, s32[1,1,4,12]{3,2,1,0:T(4,128)}, u32[]{:S(2)}) copy-start(s32[1,1,4,12]{3,2,1,0:T(4,128)} %param.12) | copy-start | bytes 580
  0.7 33.1 %copy-start = (s32[1,1,4,12]{3,2,1,0:T(4,128)S(1)}, s32[1,1,4,12]{3,2,1,0:T(4,128)}, u32[]{:S(2)}) copy-start(s32[1,1,4,12]{3,2,1,0:T(4,128)} %param.11) | copy-start | bytes 580
  43.6 38.7 %copy-start.3 = (f32[128,256]{1,0:T(8,128)S(1)}, f32[128,256]{1,0:T(8,128)}, u32[]{:S(2)}) copy-start(f32[128,256]{1,0:T(8,128)} %param.16) | copy-start | bytes 393220
  43.6 38.7 %copy-start.4 = (f32[128,256]{1,0:T(8,128)S(1)}, f32[128,256]{1,0:T(8,128)}, u32[]{:S(2)}) copy-start(f32[128,256]{1,0:T(8,128)} %param.15) | copy-start | bytes 393220
  43.7 38.7 %copy-start.5 = (f32[128,256]{1,0:T(8,128)S(1)}, f32[128,256]{1,0:T(8,128)}, u32[]{:S(2)}) copy-start(f32[128,256]{1,0:T(8,128)} %param.14) | copy-start | bytes 393220
  43.7 38.7 %copy-start.6 = (f32[128,256]{1,0:T(8,128)S(1)}, f32[128,256]{1,0:T(8,128)}, u32[]{:S(2)}) copy-start(f32[128,256]{1,0:T(8,128)} %param.17) | copy-start | bytes 393220

commit v26 on v23

--- a/solution.py
+++ b/solution.py
@@ -58,22 +58,22 @@
     order += [z * 2 + way for way in range(2)]
     handed = {}
     for index, block in enumerate(order):
-        copy = pltpu.make_async_remote_copy(
-            src_ref=part_ref.at[1, block],
-            dst_ref=mate.at[block],
-            send_sem=mate_sem.at[0, index],
-            recv_sem=mate_sem.at[1, index],
-            device_id=partner,
-            device_id_type=MESH,
-        )
-        copy.start()
-        handed[index] = copy
-    ready = set()
-
-    def own(index, span):
-        if index not in ready:
-            handed[index].wait_recv()
-            ready.add(index)
+        for piece in range(n_pieces):
+            span = pl.ds(piece * rows, rows)
+            copy = pltpu.make_async_remote_copy(
+                src_ref=part_ref.at[1, block, span],
+                dst_ref=mate.at[block, span],
+                send_sem=mate_sem.at[0, index, piece],
+                recv_sem=mate_sem.at[1, index, piece],
+                device_id=partner,
+                device_id_type=MESH,
+            )
+            copy.start()
+            handed[index, piece] = copy
+
+    def own(index, piece):
+        handed[index, piece].wait_recv()
+        span = pl.ds(piece * rows, rows)
         block = order[index]
         return part_ref[0, block, span] + mate[block, span]
 
@@ -92,11 +92,11 @@
                                   if step < length(w, sd)])
                     index += len([1 for w in range(way) if step < length(w, side)])
                     if step == 0:
-                        forward[side, way, step, piece] = own(index, span)
+                        forward[side, way, step, piece] = own(index, piece)
                     else:
                         copies[side, way, step - 1, piece].wait_recv()
                         forward[side, way, step, piece] = (
-                            recv[side, way, step - 1, piece] + own(index, span)
+                            recv[side, way, step - 1, piece] + own(index, piece)
                         )
                     source = forward.at[side, way, step, piece]
                     copy = pltpu.make_async_remote_copy(
@@ -114,7 +114,7 @@
     for piece in range(n_pieces):
         span = pl.ds(piece * rows, rows)
         for way in range(2):
-            total = own(len(order) - 2 + way, span)
+            total = own(len(order) - 2 + way, piece)
             for side in range(2):
                 last = length(way, side) - 1
                 copies[side, way, last, piece].wait_recv()
@@ -160,7 +160,7 @@
             pltpu.SemaphoreType.DMA((2, 2, longer, n_pieces)),
             pltpu.SemaphoreType.DMA((2, 2, longer, n_pieces)),
             pltpu.SemaphoreType.DMA((2, n_pieces)),
-            pltpu.SemaphoreType.DMA((2, group)),
+            pltpu.SemaphoreType.DMA((2, group, n_pieces)),
         ],
         compiler_params=pltpu.CompilerParams(
             collective_id=0, has_side_effects=True, vmem_limit_bytes=48 * 1024 * 1024

time: 84.2 us -> 84.9 us (level)
  no operation moved by 1% of the time
where the time goes in v26:
time: 84.9 us; the launch traced here: 84.6 us
  Pallas kernels  81.8 us (96%)
  other arithmetic  1.27 us (1%)
    pallas_call x1, Pallas kernels, reduce_scatter(): pl.pallas_call(functools.partial(ring_kernel, n_z, n_pieces), out_shape=j...  39.1 us
    pallas_call x1, Pallas kernels, all_gather_rows(): pl.pallas_call(functools.partial(gather_kernel, n_x), out_shape=jax.Shape...  33.4 us
    pallas_call x1, Pallas kernels, stress_parts(): pl.pallas_call(functools.partial(parts_kernel, n_lag), out_shape=jax.Shap...  9.35 us

profile of v26, /device:TPU:1, one launch (start us, length us, event | category | flops | bytes accessed | tf_op | source)
XLA Modules:
  0.0 84.6 jit_solution(10972103359566437643)
XLA Ops:
  0.6 0.0 copy-start.2
  0.6 0.0 copy-start.1
  0.7 0.0 copy-start
  0.7 33.4 %shard_map.104.hist_ref = bf16[8,4,128,512]{3,2,1,0:T(8,128)(2,1)} custom-call(bf16[4,128,512]{2,1,0:T(8,128)(2,1)} %bitcast.10), custom_call_target="tpu_custom_call" | custom-call | tf_op jit(solution)/shard_map/pallas_call | solution.py:271
  34.0 0.0 copy-done.2
  34.1 0.0 copy-done.1
  34.1 0.0 copy-done
  34.1 9.4 %shard_map.105.part_ref = f32[2,16,128,256]{3,2,1,0:T(8,128)S(1)} custom-call(s32[4,12]{1,0:T(4,128)S(1)} %bitcast.6, s32[4,12]{1,0:T(4,128)S(1)} %bitcast.7, s32[4]{0:T(128)S(1)} %bitcast.8, s32[1]{0:T(128)} %bitcast.3.lag_ref, bf16[8,4,128,512]{3,2,1,0:T(8,128)(2,1)} %shard_map.104.hist_ref, bf16[4,12,256,256]{3,2,1,0:T(8,128)(2,1)} %bitcast.9), custom_call_target="tpu_custom_call" | custom-call | tf_op jit(solution)/shard_map/pallas_call | solution.py:323
  43.4 0.0 copy-start.3
  43.5 0.0 copy-start.4
  43.5 0.0 copy-start.5
  43.5 0.0 copy-start.6
  43.5 39.1 %shard_map.106 = f32[128,256]{1,0:T(8,128)S(1)} custom-call(f32[2,16,128,256]{3,2,1,0:T(8,128)S(1)} %shard_map.105.part_ref), custom_call_target="tpu_custom_call" | custom-call | tf_op jit(solution)/shard_map/pallas_call | solution.py:149
  82.6 0.0 copy-done.3
  82.6 0.0 copy-done.4
  82.6 0.0 copy-done.5
  82.6 0.0 copy-done.6
  82.6 1.3 %divide_subtract_fusion = f32[128,256]{1,0:T(8,128)} fusion(f32[128,256]{1,0:T(8,128)S(1)} %copy-done.3, f32[128,256]{1,0:T(8,128)S(1)} %copy-done.4, f32[128,256]{1,0:T(8,128)S(1)} %copy-done.5, f32[128,256]{1,0:T(8,128)S(1)} %shard_map.106, f32[128,256]{1,0:T(8,128)S(1)} %copy-done.6), kind=kLoop, calls=%fused_computation | loop fusion | flops 2064384 | bytes 786432 | tf_op jit(solution)/shard_map/sub | solution.py:357
  83.9 0.7 copy.12
Async XLA Ops:
  0.6 33.4 %copy-start.2 = (s32[1,1,4]{2,1,0:T(1,128)S(1)}, s32[1,1,4]{2,1,0:T(1,128)}, u32[]{:S(2)}) copy-start(s32[1,1,4]{2,1,0:T(1,128)} %param.13) | copy-start | bytes 52
  0.6 33.4 %copy-start.1 = (s32[1,1,4,12]{3,2,1,0:T(4,128)S(1)}, s32[1,1,4,12]{3,2,1,0:T(4,128)}, u32[]{:S(2)}) copy-start(s32[1,1,4,12]{3,2,1,0:T(4,128)} %param.12) | copy-start | bytes 580
  0.7 33.4 %copy-start = (s32[1,1,4,12]{3,2,1,0:T(4,128)S(1)}, s32[1,1,4,12]{3,2,1,0:T(4,128)}, u32[]{:S(2)}) copy-start(s32[1,1,4,12]{3,2,1,0:T(4,128)} %param.11) | copy-start | bytes 580
  43.4 39.2 %copy-start.3 = (f32[128,256]{1,0:T(8,128)S(1)}, f32[128,256]{1,0:T(8,128)}, u32[]{:S(2)}) copy-start(f32[128,256]{1,0:T(8,128)} %param.16) | copy-start | bytes 393220
  43.5 39.2 %copy-start.4 = (f32[128,256]{1,0:T(8,128)S(1)}, f32[128,256]{1,0:T(8,128)}, u32[]{:S(2)}) copy-start(f32[128,256]{1,0:T(8,128)} %param.15) | copy-start | bytes 393220
  43.5 39.2 %copy-start.5 = (f32[128,256]{1,0:T(8,128)S(1)}, f32[128,256]{1,0:T(8,128)}, u32[]{:S(2)}) copy-start(f32[128,256]{1,0:T(8,128)} %param.14) | copy-start | bytes 393220
  43.5 39.1 %copy-start.6 = (f32[128,256]{1,0:T(8,128)S(1)}, f32[128,256]{1,0:T(8,128)}, u32[]{:S(2)}) copy-start(f32[128,256]{1,0:T(8,128)} %param.17) | copy-start | bytes 393220
